TPU v7x, 32 devices: a whole 2x2x4 slice. The times are simulated.
32 devices in a mesh: dp: 8 (over z, y), seq: 4 (over x, core).
Axes of the slice: x: 2, y: 2, z: 4, core: 2. Of those that a mesh axis runs over, the one named last changes fastest.
Arguments:
- tokens: bfloat16 [16, 2048, 768], P('dp', 'seq'), may hold values from -6 to 6
- first_values: bfloat16 [16, 2048, 384], P('dp', 'seq'), may hold values from -6 to 6
- cotangent: bfloat16 [16, 2048, 768], P('dp', 'seq'), may hold values from -6 to 6
- lengths: int32 [16], P('dp'), may hold values from 64 to 2048, as said below
- master_tiles: float32 [416, 128, 128], P(('dp', 'seq'))
- left_stat: float32 [416, 128, 128], P(('dp', 'seq'))
- right_stat: float32 [416, 128, 128], P(('dp', 'seq'))
- left_root: float32 [416, 128, 128], P(('dp', 'seq'))
- right_root: float32 [416, 128, 128], P(('dp', 'seq'))
- vector_params: float32 [8832], replicated
- vector_stat: float32 [8832], replicated
Outputs:
- block_output: bfloat16 [16, 2048, 768], P('dp', 'seq')
- tokens_grad: float32 [16, 2048, 768], P('dp', 'seq')
- first_values_grad: float32 [16, 2048, 384], P('dp', 'seq')
- tile_grads: float32 [416, 128, 128], P(('dp', 'seq'))
- left_new: float32 [416, 128, 128], P(('dp', 'seq'))
- right_new: float32 [416, 128, 128], P(('dp', 'seq'))
- tiles_new: float32 [416, 128, 128], P(('dp', 'seq'))
- vector_grads: float32 [8832], replicated
- vector_stat_new: float32 [8832], replicated
- vector_new: float32 [8832], replicated
- grad_norm: float32 [], replicated
Inputs may be any that keep to these rules, and one draw needn't show every extreme that they name: `lengths`: each sequence's length; in every draw some sequence has exactly 2048.
All inputs are finite; a program needn't handle non-finite values.
Results may differ from a plain program's by a relative error of at most 0.012.
The roundings to bfloat16 on the way count: a program that leaves them out, or rounds other values in their place, can miss the bound.
Values may be sent and summed in bfloat16 or wider, within the bound.
A program may use at most 192 MiB of HBM per device.

v0:
```python
import jax
import jax.numpy as jnp
from jax import lax
from jax.sharding import PartitionSpec as P

D = 768
HD = 64
FF = 3072
VW = 384
QBLK = 512
TILE = 128
CLIP = 256


highest = lax.Precision.HIGHEST
norm_eps = 1e-05
clip_eps = 1e-06
decay_rate = 0.5
matrix_rate = 0.3
vector_rate = 0.1
moment_eps = 1e-08
masked_score = -1e30


def matrix_shapes():
    return ((D, D), (D, D), (D, VW), (D, D), (D, FF), (FF, D))


def untile(stacked, row_count, col_count):
    shaped = stacked.reshape(row_count // TILE, col_count // TILE, TILE, TILE)
    return shaped.transpose(0, 2, 1, 3).reshape(row_count, col_count)


def retile(matrix):
    row_count, col_count = matrix.shape
    shaped = matrix.reshape(row_count // TILE, TILE, col_count // TILE, TILE)
    return shaped.transpose(0, 2, 1, 3).reshape(-1, TILE, TILE)


def split_tiles(stacked):
    matrices = []
    offset = 0
    for row_count, col_count in matrix_shapes():
        amount = row_count // TILE * (col_count // TILE)
        matrices.append(untile(stacked[offset : offset + amount], row_count, col_count))
        offset = offset + amount
    return matrices


def join_tiles(matrices, total_tiles):
    joined = jnp.concatenate([retile(matrix) for matrix in matrices], axis=0)
    padding = jnp.zeros((total_tiles - joined.shape[0], TILE, TILE), joined.dtype)
    return jnp.concatenate([joined, padding], axis=0)


def split_vector(vector):
    pieces = []
    offset = 0
    for length in (D, D, D, D, D, D, D, VW, FF):
        pieces.append(vector[offset : offset + length])
        offset = offset + length
    return pieces


def matmul(left_in, right_in):
    return jnp.dot(left_in, right_in, preferred_element_type=jnp.float32)


def contract_rows(left_in, right_in):
    return lax.dot_general(
        left_in, right_in, (((0,), (0,)), ((), ())), preferred_element_type=jnp.float32
    )


def contract_cols(left_in, right_in):
    return lax.dot_general(
        left_in, right_in, (((1,), (1,)), ((), ())), preferred_element_type=jnp.float32
    )


def norm_forward(values, gain_row, shift_row):
    centered = values - jnp.mean(values, axis=-1, keepdims=True)
    variance = jnp.mean(centered * centered, axis=-1, keepdims=True)
    inv_std = lax.rsqrt(variance + norm_eps)
    unit_rows = centered * inv_std
    return (unit_rows * gain_row + shift_row, unit_rows, inv_std)


def norm_backward(grad_in, unit_rows, inv_std, gain_row):
    scaled = grad_in * gain_row
    term = (
        scaled
        - jnp.mean(scaled, axis=-1, keepdims=True)
        - unit_rows * jnp.mean(scaled * unit_rows, axis=-1, keepdims=True)
    )
    return (term * inv_std, jnp.sum(grad_in * unit_rows, axis=0), jnp.sum(grad_in, axis=0))


def allowed_keys(block_index, length, key_count):
    query_pos = block_index * QBLK + jnp.arange(QBLK, dtype=jnp.int32)
    key_pos = jnp.arange(key_count, dtype=jnp.int32)
    return (key_pos[None, :] <= query_pos[:, None]) & (key_pos[None, :] < length)


def attend_forward(inputs):
    query_seq, key_seq, value_seq, length = inputs
    key_count = query_seq.shape[0]
    head_count = query_seq.shape[1] // HD
    query_heads = query_seq.reshape(key_count, head_count, HD)
    key_heads = key_seq.reshape(key_count, head_count, HD)
    value_heads = value_seq.reshape(key_count, head_count, HD)
    score_scale = HD ** (-0.5)

    def one_block(block_index):
        query_rows = lax.dynamic_slice_in_dim(query_heads, block_index * QBLK, QBLK, 0)
        scores = (
            jnp.einsum("qhd,khd->hqk", query_rows, key_heads, preferred_element_type=jnp.float32)
            * score_scale
        )
        scores = jnp.where(allowed_keys(block_index, length, key_count)[None], scores, masked_score)
        top_score = jnp.max(scores, axis=-1, keepdims=True)
        exponent = jnp.exp(scores - top_score)
        totals = jnp.sum(exponent, axis=-1, keepdims=True)
        weights = (exponent / totals).astype(jnp.bfloat16)
        attended = jnp.einsum(
            "hqk,khd->qhd", weights, value_heads, preferred_element_type=jnp.float32
        )
        return (attended.astype(jnp.bfloat16), (top_score + jnp.log(totals))[..., 0])

    attended, log_sums = lax.map(one_block, jnp.arange(key_count // QBLK, dtype=jnp.int32))
    return (
        attended.reshape(key_count, head_count * HD),
        log_sums.transpose(1, 0, 2).reshape(head_count, key_count),
    )


def attend_backward(inputs):
    query_seq, key_seq, value_seq, grad_seq, log_sums, length = inputs
    key_count = query_seq.shape[0]
    head_count = query_seq.shape[1] // HD
    query_heads = query_seq.reshape(key_count, head_count, HD)
    key_heads = key_seq.reshape(key_count, head_count, HD)
    value_heads = value_seq.reshape(key_count, head_count, HD)
    grad_heads = grad_seq.reshape(key_count, head_count, HD)
    score_scale = HD ** (-0.5)

    def one_block(carried, block_index):
        key_acc, value_acc = carried
        query_rows = lax.dynamic_slice_in_dim(query_heads, block_index * QBLK, QBLK, 0)
        grad_rows = lax.dynamic_slice_in_dim(grad_heads, block_index * QBLK, QBLK, 0)
        sums_rows = lax.dynamic_slice_in_dim(log_sums, block_index * QBLK, QBLK, 1)
        scores = (
            jnp.einsum("qhd,khd->hqk", query_rows, key_heads, preferred_element_type=jnp.float32)
            * score_scale
        )
        scores = jnp.where(allowed_keys(block_index, length, key_count)[None], scores, masked_score)
        probs = jnp.exp(scores - sums_rows[..., None])
        probs_grad = jnp.einsum(
            "qhd,khd->hqk", grad_rows, value_heads, preferred_element_type=jnp.float32
        )
        delta = jnp.sum(probs * probs_grad, axis=-1, keepdims=True)
        score_grad = (probs * (probs_grad - delta)).astype(jnp.bfloat16)
        query_grad = (
            jnp.einsum("hqk,khd->qhd", score_grad, key_heads, preferred_element_type=jnp.float32)
            * score_scale
        )
        key_acc = (
            key_acc
            + jnp.einsum("hqk,qhd->khd", score_grad, query_rows, preferred_element_type=jnp.float32)
            * score_scale
        )
        value_acc = value_acc + jnp.einsum(
            "hqk,qhd->khd",
            probs.astype(jnp.bfloat16),
            grad_rows,
            preferred_element_type=jnp.float32,
        )
        return ((key_acc, value_acc), query_grad.astype(jnp.bfloat16))

    zero_acc = jnp.zeros((key_count, head_count, HD), jnp.float32)
    (key_acc, value_acc), query_grad = lax.scan(
        one_block, (zero_acc, zero_acc), jnp.arange(key_count // QBLK, dtype=jnp.int32)
    )
    local_width = head_count * HD
    return (
        query_grad.reshape(key_count, local_width),
        key_acc.astype(jnp.bfloat16).reshape(key_count, local_width),
        value_acc.astype(jnp.bfloat16).reshape(key_count, local_width),
    )


def per_device(
    tokens,
    first_values,
    cotangent,
    lengths,
    master_tiles,
    left_stat,
    right_stat,
    left_root,
    right_root,
    vector_params,
    vector_stat,
):
    seq_count, block_len, model_width = tokens.shape
    gathered = lax.all_gather(master_tiles.astype(jnp.bfloat16), ("dp", "seq"), axis=0, tiled=True)
    w_query, w_key, w_value, w_out, w_hidden, w_proj = split_tiles(gathered)
    (
        gain_one,
        shift_one,
        gain_two,
        shift_two,
        query_bias,
        out_bias,
        proj_bias,
        value_bias,
        hidden_bias,
    ) = split_vector(vector_params)
    flat_tokens = tokens.reshape(-1, model_width).astype(jnp.float32)
    normed_one, unit_one, inv_one = norm_forward(flat_tokens, gain_one, shift_one)
    normed_one = normed_one.astype(jnp.bfloat16)
    queries = (matmul(normed_one, w_query) + query_bias).astype(jnp.bfloat16)
    keys_all = matmul(normed_one, w_key).astype(jnp.bfloat16)
    fresh = (matmul(normed_one, w_value) + value_bias).astype(jnp.bfloat16)
    values_all = jnp.concatenate([fresh, first_values.reshape(-1, VW)], axis=-1)
    packed = jnp.stack([queries, keys_all, values_all]).reshape(
        3, seq_count, block_len, model_width
    )
    head_data = lax.all_to_all(packed, "seq", split_axis=3, concat_axis=2, tiled=True)
    attn_heads, log_sums = lax.map(
        attend_forward, (head_data[0], head_data[1], head_data[2], lengths)
    )
    returned = lax.all_to_all(attn_heads, "seq", split_axis=1, concat_axis=2, tiled=True)
    attended = returned.reshape(-1, model_width)
    residual = flat_tokens + matmul(attended, w_out) + out_bias
    normed_two, unit_two, inv_two = norm_forward(residual, gain_two, shift_two)
    normed_two = normed_two.astype(jnp.bfloat16)
    hidden = matmul(normed_two, w_hidden) + hidden_bias
    active = jax.nn.gelu(hidden, approximate=True).astype(jnp.bfloat16)
    output = residual + matmul(active, w_proj) + proj_bias
    block_output = output.astype(jnp.bfloat16).reshape(tokens.shape)
    positions = lax.axis_index("seq") * block_len + jnp.arange(block_len, dtype=jnp.int32)
    live = positions[None, :] < lengths[:, None]
    out_grad = jnp.where(live[:, :, None], cotangent, jnp.zeros_like(cotangent)).reshape(
        -1, model_width
    )
    grad_w_proj = contract_rows(active, out_grad)
    proj_bias_grad = jnp.sum(out_grad.astype(jnp.float32), axis=0)
    active_grad = contract_cols(out_grad, w_proj)
    gelu_value, gelu_back = jax.vjp(lambda inner: jax.nn.gelu(inner, approximate=True), hidden)
    hidden_grad = gelu_back(active_grad)[0].astype(jnp.bfloat16)
    grad_w_hidden = contract_rows(normed_two, hidden_grad)
    hidden_bias_grad = jnp.sum(hidden_grad.astype(jnp.float32), axis=0)
    norm_two_in = contract_cols(hidden_grad, w_hidden)
    resid_part, gain_two_grad, shift_two_grad = norm_backward(
        norm_two_in, unit_two, inv_two, gain_two
    )
    residual_grad = out_grad.astype(jnp.float32) + resid_part
    branch_grad = residual_grad.astype(jnp.bfloat16)
    grad_w_out = contract_rows(attended, branch_grad)
    out_bias_grad = jnp.sum(branch_grad.astype(jnp.float32), axis=0)
    attended_grad = contract_cols(branch_grad, w_out).astype(jnp.bfloat16)
    grad_heads = lax.all_to_all(
        attended_grad.reshape(seq_count, block_len, model_width),
        "seq",
        split_axis=2,
        concat_axis=1,
        tiled=True,
    )
    query_grad, key_grad, value_grad = lax.map(
        attend_backward, (head_data[0], head_data[1], head_data[2], grad_heads, log_sums, lengths)
    )
    sent_back = lax.all_to_all(
        jnp.stack([query_grad, key_grad, value_grad]),
        "seq",
        split_axis=2,
        concat_axis=3,
        tiled=True,
    )
    queries_grad = sent_back[0].reshape(-1, model_width)
    keys_grad = sent_back[1].reshape(-1, model_width)
    values_grad = sent_back[2].reshape(-1, model_width)
    fresh_grad = values_grad[:, :VW]
    first_grad = values_grad[:, VW:].astype(jnp.float32).reshape(first_values.shape)
    grad_w_query = contract_rows(normed_one, queries_grad)
    grad_w_key = contract_rows(normed_one, keys_grad)
    grad_w_value = contract_rows(normed_one, fresh_grad)
    query_bias_grad = jnp.sum(queries_grad.astype(jnp.float32), axis=0)
    value_bias_grad = jnp.sum(fresh_grad.astype(jnp.float32), axis=0)
    norm_one_in = (
        contract_cols(queries_grad, w_query)
        + contract_cols(keys_grad, w_key)
        + contract_cols(fresh_grad, w_value)
    )
    token_part, gain_one_grad, shift_one_grad = norm_backward(
        norm_one_in, unit_one, inv_one, gain_one
    )
    tokens_grad = (residual_grad + token_part).reshape(tokens.shape)
    grad_stack = join_tiles(
        [grad_w_query, grad_w_key, grad_w_value, grad_w_out, grad_w_hidden, grad_w_proj],
        gathered.shape[0],
    )
    vector_local = jnp.concatenate(
        [
            gain_one_grad,
            shift_one_grad,
            gain_two_grad,
            shift_two_grad,
            query_bias_grad,
            out_bias_grad,
            proj_bias_grad,
            value_bias_grad,
            hidden_bias_grad,
        ]
    )
    owned = lax.psum_scatter(grad_stack, ("dp", "seq"), scatter_dimension=0, tiled=True)
    summed_vector, owned_square = lax.psum((vector_local, jnp.sum(owned * owned)), ("dp", "seq"))
    grad_norm = jnp.sqrt(owned_square + jnp.sum(summed_vector * summed_vector))
    factor = jnp.minimum(1.0, CLIP / (grad_norm + clip_eps))
    clipped = owned * factor
    left_gram = jnp.einsum("tij,tkj->tik", clipped, clipped, precision=highest)
    right_gram = jnp.einsum("tji,tjk->tik", clipped, clipped, precision=highest)
    inner = jnp.einsum("tij,tjk->tik", clipped, right_root, precision=highest)
    step = jnp.einsum("tij,tjk->tik", left_root, inner, precision=highest)
    left_new = decay_rate * left_stat + (1.0 - decay_rate) * left_gram
    right_new = decay_rate * right_stat + (1.0 - decay_rate) * right_gram
    tiles_new = master_tiles - matrix_rate * step
    vector_grads = summed_vector * factor
    vector_stat_new = decay_rate * vector_stat + (1.0 - decay_rate) * vector_grads * vector_grads
    vector_new = vector_params - vector_rate * vector_grads / (
        jnp.sqrt(vector_stat_new) + moment_eps
    )
    return (
        block_output,
        tokens_grad,
        first_grad,
        clipped,
        left_new,
        right_new,
        tiles_new,
        vector_grads,
        vector_stat_new,
        vector_new,
        grad_norm,
    )


def solution(mesh):
    in_specs = (
        P("dp", "seq", None),
        P("dp", "seq", None),
        P("dp", "seq", None),
        P("dp"),
        P(("dp", "seq"), None, None),
        P(("dp", "seq"), None, None),
        P(("dp", "seq"), None, None),
        P(("dp", "seq"), None, None),
        P(("dp", "seq"), None, None),
        P(),
        P(),
    )
    out_specs = (
        P("dp", "seq", None),
        P("dp", "seq", None),
        P("dp", "seq", None),
        P(("dp", "seq"), None, None),
        P(("dp", "seq"), None, None),
        P(("dp", "seq"), None, None),
        P(("dp", "seq"), None, None),
        P(),
        P(),
        P(),
        P(),
    )
    return jax.shard_map(
        per_device, mesh=mesh, in_specs=in_specs, out_specs=out_specs, check_vma=False
    )
```

profile of v0, /device:TPU:0, one launch (start us, length us, event | category | flops | bytes accessed | tf_op | source)
XLA Modules:
  0.0 1392.7 jit_solution(12912429408049028219)
XLA Ops:
  17.5 97.4 %all-gather.2.cloned.1.call-done = bf16[416,128,128]{2,1,0:T(8,128)(2,1)} async-done(((bf16[13,128,128]{2,1,0:T(8,128)(2,1)}), bf16[416,128,128]{2,1,0:T(8,128)(2,1)}) %all-gather.2.cloned.1.call-update) | async-done | bytes 13631504 | tf_op jit(solution)/shard_map/all_gather | solution.py:206
  143.5 13.7 maximum_maximum_fusion
  163.1 53.2 %all-to-all-done = bf16[3,2,512,768]{2,1,0,3:T(2,128)(2,1)} async-done(((bf16[3,2,512,768]{2,1,0,3:T(2,128)(2,1)}), bf16[3,2,512,768]{2,1,0,3:T(2,128)(2,1)}, u32[]{:S(2)}, u32[]{:S(2)}) %all-to-all-start) | async-done | bytes 4718624 | tf_op jit(solution)/shard_map/all_to_all | solution.py:229
  242.3 197.6 %while.54 = (s32[]{:T(128)}, bf16[2,2048,192]{1,2,0:T(8,128)(2,1)}, f32[2,3,2048]{2,1,0:T(4,128)S(1)}, bf16[2,2048,192]{1,2,0:T(8,128)(2,1)}, bf16[2,2048,192]{1...) while((s32[]{:T(128)}, bf16[2,2048,192]{1,2,0:T(8,128)(2,1)}, ...), condition=%wide.region_7.8_spmd, body=%wide.region_2.7_spmd.sunk | while | flops 845251584 | bytes 53479908 | solution.py:230
  246.7 92.3 %while.57 = (s32[]{:T(128)}, bf16[4,512,3,64]{1,3,2,0:T(8,128)(2,1)S(1)}, f32[4,3,512]{2,1,0:T(4,128)S(1)}, s32[4]{0:T(128)S(1)}, s32[]{:T(128)}, /*index=5*/bf1...) while((s32[]{:T(128)}, ...), condition=%wide.region_6.6_spmd, body=%wide.region_3.5_spmd.sunk | while | flops 845251584 | bytes 43976908 | solution.py:130
  249.2 7.0 fusion.206
  256.2 6.8 fusion.207
  263.0 6.7 fusion.208
  272.3 7.0 fusion.206
  279.3 6.8 fusion.207
  286.1 6.7 fusion.208
  295.4 7.0 fusion.206
  302.4 6.8 fusion.207
  309.2 6.7 fusion.208
  318.5 7.0 fusion.206
  325.5 6.8 fusion.207
  332.3 6.7 fusion.208
  345.3 92.3 %while.57 = (s32[]{:T(128)}, bf16[4,512,3,64]{1,3,2,0:T(8,128)(2,1)S(1)}, f32[4,3,512]{2,1,0:T(4,128)S(1)}, s32[4]{0:T(128)S(1)}, s32[]{:T(128)}, /*index=5*/bf1...) while((s32[]{:T(128)}, ...), condition=%wide.region_6.6_spmd, body=%wide.region_3.5_spmd.sunk | while | flops 845251584 | bytes 43976908 | solution.py:130
  347.9 7.0 fusion.206
  354.9 6.8 fusion.207
  361.7 6.7 fusion.208
  371.0 7.0 fusion.206
  378.0 6.8 fusion.207
  384.8 6.7 fusion.208
  394.1 7.0 fusion.206
  401.1 6.8 fusion.207
  407.9 6.7 fusion.208
  417.2 7.0 fusion.206
  424.2 6.8 fusion.207
  453.6 9.1 fusion.122
  467.8 6.9 copy.229
  479.3 10.4 copy.226
  495.2 22.7 %fusion.54 = (bf16[3072,1024]{0,1:T(8,128)(2,1)}, f32[1024,3072]{1,0:T(8,128)}) fusion(f32[3072]{0:T(1024)S(1)} %copy-done.64, bf16[96,8,24,128]{3,2,1,0:T(8,128)(2,1)S(1)} %bitcast.413, f32[1024,768]{1,0:T(8,128)S(1)} %get-tuple-element.458, f32[768]{0:T(1024)S(1)} %copy-done.51, f32[768]{0:T(1024)S(1)} %copy-done.49, f32[1024]{0:T(1024)S(1)} %add_rsqrt_fusion, ...), kind=kOutput, calls=%fused_computation.81 | convolution fusion | flops 4867227648 | bytes 26765312 | tf_op jit(solution)/shard_map/dot_general | solution.py:66
  517.9 15.1 %convert_reduce_fusion = (f32[3072]{0:T(1024)}, bf16[1024,3072]{1,0:T(8,128)(2,1)S(1)}) fusion(f32[1024,3072]{1,0:T(8,128)} %get-tuple-element.462, f32[3072]{0:T(1024)S(1)} %copy-done.64, bf16[1024,768]{1,0:T(8,128)(2,1)S(1)} %bitcast.391, bf16[96,8,24,128]{3,2,1,0:T(8,128)(2,1)S(1)} %bitcast.410), kind=kOutput, calls=%fused_computation.82 | convolution fusion | flops 4904186880 | bytes 25190400 | tf_op jit(solution)/shard_map/dot_general | solution.py:76
  556.1 8.6 copy.261
  564.7 8.7 all-to-all-done.2
  579.3 277.4 %while.56 = (s32[]{:T(128)}, bf16[2,2048,192]{1,2,0:T(8,128)(2,1)}, bf16[2,2048,192]{1,2,0:T(8,128)(2,1)}, bf16[2,2048,192]{1,2,0:T(8,128)(2,1)}, bf16[2,2048,19...) while((s32[]{:T(128)}, bf16[2,2048,192]{1,2,0:T(8,128)(2,1)}, ...), condition=%wide.region_16.17_spmd, body=%wide.region_12.16_spmd.sunk | while | flops 2065499136 | bytes 171613168 | solution.py:270
  586.7 121.9 %while.58 = (s32[]{:T(128)}, f32[2048,3,64]{0,2,1:T(8,128)S(1)}, f32[2048,3,64]{0,2,1:T(8,128)}, bf16[4,512,3,64]{1,3,2,0:T(8,128)(2,1)}, s32[4]{0:T(128)S(1)}, ...) while((s32[]{:T(128)}, f32[2048,3,64]{0,2,1:T(8,128)S(1)}, ...), condition=%wide.region_15.15_spmd.clone, body=%wide.region_13.14_spmd.clone.sunk | while | flops 2064712704 | bytes 114546992 | solution.py:181
  597.1 7.1 multiply_reduce_fusion.9
  604.2 6.9 multiply_convert_fusion.6
  627.9 7.1 multiply_reduce_fusion.9
  635.1 6.9 multiply_convert_fusion.6
  658.8 7.1 multiply_reduce_fusion.9
  665.9 6.9 multiply_convert_fusion.6
  689.6 7.1 multiply_reduce_fusion.9
  696.8 6.9 multiply_convert_fusion.6
  725.1 121.9 %while.58 = (s32[]{:T(128)}, f32[2048,3,64]{0,2,1:T(8,128)S(1)}, f32[2048,3,64]{0,2,1:T(8,128)}, bf16[4,512,3,64]{1,3,2,0:T(8,128)(2,1)}, s32[4]{0:T(128)S(1)}, ...) while((s32[]{:T(128)}, f32[2048,3,64]{0,2,1:T(8,128)S(1)}, ...), condition=%wide.region_15.15_spmd.clone, body=%wide.region_13.14_spmd.clone.sunk | while | flops 2064712704 | bytes 114546992 | solution.py:181
  735.5 7.1 multiply_reduce_fusion.9
  742.6 6.9 multiply_convert_fusion.6
  766.3 7.1 multiply_reduce_fusion.9
  773.5 6.9 multiply_convert_fusion.6
  797.2 7.1 multiply_reduce_fusion.9
  804.3 6.9 multiply_convert_fusion.6
  828.0 7.1 multiply_reduce_fusion.9
  835.2 6.9 multiply_convert_fusion.6
  873.5 11.7 pad_maximum_fusion
  890.6 8.9 convolution_bitcast_fusion
  915.1 9.3 fusion.133
  924.4 36.8 %all-to-all-done.3 = bf16[3,2,2048,192]{3,1,0,2:T(2,128)(2,1)} async-done(((bf16[3,2,2048,192]{3,1,0,2:T(2,128)(2,1)}), bf16[3,2,2048,192]{3,1,0,2:T(2,128)(2,1)}, u32[]{:S(2)}, u32[]{:S(2)}) %all-to-all-start.3) | async-done | bytes 4718624 | tf_op jit(solution)/shard_map/all_to_all | solution.py:273
  961.2 16.2 %copy.237 = bf16[3,2,4,512,192]{3,4,2,1,0:T(8,128)(2,1)} copy(bf16[3,2,4,512,192]{4,1,0,3,2:T(2,128)(2,1)} %bitcast.49) | data formatting | bytes 9437184 | tf_op jit(solution)/shard_map/all_to_all | solution.py:273
  1020.7 8.6 constant_dynamic-update-slice_fusion.5
  1032.4 14.6 %add_convert_fusion = bf16[1024,768]{1,0:T(8,128)(2,1)} fusion(f32[1024,768]{1,0:T(8,128)} %copy-done.6, bf16[96,8,24,128]{3,2,1,0:T(8,128)(2,1)} %bitcast.407, f32[1024,3072]{1,0:T(8,128)} %get-tuple-element.462, f32[3072]{0:T(1024)S(1)} %copy-done.65, f32[768]{0:T(1024)S(1)} %copy-done.67), kind=kOutput, calls=%fused_computation.130 | convolution fusion | flops 4865654784 | bytes 22035456 | tf_op jit(solution)/shard_map/dot_general | solution.py:66
  1049.2 268.4 %reduce-scatter.2.cloned.1.call-done = f32[13,128,128]{2,1,0:T(8,128)} async-done(((f32[416,128,128]{2,1,0:T(8,128)}), f32[13,128,128]{2,1,0:T(8,128)}) %reduce-scatter.2.cloned.1.call-update) | async-done | bytes 851984 | tf_op jit(solution)/shard_map/reduce_scatter | solution.py:316
  1322.8 46.8 %all-reduce = (f32[]{:T(128)}, f32[8832]{0:T(1024)S(1)}) all-reduce(f32[]{:T(128)} %multiply_reduce_fusion.6, f32[8832]{0:T(1024)S(1)} %constant_dynamic-update-slice_fusion.12), channel_id=1, replica_groups=mesh['dp'=8,'seq'=4] {'dp','seq'}, use_global_device_ids=true, to_apply=%region_21.22 | all-reduce | flops 8833 | bytes 70664 | tf_op jit(solution)/shard_map/psum | solution.py:317
  (503 shorter events, 425.4 us)
Async XLA Ops:
  7.2 1365.1 %copy-start = (f32[13,128,128]{2,1,0:T(8,128)S(1)}, f32[13,128,128]{2,1,0:T(8,128)}, u32[]{:S(2)}) copy-start(f32[13,128,128]{2,1,0:T(8,128)} %param.27) | copy-start | bytes 2555908
  7.2 7.3 copy-start.47
  7.2 5.2 copy-start.3
  7.2 107.7 %all-gather.2.cloned.1.call-start = ((), (), s32[]{:S(2)}) async-start(), calls=%async_computation.5 | async-start | bytes 14057472 | tf_op jit(solution)/shard_map/all_gather | solution.py:206
  116.5 8.5 copy-start.22
  121.0 4.7 copy-start.31
  134.1 4.5 copy-start.34
  157.3 59.0 %all-to-all-start = ((bf16[3,2,512,768]{2,1,0,3:T(2,128)(2,1)}), bf16[3,2,512,768]{2,1,0,3:T(2,128)(2,1)}, u32[]{:S(2)}, u32[]{:S(2)}) async-start(bf16[3,2,512,768]{2,1,0,3:T(2,128)(2,1)} %maximum_maximum_fusion), calls=%async_computation | async-start | bytes 9437184 | tf_op jit(solution)/shard_map/all_to_all | solution.py:229
  237.1 5.2 copy-start.71
  445.9 32.1 %all-to-all-start.1 = ((bf16[2,2048,192]{2,0,1:T(2,128)(2,1)}), bf16[2,2048,192]{2,0,1:T(2,128)(2,1)S(1)}, u32[]{:S(2)}, u32[]{:S(2)}) async-start(bf16[2,2048,192]{2,0,1:T(2,128)(2,1)} %copy.225), calls=%async_computation.1 | async-start | bytes 4194304 | tf_op jit(solution)/shard_map/all_to_all | solution.py:233
  479.3 12.4 copy-start.4
  479.3 12.4 copy-start.68
  493.4 45.8 %copy-start.6 = (f32[1024,768]{1,0:T(8,128)}, f32[1024,768]{1,0:T(8,128)S(1)}, u32[]{:S(2)}) copy-start(f32[1024,768]{1,0:T(8,128)S(1)} %get-tuple-element.458) | copy-start | bytes 9437188
  493.5 45.8 %copy-start.43 = (f32[1024]{0:T(1024)}, f32[1024]{0:T(1024)S(1)}, u32[]{:S(2)}) copy-start(f32[1024]{0:T(1024)S(1)} %broadcast_multiply_fusion.6) | copy-start | bytes 12292
  493.5 24.4 %slice-start.5 = ((s8[4718592]{0:T(1024)(128)(4,1)}), s8[4194304]{0:T(1024)(128)(4,1)S(1)}, s32[]{:S(2)}) async-start(s8[4718592]{0:T(1024)(128)(4,1)} %bitcast.408), calls=%async_computation.12 | async-start | bytes 8388608
  494.1 45.2 %copy-start.45 = (f32[1024]{0:T(1024)}, f32[1024]{0:T(1024)S(1)}, u32[]{:S(2)}) copy-start(f32[1024]{0:T(1024)S(1)} %add_rsqrt_fusion) | copy-start | bytes 12292
  495.2 22.7 %copy-start.10 = (bf16[2,512,768]{2,1,0:T(8,128)(2,1)S(1)}, bf16[2,512,768]{2,1,0:T(8,128)(2,1)}, u32[]{:S(2)}) copy-start(bf16[2,512,768]{2,1,0:T(8,128)(2,1)} %get-tuple-element.419) | copy-start | bytes 4718596
  495.2 22.7 %slice-start.6 = ((s8[4718592]{0:T(1024)(128)(4,1)}), s8[524288]{0:T(1024)(128)(4,1)S(1)}, s32[]{:S(2)}) async-start(s8[4718592]{0:T(1024)(128)(4,1)} %bitcast.408), calls=%async_computation.13 | async-start | bytes 1048576
  533.0 6.2 copy-start.14
  544.0 9.3 copy-start.62
  544.0 9.9 copy-start.63
  548.9 24.5 %all-to-all-start.2 = ((bf16[2,512,768]{1,0,2:T(2,128)(2,1)}), bf16[2,512,768]{1,0,2:T(2,128)(2,1)}, u32[]{:S(2)}, u32[]{:S(2)}) async-start(bf16[2,512,768]{1,0,2:T(2,128)(2,1)} %copy.230), calls=%async_computation.2 | async-start | bytes 3145728 | tf_op jit(solution)/shard_map/all_to_all | solution.py:263
  579.7 7.0 copy-start.8
  579.7 7.0 copy-start.41
  579.7 7.0 copy-start.72
  592.4 4.7 copy-start.1
  621.8 6.2 copy-start.1
  652.6 6.2 copy-start.1
  683.5 6.2 copy-start.1
  714.4 3.6 copy-start.9
  714.5 3.6 copy-start.42
  714.5 3.6 copy-start.73
  718.1 7.0 copy-start.8
  718.1 7.0 copy-start.41
  718.1 7.0 copy-start.72
  730.8 4.7 copy-start.1
  760.2 6.2 copy-start.1
  791.0 6.2 copy-start.1
  821.9 6.2 copy-start.1
  852.9 3.6 copy-start.9
  852.9 3.6 copy-start.42
  885.2 5.4 copy-start.44
  885.2 5.4 copy-start.46
  885.2 5.4 copy-start.50
  885.2 5.4 copy-start.52
  885.2 76.0 %all-to-all-start.3 = ((bf16[3,2,2048,192]{3,1,0,2:T(2,128)(2,1)}), bf16[3,2,2048,192]{3,1,0,2:T(2,128)(2,1)}, u32[]{:S(2)}, u32[]{:S(2)}) async-start(bf16[3,2,2048,192]{3,1,0,2:T(2,128)(2,1)} %pad_maximum_fusion), calls=%async_computation.3 | async-start | bytes 12582912 | tf_op jit(solution)/shard_map/all_to_all | solution.py:273
  890.5 427.1 %reduce-scatter.2.cloned.1.call-start = ((), (), s32[]{:S(2)}) async-start(), calls=%async_computation.6 | async-start | bytes 28114944 | tf_op jit(solution)/shard_map/reduce_scatter | solution.py:316
  905.4 9.7 slice-start.3
  909.8 5.3 slice-start.4
  909.8 5.3 copy-start.26
  1010.7 5.8 slice-start
  1010.7 5.8 slice-start.1
  1012.2 4.3 slice-start.2
  1032.4 16.5 %copy-start.70 = (f32[768]{0:T(1024)S(1)}, f32[768]{0:T(1024)}, u32[]{:S(2)}) copy-start(f32[768]{0:T(1024)} %get-tuple-element.333) | copy-start | bytes 9220
  1032.4 16.5 %copy-start.69 = (f32[768]{0:T(1024)S(1)}, f32[768]{0:T(1024)}, u32[]{:S(2)}) copy-start(f32[768]{0:T(1024)} %get-tuple-element.339) | copy-start | bytes 9220
  1032.4 16.5 %copy-start.61 = (f32[768]{0:T(1024)S(1)}, f32[768]{0:T(1024)}, u32[]{:S(2)}) copy-start(f32[768]{0:T(1024)} %get-tuple-element.420) | copy-start | bytes 9220
  1032.4 16.5 %copy-start.60 = (f32[768]{0:T(1024)S(1)}, f32[768]{0:T(1024)}, u32[]{:S(2)}) copy-start(f32[768]{0:T(1024)} %get-tuple-element.418) | copy-start | bytes 9220
  1032.4 16.7 %copy-start.66 = (f32[3072]{0:T(1024)S(1)}, f32[3072]{0:T(1024)}, u32[]{:S(2)}) copy-start(f32[3072]{0:T(1024)} %get-tuple-element.463) | copy-start | bytes 36868
  1047.0 324.5 %copy-start.48 = (f32[8832]{0:T(1024)S(1)}, f32[8832]{0:T(1024)}, u32[]{:S(2)}) copy-start(f32[8832]{0:T(1024)} %param.28) | copy-start | bytes 105988
  1047.0 324.5 %copy-start.55 = (f32[8832]{0:T(1024)S(1)}, f32[8832]{0:T(1024)}, u32[]{:S(2)}) copy-start(f32[8832]{0:T(1024)} %param.29) | copy-start | bytes 105988
  1317.6 54.6 %copy-start.19 = (f32[13,128,128]{2,1,0:T(8,128)S(1)}, f32[13,128,128]{2,1,0:T(8,128)}, u32[]{:S(2)}) copy-start(f32[13,128,128]{2,1,0:T(8,128)} %reduce-scatter.2.cloned.1.call-done) | copy-start | bytes 2555908
  1319.7 54.2 %copy-start.21 = (f32[13,128,128]{1,2,0:T(8,128)S(1)}, f32[13,128,128]{1,2,0:T(8,128)}, u32[]{:S(2)}) copy-start(f32[13,128,128]{1,2,0:T(8,128)} %copy.250) | copy-start | bytes 2555908
  1372.3 9.4 copy-start.7
  1376.9 4.8 copy-start.40
  (49 other events, 107.1 us)
Sparse Core Ops, SparseCore 0:
  11.5 103.4 all-gather.1
  1030.2 287.3 reduce-scatter.1
where the time goes:
time: 1410 us; the launch traced here: 1390 us
  waiting for transfers between devices  465 us (33%)
  matrix products  390 us (28%)
  local copies, waits for them, and re-layouts  260 us (18%)
  other arithmetic  182 us (13%)
  blocking collectives  46.8 us (3%)
  starting transfers between devices  18.8 us (1%)
  between operations  17.8 us (1%)
    reduce_scatter x1, waiting for transfers between devices, per_device(): lax.psum_scatter(grad_stack, ('dp', 'seq'), scatter_dimension=0, tiled=True)  268 us
    all_gather x1, waiting for transfers between devices, per_device(): lax.all_gather(master_tiles.astype(jnp.bfloat16), ('dp', 'seq'), axis=0,...  97.4 us
    dot_general x16, matrix products, one_block(): jnp.einsum('qhd,khd->hqk', query_rows, key_heads, preferred_element_type=...  78.9 us
    dot_general x8, matrix products, one_block(): jnp.einsum('qhd,khd->hqk', grad_rows, value_heads, preferred_element_type...  57.1 us
    convert_element_type x8, other arithmetic, one_block(): score_grad = (probs * (probs_grad - delta)).astype(jnp.bfloat16)  54.9 us
    reduce_sum x8, other arithmetic, one_block(): totals = jnp.sum(exponent, axis=-1, keepdims=True)  54.1 us
    dot_general x8, matrix products, one_block(): jnp.einsum('hqk,khd->qhd', weights, value_heads, preferred_element_type=j...  53.5 us
    all_to_all x1, waiting for transfers between devices, per_device(): lax.all_to_all(packed, 'seq', split_axis=3, concat_axis=2, tiled=True)  53.2 us
  transfers between devices with their start and end apart: 6, of which 5 were waited for; matrix products, arithmetic and copies ran while one was open for 7% of the time, Pallas kernels for 0%

commit v1 on v0

v1 whole, which is shorter than its diff:
```python
import functools

import jax
import jax.numpy as jnp
from jax import lax
from jax.experimental import pallas as pl
from jax.experimental.pallas import tpu as pltpu
from jax.sharding import PartitionSpec as P

D = 768
HD = 64
FF = 3072
VW = 384
TILE = 128
CLIP = 256
LOG2E = 1.4426950408889634
SCALE = HD**-0.5
QUERY_BLOCK = 512
KEY_BLOCK = 512
BACK_QUERY_BLOCK = 512
BACK_KEY_BLOCK = 512
N_QKV = 90
N_OUT = 36
N_HID = 144
N_PROJ = 144
N_REST = N_OUT + N_HID + N_PROJ
FIRST_PROJ = N_QKV + N_OUT + N_HID

highest = lax.Precision.HIGHEST
norm_eps = 1e-05
clip_eps = 1e-06
decay_rate = 0.5
matrix_rate = 0.3
vector_rate = 0.1
moment_eps = 1e-08
masked_score = -1e30

f32 = jnp.float32
bf16 = jnp.bfloat16
NN = (((1,), (0,)), ((), ()))
NT = (((1,), (1,)), ((), ()))
TN = (((0,), (0,)), ((), ()))
VMEM_LIMIT = 60 << 20


def dot(left_in, right_in, dims=NN):
    return lax.dot_general(left_in, right_in, dims, preferred_element_type=f32)


def split_vector(vector):
    pieces = []
    offset = 0
    for length in (D, D, D, D, D, D, D, VW, FF):
        pieces.append(vector[offset : offset + length])
        offset = offset + length
    return pieces


def norm_forward(values, gain_row, shift_row):
    centered = values - jnp.mean(values, axis=-1, keepdims=True)
    variance = jnp.mean(centered * centered, axis=-1, keepdims=True)
    inv_std = lax.rsqrt(variance + norm_eps)
    unit_rows = centered * inv_std
    return (unit_rows * gain_row + shift_row, unit_rows, inv_std)


def norm_backward(grad_in, unit_rows, inv_std, gain_row):
    scaled = grad_in * gain_row
    term = (
        scaled
        - jnp.mean(scaled, axis=-1, keepdims=True)
        - unit_rows * jnp.mean(scaled * unit_rows, axis=-1, keepdims=True)
    )
    return term * inv_std


def whole(shape):
    return pl.BlockSpec(shape, lambda i, *_: (0,) * len(shape))


def params():
    return pltpu.CompilerParams(dimension_semantics=("arbitrary",), vmem_limit_bytes=VMEM_LIMIT)


def attend_forward_kernel(
    heads,
    len_ref,
    fresh_ref,
    x_ref,
    wq_ref,
    wk_ref,
    wv_ref,
    qb_ref,
    vb_ref,
    fv_ref,
    o_ref,
    q_ref,
    k_ref,
    v_ref,
    lse_ref,
    k_heads,
    values,
    acc,
    top,
    total,
):
    blocks, _, span, width_in = x_ref.shape
    count = blocks * span
    length = len_ref[pl.program_id(0)]
    x = x_ref[...].reshape(count, width_in)
    q_ref[0] = (dot(wq_ref[...], x, NT) + qb_ref[...]).astype(bf16)
    keys = dot(x, wk_ref[...], NT).astype(bf16)
    k_ref[0] = keys
    for h in range(heads):
        k_heads[h] = keys[:, h * HD : (h + 1) * HD]

    @pl.when(fresh_ref[0] == 1)
    def _():
        values[...] = (dot(wv_ref[...], x, NT) + vb_ref[...]).astype(bf16)

    @pl.when(fresh_ref[0] == 0)
    def _():
        for b in range(blocks):
            values[:, b * span : (b + 1) * span] = fv_ref[b, 0]

    v_ref[0] = values[...].T
    bq, bk = QUERY_BLOCK, KEY_BLOCK

    def one_query_block(qi, carry):
        q0 = pl.multiple_of(qi * bq, bq)
        top[...] = jnp.full_like(top, masked_score)
        total[...] = jnp.zeros_like(total)
        acc[...] = jnp.zeros_like(acc)

        def step(ki, masked):
            k0 = pl.multiple_of(ki * bk, bk)
            if masked:
                key_pos = k0 + lax.broadcasted_iota(jnp.int32, (bk, bq), 0)
                query_pos = q0 + lax.broadcasted_iota(jnp.int32, (bk, bq), 1)
                allowed = (key_pos <= query_pos) & (key_pos < length)
            for h in range(heads):
                rows = slice(h * HD, (h + 1) * HD)
                s = dot(k_heads[h, pl.ds(k0, bk), :], q_ref[0, rows, pl.ds(q0, bq)])
                s = s * (SCALE * LOG2E)
                if masked:
                    s = jnp.where(allowed, s, masked_score)
                top_old = top[h : h + 1, :]
                top_new = jnp.maximum(top_old, jnp.max(s, axis=0, keepdims=True))
                p = jnp.exp2(s - top_new)
                fade = jnp.exp2(top_old - top_new)
                top[h : h + 1, :] = top_new
                total[h : h + 1, :] = total[h : h + 1, :] * fade + jnp.sum(
                    p, axis=0, keepdims=True
                )
                acc[rows, :] = acc[rows, :] * fade + dot(
                    values[rows, pl.ds(k0, bk)], p.astype(bf16)
                )

        plain = jnp.minimum(q0, length) // bk
        end = (jnp.minimum(q0 + bq, length) + bk - 1) // bk
        lax.fori_loop(0, plain, lambda i, c: (step(i, False), c)[1], 0)
        lax.fori_loop(plain, end, lambda i, c: (step(i, True), c)[1], 0)
        for h in range(heads):
            rows = slice(h * HD, (h + 1) * HD)
            sums = total[h : h + 1, :]
            o_ref[qi, 0, rows, :] = (acc[rows, :] / sums).astype(bf16)
            lse_ref[0, h : h + 1, pl.ds(q0, bq)] = top[h : h + 1, :] + jnp.log2(sums)
        return carry

    lax.fori_loop(0, count // bq, one_query_block, 0)


def attend_forward(lengths, fresh, x, wq, wk, wv, qb, vb, fv):
    blocks, seqs, span, _ = x.shape
    width = wq.shape[0]
    heads = width // HD
    count = blocks * span
    one = lambda shape: pl.BlockSpec((1,) + shape, lambda i, *_: (i,) + (0,) * len(shape))
    mid = lambda shape: pl.BlockSpec((blocks, 1) + shape, lambda i, *_: (0, i, 0, 0))
    return pl.pallas_call(
        functools.partial(attend_forward_kernel, heads),
        grid_spec=pltpu.PrefetchScalarGridSpec(
            num_scalar_prefetch=2,
            grid=(seqs,),
            in_specs=[mid((span, D))]
            + [whole((width, D))] * 3
            + [whole((width, 1))] * 2
            + [mid((width, span))],
            out_specs=[
                mid((width, span)),
                one((width, count)),
                one((count, width)),
                one((count, width)),
                one((8, count)),
            ],
            scratch_shapes=[
                pltpu.VMEM((heads, count, HD), bf16),
                pltpu.VMEM((width, count), bf16),
                pltpu.VMEM((width, QUERY_BLOCK), f32),
                pltpu.VMEM((8, QUERY_BLOCK), f32),
                pltpu.VMEM((8, QUERY_BLOCK), f32),
            ],
        ),
        out_shape=[
            jax.ShapeDtypeStruct((blocks, seqs, width, span), bf16),
            jax.ShapeDtypeStruct((seqs, width, count), bf16),
            jax.ShapeDtypeStruct((seqs, count, width), bf16),
            jax.ShapeDtypeStruct((seqs, count, width), bf16),
            jax.ShapeDtypeStruct((seqs, 8, count), f32),
        ],
        compiler_params=params(),
        cost_estimate=pl.CostEstimate(
            flops=40_000_000_000, bytes_accessed=20_000_000, transcendentals=0
        ),
        name="attend_forward",
    )(lengths, fresh, x, wq, wk, wv, qb, vb, fv)


def attend_backward_kernel(
    heads,
    len_ref,
    fresh_ref,
    q_ref,
    k_ref,
    v_ref,
    o_ref,
    g_ref,
    lse_ref,
    x_ref,
    w_ref,
    dx_ref,
    dv_ref,
    dw_ref,
    db_ref,
    k_heads,
    v_heads,
    q_heads,
    g_heads,
    k_turned,
    g_turned,
    dq_acc,
    delta,
    grads,
    dk_acc,
    dv_acc,
):
    n = pl.program_id(0)
    blocks, _, span, width_in = x_ref.shape
    count = blocks * span
    width = heads * HD
    length = len_ref[n]
    bq, bk = BACK_QUERY_BLOCK, BACK_KEY_BLOCK
    delta[...] = jnp.zeros_like(delta)
    for h in range(heads):
        rows = slice(h * HD, (h + 1) * HD)
        k_heads[h] = k_ref[0, :, rows]
        v_heads[h] = v_ref[0, :, rows]
        q_heads[h] = q_ref[0, rows, :].T
    for b in range(blocks):
        at = slice(b * span, (b + 1) * span)
        g_block = g_ref[b, 0]
        g_turned[:, at] = g_block
        product = o_ref[b, 0].astype(f32) * g_block.astype(f32)
        for h in range(heads):
            rows = slice(h * HD, (h + 1) * HD)
            g_heads[h, at, :] = g_block[rows, :].T
            delta[h : h + 1, at] = jnp.sum(product[rows, :], axis=0, keepdims=True)
    k_turned[...] = k_ref[0].T
    dq_acc[...] = jnp.zeros_like(dq_acc)
    grads[...] = jnp.zeros_like(grads)
    key_blocks = (length + bk - 1) // bk
    query_blocks = (length + bq - 1) // bq

    def one_key_block(ki, carry):
        k0 = pl.multiple_of(ki * bk, bk)
        dk_acc[...] = jnp.zeros_like(dk_acc)
        dv_acc[...] = jnp.zeros_like(dv_acc)

        def step(qi, masked):
            q0 = pl.multiple_of(qi * bq, bq)
            at = pl.ds(q0, bq)
            if masked:
                key_pos = k0 + lax.broadcasted_iota(jnp.int32, (bk, bq), 0)
                query_pos = q0 + lax.broadcasted_iota(jnp.int32, (bk, bq), 1)
                allowed = (key_pos <= query_pos) & (key_pos < length)
            for h in range(heads):
                rows = slice(h * HD, (h + 1) * HD)
                s = dot(k_heads[h, pl.ds(k0, bk), :], q_ref[0, rows, at])
                dp = dot(v_heads[h, pl.ds(k0, bk), :], g_turned[rows, at])
                p = jnp.exp2(s * (SCALE * LOG2E) - lse_ref[0, h : h + 1, at])
                if masked:
                    p = jnp.where(allowed, p, 0.0)
                ds = (p * (dp - delta[h : h + 1, at])).astype(bf16)
                dv_acc[h] = dv_acc[h] + dot(p.astype(bf16), g_heads[h, at, :])
                dk_acc[h] = dk_acc[h] + dot(ds, q_heads[h, at, :])
                dq_acc[rows, at] = dq_acc[rows, at] + dot(k_turned[rows, pl.ds(k0, bk)], ds)

        first = k0 // bq
        plain = jnp.where(k0 + bk <= length, (k0 + bk + bq - 1) // bq, query_blocks)
        plain = jnp.minimum(plain, query_blocks)
        lax.fori_loop(first, plain, lambda i, c: (step(i, True), c)[1], 0)
        lax.fori_loop(plain, query_blocks, lambda i, c: (step(i, False), c)[1], 0)
        for h in range(heads):
            grads[pl.ds(k0, bk), width + h * HD : width + (h + 1) * HD] = (
                dk_acc[h] * SCALE
            ).astype(bf16)
            grads[pl.ds(k0, bk), 2 * width + h * HD : 2 * width + (h + 1) * HD] = dv_acc[h].astype(
                bf16
            )
        return carry

    lax.fori_loop(0, key_blocks, one_key_block, 0)
    grads[:, 0:width] = (dq_acc[...] * SCALE).astype(bf16).T
    for b in range(blocks):
        dv_ref[b, 0] = grads[b * span : (b + 1) * span, 2 * width : 3 * width].T

    @pl.when(fresh_ref[0] == 0)
    def _():
        grads[:, 2 * width : 3 * width] = jnp.zeros((count, width), bf16)

    dx_ref[...] = dot(grads[...], w_ref[...]).astype(bf16).reshape(dx_ref.shape)
    dw = dot(grads[...], x_ref[...].reshape(count, width_in), TN)
    db = jnp.sum(grads[...].astype(f32), axis=0, keepdims=True)

    @pl.when(n == 0)
    def _():
        dw_ref[...] = dw
        db_ref[...] = db

    @pl.when(n > 0)
    def _():
        dw_ref[...] += dw
        db_ref[...] += db


def attend_backward(lengths, fresh, q, k, v, o, g, lse, x, w):
    blocks, seqs, span, _ = x.shape
    width = q.shape[1]
    heads = width // HD
    count = blocks * span
    one = lambda shape: pl.BlockSpec((1,) + shape, lambda i, *_: (i,) + (0,) * len(shape))
    mid = lambda shape: pl.BlockSpec((blocks, 1) + shape, lambda i, *_: (0, i, 0, 0))
    return pl.pallas_call(
        functools.partial(attend_backward_kernel, heads),
        grid_spec=pltpu.PrefetchScalarGridSpec(
            num_scalar_prefetch=2,
            grid=(seqs,),
            in_specs=[
                one((width, count)),
                one((count, width)),
                one((count, width)),
                mid((width, span)),
                mid((width, span)),
                one((8, count)),
                mid((span, D)),
                whole((3 * width, D)),
            ],
            out_specs=[
                mid((span, D)),
                mid((width, span)),
                whole((3 * width, D)),
                whole((1, 3 * width)),
            ],
            scratch_shapes=[pltpu.VMEM((heads, count, HD), bf16)] * 4
            + [
                pltpu.VMEM((width, count), bf16),
                pltpu.VMEM((width, count), bf16),
                pltpu.VMEM((width, count), f32),
                pltpu.VMEM((8, count), f32),
                pltpu.VMEM((count, 3 * width), bf16),
                pltpu.VMEM((heads, BACK_KEY_BLOCK, HD), f32),
                pltpu.VMEM((heads, BACK_KEY_BLOCK, HD), f32),
            ],
        ),
        out_shape=[
            jax.ShapeDtypeStruct((blocks, seqs, span, D), bf16),
            jax.ShapeDtypeStruct((blocks, seqs, width, span), bf16),
            jax.ShapeDtypeStruct((3 * width, D), f32),
            jax.ShapeDtypeStruct((1, 3 * width), f32),
        ],
        compiler_params=params(),
        cost_estimate=pl.CostEstimate(
            flops=70_000_000_000, bytes_accessed=25_000_000, transcendentals=0
        ),
        name="attend_backward",
    )(lengths, fresh, q, k, v, o, g, lse, x, w)


HIDDEN_CHUNK = 512
GELU_A = 0.7978845608028654
GELU_B = 0.044715


def feed_forward_kernel(
    len_ref,
    pos_ref,
    att_ref,
    tok_ref,
    cot_ref,
    tiles_ref,
    rows_ref,
    hb_ref,
    out_ref,
    rg_ref,
    ag_ref,
    act_ref,
    hg_ref,
    nt_ref,
    bg_ref,
    og_ref,
    sums_ref,
    hsum_ref,
    tiles,
    w_out,
    w_hidden,
    w_proj,
    sem,
):
    n = pl.program_id(0)
    span = tok_ref.shape[1]

    @pl.when(n == 0)
    def _():
        copies = []
        for i, (start, amount) in enumerate(
            ((0, N_OUT), (N_OUT, N_HID), (N_OUT + N_HID, N_PROJ))
        ):
            copy = pltpu.make_async_copy(
                tiles_ref.at[pl.ds(N_QKV + start, amount)],
                tiles.at[pl.ds(start, amount)],
                sem.at[i],
            )
            copy.start()
            copies.append(copy)
        for copy, start, matrix in zip(
            copies, (0, N_OUT, N_OUT + N_HID), (w_out, w_hidden, w_proj)
        ):
            copy.wait()
            row_tiles, col_tiles = matrix.shape[0] // TILE, matrix.shape[1] // TILE
            for r in range(row_tiles):
                for c in range(col_tiles):
                    matrix[r * TILE : (r + 1) * TILE, c * TILE : (c + 1) * TILE] = tiles[
                        start + r * col_tiles + c
                    ]
        sums_ref[...] = jnp.zeros_like(sums_ref)
        hsum_ref[...] = jnp.zeros_like(hsum_ref)

    gain_two, shift_two = rows_ref[0:1, :], rows_ref[1:2, :]
    out_bias, proj_bias = rows_ref[2:3, :], rows_ref[3:4, :]
    attended = att_ref[...].reshape(D, span)
    residual = tok_ref[0].astype(f32) + dot(attended, w_out[...], TN) + out_bias
    normed, unit, inv = norm_forward(residual, gain_two, shift_two)
    normed = normed.astype(bf16)
    nt_ref[...] = normed
    live = pos_ref[0] + lax.broadcasted_iota(jnp.int32, (span, 1), 0) < len_ref[n]
    out_grad = jnp.where(live, cot_ref[0].astype(f32), 0.0)
    out_grad_low = out_grad.astype(bf16)
    og_ref[...] = out_grad_low
    output = residual + proj_bias
    norm_in = jnp.zeros((span, D), f32)
    for c in range(FF // HIDDEN_CHUNK):
        cols = slice(c * HIDDEN_CHUNK, (c + 1) * HIDDEN_CHUNK)
        hidden = dot(normed, w_hidden[:, cols]) + hb_ref[:, cols]
        square = hidden * hidden
        bend = jnp.tanh(GELU_A * (hidden + GELU_B * (hidden * square)))
        active = (0.5 * hidden * (1.0 + bend)).astype(bf16)
        slope = 0.5 * (1.0 + bend) + 0.5 * hidden * (1.0 - bend * bend) * (
            GELU_A * (1.0 + (3.0 * GELU_B) * square)
        )
        act_ref[:, cols] = active
        hidden_grad = (dot(out_grad_low, w_proj[cols, :], NT) * slope).astype(bf16)
        hg_ref[:, cols] = hidden_grad
        hsum_ref[:, cols] += jnp.sum(hidden_grad.astype(f32), axis=0, keepdims=True)
        output = output + dot(active, w_proj[cols, :])
        norm_in = norm_in + dot(hidden_grad, w_hidden[:, cols], NT)
    out_ref[0] = output.astype(bf16)
    residual_grad = out_grad + norm_backward(norm_in, unit, inv, gain_two)
    rg_ref[0] = residual_grad
    branch = residual_grad.astype(bf16)
    bg_ref[...] = branch
    ag_ref[...] = dot(w_out[...], branch, NT).astype(bf16).reshape(ag_ref.shape)
    sums_ref[0:1, :] += jnp.sum(norm_in * unit, axis=0, keepdims=True)
    sums_ref[1:2, :] += jnp.sum(norm_in, axis=0, keepdims=True)
    sums_ref[2:3, :] += jnp.sum(branch.astype(f32), axis=0, keepdims=True)
    sums_ref[3:4, :] += jnp.sum(out_grad, axis=0, keepdims=True)


def feed_forward(lengths, position, att, tokens, cotangent, tiles, rows, hidden_bias):
    groups, seqs, width, span = att.shape
    one = lambda shape: pl.BlockSpec((1,) + shape, lambda i, *_: (i,) + (0,) * len(shape))
    mid = lambda shape: pl.BlockSpec((groups, 1) + shape, lambda i, *_: (0, i, 0, 0))
    row = lambda cols: pl.BlockSpec((span, cols), lambda i, *_: (i, 0))
    total = seqs * span
    return pl.pallas_call(
        feed_forward_kernel,
        grid_spec=pltpu.PrefetchScalarGridSpec(
            num_scalar_prefetch=2,
            grid=(seqs,),
            in_specs=[
                mid((width, span)),
                one((span, D)),
                one((span, D)),
                pl.BlockSpec(memory_space=pl.ANY),
                whole((8, D)),
                whole((1, FF)),
            ],
            out_specs=[
                one((span, D)),
                one((span, D)),
                mid((width, span)),
                row(FF),
                row(FF),
                row(D),
                row(D),
                row(D),
                whole((8, D)),
                whole((1, FF)),
            ],
            scratch_shapes=[
                pltpu.VMEM((N_REST, TILE, TILE), bf16),
                pltpu.VMEM((D, D), bf16),
                pltpu.VMEM((D, FF), bf16),
                pltpu.VMEM((FF, D), bf16),
                pltpu.SemaphoreType.DMA((3,)),
            ],
        ),
        out_shape=[
            jax.ShapeDtypeStruct((seqs, span, D), bf16),
            jax.ShapeDtypeStruct((seqs, span, D), f32),
            jax.ShapeDtypeStruct((groups, seqs, width, span), bf16),
            jax.ShapeDtypeStruct((total, FF), bf16),
            jax.ShapeDtypeStruct((total, FF), bf16),
            jax.ShapeDtypeStruct((total, D), bf16),
            jax.ShapeDtypeStruct((total, D), bf16),
            jax.ShapeDtypeStruct((total, D), bf16),
            jax.ShapeDtypeStruct((8, D), f32),
            jax.ShapeDtypeStruct((1, FF), f32),
        ],
        compiler_params=params(),
        cost_estimate=pl.CostEstimate(
            flops=24_000_000_000, bytes_accessed=40_000_000, transcendentals=0
        ),
        name="feed_forward",
    )(lengths, position, att, tokens, cotangent, tiles, rows, hidden_bias)


GRAD_CHUNK = 256


def weight_grad_kernel(
    att_ref, bg_ref, og_ref, nt_ref, act_ref, hg_ref, out_ref, hid_ref, proj_ref, og_turned, nt_turned
):
    i = pl.program_id(0)
    groups, seqs, width, span = att_ref.shape

    @pl.when(i == 0)
    def _():
        og_turned[...] = og_ref[...].T
        nt_turned[...] = nt_ref[...].T
        total = jnp.zeros((D, D), f32)
        for s in range(seqs):
            total = total + dot(
                att_ref[:, s].reshape(groups * width, span), bg_ref[s * span : (s + 1) * span, :]
            )
        total = total.astype(bf16)
        for r in range(D // TILE):
            for c in range(D // TILE):
                out_ref[r * (D // TILE) + c] = total[
                    r * TILE : (r + 1) * TILE, c * TILE : (c + 1) * TILE
                ]

    proj = dot(og_turned[...], act_ref[...]).astype(bf16)
    hid = dot(nt_turned[...], hg_ref[...]).astype(bf16)
    for c in range(GRAD_CHUNK // TILE):
        for r in range(D // TILE):
            rows, cols = slice(r * TILE, (r + 1) * TILE), slice(c * TILE, (c + 1) * TILE)
            proj_ref[c * (D // TILE) + r] = proj[rows, cols]
            hid_ref[r, c] = hid[rows, cols]


def weight_grads(att, bg, og, nt, act, hg):
    total = bg.shape[0]
    chunks = FF // GRAD_CHUNK
    per = GRAD_CHUNK // TILE
    return pl.pallas_call(
        weight_grad_kernel,
        grid=(chunks,),
        in_specs=[
            whole(att.shape),
            whole(bg.shape),
            whole(og.shape),
            whole(nt.shape),
            pl.BlockSpec((total, GRAD_CHUNK), lambda i: (0, i)),
            pl.BlockSpec((total, GRAD_CHUNK), lambda i: (0, i)),
        ],
        out_specs=[
            whole((N_OUT, TILE, TILE)),
            pl.BlockSpec((D // TILE, per, TILE, TILE), lambda i: (0, i, 0, 0)),
            pl.BlockSpec((per * (D // TILE), TILE, TILE), lambda i: (i, 0, 0)),
        ],
        out_shape=[
            jax.ShapeDtypeStruct((N_OUT, TILE, TILE), bf16),
            jax.ShapeDtypeStruct((D // TILE, FF // TILE, TILE, TILE), bf16),
            jax.ShapeDtypeStruct((N_PROJ, TILE, TILE), bf16),
        ],
        scratch_shapes=[pltpu.VMEM((D, total), bf16), pltpu.VMEM((D, total), bf16)],
        compiler_params=params(),
        cost_estimate=pl.CostEstimate(
            flops=12_000_000_000, bytes_accessed=40_000_000, transcendentals=0
        ),
        name="weight_grads",
    )(att, bg, og, nt, act, hg)


def per_device(
    tokens,
    first_values,
    cotangent,
    lengths,
    master_tiles,
    left_stat,
    right_stat,
    left_root,
    right_root,
    vector_params,
    vector_stat,
):
    seqs, span, _ = tokens.shape
    owned_count = master_tiles.shape[0]
    groups = lax.axis_size("seq")
    me_seq = lax.axis_index("seq")
    me = lax.axis_index("dp") * groups + me_seq
    width = D // groups
    fresh_groups = VW // width
    total_tiles = owned_count * groups * lax.axis_size("dp")

    (
        gain_one,
        shift_one,
        gain_two,
        shift_two,
        query_bias,
        out_bias,
        proj_bias,
        value_bias,
        hidden_bias,
    ) = split_vector(vector_params)

    gathered = lax.all_gather(master_tiles.astype(bf16), ("dp", "seq"), axis=0, tiled=True)
    flat_tokens = tokens.reshape(-1, D).astype(f32)
    normed_one, unit_one, inv_one = norm_forward(flat_tokens, gain_one, shift_one)
    normed_one = normed_one.astype(bf16).reshape(seqs, span, D)
    x_all = lax.all_gather(normed_one, "seq", axis=0, tiled=False)
    first_turned = first_values.transpose(2, 0, 1).reshape(groups - fresh_groups, width, seqs, span)
    first_turned = first_turned.transpose(0, 2, 1, 3)
    first_send = jnp.concatenate(
        [jnp.zeros((fresh_groups,) + first_turned.shape[1:], bf16), first_turned], axis=0
    )
    first_mine = lax.all_to_all(first_send, "seq", 0, 0, tiled=True)

    is_fresh = (me_seq < fresh_groups).astype(jnp.int32).reshape(1)
    fresh_seq = jnp.minimum(me_seq, fresh_groups - 1)

    def turned(start, cols):
        amount = D // TILE * (cols // TILE)
        tiles = gathered[start : start + amount].reshape(D // TILE, cols // TILE, TILE, TILE)
        return tiles.transpose(1, 3, 0, 2).reshape(cols, D)

    wq = lax.dynamic_slice_in_dim(turned(0, D), me_seq * width, width, 0)
    wk = lax.dynamic_slice_in_dim(turned(N_OUT, D), me_seq * width, width, 0)
    wv = lax.dynamic_slice_in_dim(turned(2 * N_OUT, VW), fresh_seq * width, width, 0)
    qb = lax.dynamic_slice_in_dim(query_bias, me_seq * width, width, 0).reshape(width, 1)
    vb = lax.dynamic_slice_in_dim(value_bias, fresh_seq * width, width, 0).reshape(width, 1)

    o_heads, q, k, v, lse = attend_forward(
        lengths, is_fresh, x_all, wq, wk, wv, qb, vb, first_mine
    )
    att = lax.all_to_all(o_heads, "seq", 0, 0, tiled=True)
    rows = jnp.concatenate(
        [jnp.stack([gain_two, shift_two, out_bias, proj_bias]), jnp.zeros((4, D), f32)]
    )
    position = (me_seq * span).astype(jnp.int32).reshape(1)
    (
        block_output,
        residual_grad,
        att_grad,
        act,
        hidden_grad,
        normed_two,
        branch_grad,
        out_grad,
        row_sums,
        hidden_bias_grad,
    ) = feed_forward(
        lengths, position, att, tokens, cotangent, gathered, rows, hidden_bias.reshape(1, FF)
    )
    g_heads = lax.all_to_all(att_grad, "seq", 0, 0, tiled=True)
    grad_out, grad_hidden, grad_proj = weight_grads(
        att, branch_grad, out_grad, normed_two, act, hidden_grad
    )
    w_mine = jnp.concatenate([wq, wk, wv], axis=0)
    dx, dv, dw, db = attend_backward(
        lengths, is_fresh, q, k, v, o_heads, g_heads, lse, x_all, w_mine
    )
    norm_one_in = (
        lax.psum_scatter(dx, "seq", scatter_dimension=0, tiled=True)
        .reshape(-1, D)
        .astype(f32)
    )
    dv_back = lax.all_to_all(dv, "seq", 0, 0, tiled=True)
    first_grad = (
        dv_back[fresh_groups:]
        .transpose(1, 3, 0, 2)
        .reshape(first_values.shape)
        .astype(f32)
    )
    token_part = norm_backward(norm_one_in, unit_one, inv_one, gain_one)
    tokens_grad = residual_grad + token_part.reshape(tokens.shape)
    gain_one_grad = jnp.sum(norm_one_in * unit_one, axis=0)
    shift_one_grad = jnp.sum(norm_one_in, axis=0)

    dw = dw.astype(bf16)
    big = jnp.zeros((2 * D, D), bf16)
    big = lax.dynamic_update_slice(big, dw[0:width], (me_seq * width, 0))
    big = lax.dynamic_update_slice(big, dw[width : 2 * width], (D + me_seq * width, 0))
    small = lax.dynamic_update_slice(
        jnp.zeros((VW, D), bf16), dw[2 * width :], (fresh_seq * width, 0)
    )

    def turned_tiles(matrix):
        cols = matrix.shape[0]
        return (
            matrix.reshape(cols // TILE, TILE, D // TILE, TILE)
            .transpose(2, 0, 1, 3)
            .reshape(-1, TILE, TILE)
        )

    grad_stack = jnp.concatenate(
        [
            turned_tiles(big[:D]),
            turned_tiles(big[D:]),
            turned_tiles(small),
            grad_out,
            grad_hidden.reshape(N_HID, TILE, TILE),
            grad_proj,
            jnp.zeros((total_tiles - N_QKV - N_REST, TILE, TILE), bf16),
        ],
        axis=0,
    )
    owned = lax.psum_scatter(grad_stack, ("dp", "seq"), scatter_dimension=0, tiled=True)
    index = me * owned_count + jnp.arange(owned_count)
    flipped = (index < N_QKV) | (index >= FIRST_PROJ)
    owned = owned.astype(f32)
    owned = jnp.where(flipped[:, None, None], owned.swapaxes(1, 2), owned)

    query_bias_grad = lax.dynamic_update_slice(
        jnp.zeros((D,), f32), db[0, 0:width], (me_seq * width,)
    )
    value_bias_grad = lax.dynamic_update_slice(
        jnp.zeros((VW,), f32), db[0, 2 * width :], (fresh_seq * width,)
    )
    vector_local = jnp.concatenate(
        [
            gain_one_grad,
            shift_one_grad,
            row_sums[0],
            row_sums[1],
            query_bias_grad,
            row_sums[2],
            row_sums[3],
            value_bias_grad,
            hidden_bias_grad[0],
        ]
    )
    summed_vector, owned_square = lax.psum((vector_local, jnp.sum(owned * owned)), ("dp", "seq"))
    grad_norm = jnp.sqrt(owned_square + jnp.sum(summed_vector * summed_vector))
    factor = jnp.minimum(1.0, CLIP / (grad_norm + clip_eps))
    clipped = owned * factor
    left_gram = jnp.einsum("tij,tkj->tik", clipped, clipped, precision=highest)
    right_gram = jnp.einsum("tji,tjk->tik", clipped, clipped, precision=highest)
    inner = jnp.einsum("tij,tjk->tik", clipped, right_root, precision=highest)
    step = jnp.einsum("tij,tjk->tik", left_root, inner, precision=highest)
    left_new = decay_rate * left_stat + (1.0 - decay_rate) * left_gram
    right_new = decay_rate * right_stat + (1.0 - decay_rate) * right_gram
    tiles_new = master_tiles - matrix_rate * step
    vector_grads = summed_vector * factor
    vector_stat_new = decay_rate * vector_stat + (1.0 - decay_rate) * vector_grads * vector_grads
    vector_new = vector_params - vector_rate * vector_grads / (
        jnp.sqrt(vector_stat_new) + moment_eps
    )
    return (
        block_output,
        tokens_grad,
        first_grad,
        clipped,
        left_new,
        right_new,
        tiles_new,
        vector_grads,
        vector_stat_new,
        vector_new,
        grad_norm,
    )


def solution(mesh):
    tiles = P(("dp", "seq"), None, None)
    seqs = P("dp", "seq", None)
    in_specs = (seqs, seqs, seqs, P("dp"), tiles, tiles, tiles, tiles, tiles, P(), P())
    out_specs = (seqs, seqs, seqs, tiles, tiles, tiles, tiles, P(), P(), P(), P())
    return jax.shard_map(
        per_device, mesh=mesh, in_specs=in_specs, out_specs=out_specs, check_vma=False
    )
```

time: 1410 us -> 685 us (0.49)
  matrix products: 390 us -> 10.1 us
  local copies, waits for them, and re-layouts: 260 us -> 53.3 us
  other arithmetic: 182 us -> 18.7 us
  Pallas kernels: 0 us -> 145 us
  waiting for transfers between devices: 465 us -> 383 us
    dot_general x74 -> x0, matrix products: 379 us -> none  [the longest x16 78.9 us: one_block(): jnp.einsum('qhd,khd->hqk', query_rows, key_heads, preferred_element_type=...]
    pallas_call x0 -> x4, Pallas kernels: none -> 145 us  [the longest x1 51.1 us: feed_forward(): pl.pallas_call(feed_forward_kernel, grid_spec=pltpu.PrefetchScalarGridSpe...]
    reduce_scatter x1, waiting for transfers between devices: 268 us -> 166 us  [per_device(): lax.psum_scatter(grad_stack, ('dp', 'seq'), scatter_dimension=0, tiled=True)]
    reduce_sum x12 -> x1, other arithmetic: 61.7 us -> 2.78 us  [per_device(): gain_one_grad = jnp.sum(norm_one_in * unit_one, axis=0)]
    convert_element_type x14 -> x4, other arithmetic: 62.3 us -> 4.21 us  [the longest x1 2.14 us: per_device(): master_tiles.astype(bf16)]
    all_to_all x4, waiting for transfers between devices: 98.7 us -> 64.9 us  [the longest x1 27.2 us: per_device(): dv_back = lax.all_to_all(dv, 'seq', 0, 0, tiled=True)]
    while x80 -> x0, local copies, waits for them, and re-layouts: 32.8 us -> none  [the longest x3 16.8 us: per_device(): lax.map(attend_backward, (head_data[0], head_data[1], head_data[2], grad_...]
    all_gather x1 -> x2, waiting for transfers between devices: 97.4 us -> 130 us  [the longest x1 95.9 us: per_device(): lax.all_gather(master_tiles.astype(bf16), ('dp', 'seq'), axis=0, tiled=True)]
  transfers between devices with their start and end apart: 6 -> 8, of which waited for: 5 -> 7; matrix products, arithmetic and copies ran while one was open for 7% -> 8% of each run, Pallas kernels for 0% -> 3%
where the time goes in v1:
time: 685 us; the launch traced here: 681 us
  waiting for transfers between devices  383 us (56%)
  Pallas kernels  145 us (21%)
  local copies, waits for them, and re-layouts  53.3 us (8%)
  blocking collectives  37.7 us (6%)
  other arithmetic  18.7 us (3%)
  between operations  17.4 us (3%)
  starting transfers between devices  15.5 us (2%)
  matrix products  10.1 us (1%)
    reduce_scatter x1, waiting for transfers between devices, per_device(): lax.psum_scatter(grad_stack, ('dp', 'seq'), scatter_dimension=0, tiled=True)  166 us
    all_gather x1, waiting for transfers between devices, per_device(): lax.all_gather(master_tiles.astype(bf16), ('dp', 'seq'), axis=0, tiled=True)  95.9 us
    pallas_call x1, Pallas kernels, feed_forward(): pl.pallas_call(feed_forward_kernel, grid_spec=pltpu.PrefetchScalarGridSpe...  51.1 us
    pallas_call x1, Pallas kernels, attend_backward(): pl.pallas_call(functools.partial(attend_backward_kernel, heads), grid_spe...  38.9 us
    psum x1, blocking collectives, per_device(): lax.psum((vector_local, jnp.sum(owned * owned)), ('dp', 'seq'))  37.7 us
    pallas_call x1, Pallas kernels, attend_forward(): pl.pallas_call(functools.partial(attend_forward_kernel, heads), grid_spec...  34.4 us
    all_gather x1, waiting for transfers between devices, per_device(): x_all = lax.all_gather(normed_one, 'seq', axis=0, tiled=False)  33.7 us
    all_to_all x1, waiting for transfers between devices, per_device(): dv_back = lax.all_to_all(dv, 'seq', 0, 0, tiled=True)  27.2 us
  transfers between devices with their start and end apart: 8, of which 7 were waited for; matrix products, arithmetic and copies ran while one was open for 8% of the time, Pallas kernels for 3%

profile of v1, /device:TPU:0, one launch (start us, length us, event | category | flops | bytes accessed | tf_op | source)
XLA Modules:
  0.0 680.7 jit_solution(4959385019214051742)
XLA Ops:
  7.3 2.1 convert_element_type.52
  9.5 1.7 convert_reduce_fusion.1
  11.2 0.6 fusion.13
  11.9 1.8 fusion.9
  14.1 1.3 concatenate.15
  15.3 4.3 all-to-all-start
  19.8 0.8 copy.50.qb_ref
  20.6 0.8 copy.51.vb_ref
  21.4 95.9 %all-gather.4.cloned.1.call-done.tiles_ref = bf16[416,128,128]{2,1,0:T(8,128)(2,1)} async-done(((bf16[13,128,128]{2,1,0:T(8,128)(2,1)}), bf16[416,128,128]{2,1,0:T(8,128)(2,1)}) %all-gather.4.cloned.1.call-update) | async-done | bytes 13631504 | tf_op jit(solution)/shard_map/all_gather | solution.py:649
  117.3 3.3 fusion.23
  120.6 1.9 copy.46
  122.5 1.2 copy.71
  123.8 2.1 copy.45
  125.8 1.2 copy.72
  127.6 0.7 constant_dynamic-slice_fusion.wv_ref
  128.3 1.9 constant_dynamic-slice_fusion.1
  130.3 33.7 %all-gather.6.cloned.1.call-done = bf16[8,512,768]{2,1,0:T(8,128)(2,1)} async-done(((bf16[2,512,768]{2,1,0:T(8,128)(2,1)}), bf16[8,512,768]{2,1,0:T(8,128)(2,1)}) %all-gather.6.cloned.1.call-update) | async-done | bytes 6291472 | tf_op jit(solution)/shard_map/all_gather | solution.py:653
  164.0 34.4 %attend_forward.1 = (bf16[4,2,192,512]{3,2,1,0:T(8,128)(2,1)}, bf16[2,192,2048]{2,1,0:T(8,128)(2,1)}, bf16[2,2048,192]{2,1,0:T(8,128)(2,1)}, bf16[2,2048,192]{2,1,0:T(8,128)(2,1)}, f32[2,8,2048]{2,1,0:T(8,128)}) custom-call(s32[2]{0:T(128)} %len_ref.5, s32[1]{0:T(128)} %bitcast.1.fresh_ref, bf16[4,2,512,768]{3,2,1,0:T(8,128)(2,1)} %bitcast.111, ...), custom_call_target="tpu_custom_call" | custom-call | flops 40000000000 | bytes 20000000 | tf_op jit(solution)/shard_map/attend_forward/pallas_call | solution.py:180
  198.4 3.6 all-to-all-start.1
  202.0 0.6 slice.83
  202.6 0.6 concatenate.16.rows_ref
  203.3 18.8 %all-to-all-done.1.att_ref = bf16[4,2,192,512]{3,2,1,0:T(8,128)(2,1)S(1)} async-done(((bf16[4,2,192,512]{3,2,1,0:T(8,128)(2,1)}), bf16[4,2,192,512]{3,2,1,0:T(8,128)(2,1)S(1)}, u32[]{:S(2)}, u32[]{:S(2)}) %all-to-all-start.1) | async-done | bytes 1572896 | tf_op jit(solution)/shard_map/all_to_all | solution.py:678
  222.0 1.2 copy-done.9
  223.2 51.1 %feed_forward.1 = (bf16[2,512,768]{2,1,0:T(8,128)(2,1)}, f32[2,512,768]{2,1,0:T(8,128)}, bf16[4,2,192,512]{3,2,1,0:T(8,128)(2,1)}, bf16[1024,3072]{1,0:T(8,128)(...) custom-call(s32[2]{0:T(128)} %len_ref.5, ...), custom_call_target="tpu_custom_call" | custom-call | flops 24000000000 | bytes 40000000 | tf_op jit(solution)/shard_map/feed_forward/pallas_call | solution.py:494
  274.4 3.7 all-to-all-start.2
  278.1 1.0 pad_maximum_fusion.w_ref
  279.1 19.0 %all-to-all-done.2.g_ref = bf16[4,2,192,512]{3,2,1,0:T(8,128)(2,1)S(1)} async-done(((bf16[4,2,192,512]{3,2,1,0:T(8,128)(2,1)}), bf16[4,2,192,512]{3,2,1,0:T(8,128)(2,1)S(1)}, u32[]{:S(2)}, u32[]{:S(2)}) %all-to-all-start.2) | async-done | bytes 1572896 | tf_op jit(solution)/shard_map/all_to_all | solution.py:697
  298.1 1.1 copy-done.10
  299.3 38.9 %attend_backward.1 = (bf16[4,2,512,768]{3,2,1,0:T(8,128)(2,1)}, bf16[4,2,192,512]{3,2,1,0:T(8,128)(2,1)}, f32[576,768]{1,0:T(8,128)}, f32[1,576]{1,0:T(1,128)}) custom-call(s32[2]{0:T(128)} %len_ref.5, s32[1]{0:T(128)} %bitcast.1.fresh_ref, bf16[2,192,2048]{2,1,0:T(8,128)(2,1)} %get-tuple-element.36.q_ref, bf16[2,2048,192]{2,1,0:T(8,128)(2,1)} %get-tuple-element.37.k_ref, ...), custom_call_target="tpu_custom_call" | custom-call | flops 70000001024 | bytes 25000000 | tf_op jit(solution)/shard_map/attend_backward/pallas_call | solution.py:343
  338.2 20.7 %weight_grads.1 = (bf16[36,128,128]{2,1,0:T(8,128)(2,1)}, bf16[6,24,128,128]{3,2,1,0:T(8,128)(2,1)}, bf16[144,128,128]{2,1,0:T(8,128)(2,1)}) custom-call(bf16[4,2,192,512]{3,2,1,0:T(8,128)(2,1)} %copy-done.9, bf16[1024,768]{1,0:T(8,128)(2,1)} %get-tuple-element.44.bg_ref, bf16[1024,768]{1,0:T(8,128)(2,1)} %get-tuple-element.45.og_ref, ...), custom_call_target="tpu_custom_call" | custom-call | flops 12000000000 | bytes 40000000 | tf_op jit(solution)/shard_map/weight_grads/pallas_call | solution.py:585
  359.4 0.8 copy-done.7
  360.2 1.6 fusion.24
  361.7 2.8 reshape.247
  364.6 1.3 copy.53
  365.9 2.8 reshape.249
  368.7 1.3 copy.54
  370.0 1.8 reshape.251
  372.1 1.1 constant_dynamic-update-slice_fusion.5
  373.4 1.2 constant_dynamic-update-slice_fusion.4
  374.6 0.9 constant_dynamic-update-slice_fusion.3
  375.5 1.2 constant_dynamic-update-slice_fusion.2
  376.6 3.2 constant_dynamic-update-slice_fusion.1
  379.9 3.5 constant_dynamic-update-slice_fusion
  383.4 0.6 broadcast_dynamic-update-slice_fusion
  384.1 3.8 all-to-all-start.3
  387.9 1.2 copy.59
  389.6 27.2 %all-to-all-done.3 = bf16[4,2,192,512]{3,2,1,0:T(8,128)(2,1)S(1)} async-done(((bf16[4,2,192,512]{3,2,1,0:T(8,128)(2,1)}), bf16[4,2,192,512]{3,2,1,0:T(8,128)(2,1)S(1)}, u32[]{:S(2)}, u32[]{:S(2)}) %all-to-all-start.3) | async-done | bytes 1572896 | tf_op jit(solution)/shard_map/all_to_all | solution.py:710
  417.0 1.3 copy.52
  418.3 3.0 copy.60
  421.4 21.9 %reduce-scatter.3.cloned.1.call-done = bf16[1,2,512,768]{3,2,1,0:T(8,128)(2,1)} async-done(((bf16[4,2,512,768]{3,2,1,0:T(8,128)(2,1)}), bf16[1,2,512,768]{3,2,1,0:T(8,128)(2,1)}) %reduce-scatter.3.cloned.1.call-update) | async-done | bytes 1572880 | tf_op jit(solution)/shard_map/reduce_scatter | solution.py:706
  443.3 2.8 fusion.16
  446.2 166.3 %reduce-scatter.5.cloned.1.call-done = bf16[13,128,128]{2,1,0:T(8,128)(2,1)} async-done(((bf16[416,128,128]{2,1,0:T(8,128)(2,1)}), bf16[13,128,128]{2,1,0:T(8,128)(2,1)}) %reduce-scatter.5.cloned.1.call-update) | async-done | bytes 426000 | tf_op jit(solution)/shard_map/reduce_scatter | solution.py:750
  612.6 1.2 copy.56
  613.8 1.9 multiply_reduce_fusion
  615.7 4.1 fusion.12
  619.7 37.7 %all-reduce.1 = (f32[]{:T(128)}, f32[8832]{0:T(1024)S(1)}) all-reduce(f32[]{:T(128)} %multiply_reduce_fusion, f32[8832]{0:T(1024)S(1)} %constant_dynamic-update-slice_fusion.7), channel_id=1, replica_groups=mesh['dp'=8,'seq'=4] {'dp','seq'}, use_global_device_ids=true, to_apply=%region_7.0 | all-reduce | flops 8833 | bytes 70664 | tf_op jit(solution)/shard_map/psum | solution.py:775
  657.4 0.6 multiply_reduce_fusion.1
  659.4 0.7 divide_subtract_fusion
  660.0 1.2 broadcast_multiply_fusion
  661.2 1.5 fusion.27
  662.8 3.4 fusion.20
  666.1 1.2 copy.61
  667.3 2.4 fusion.17
  669.8 2.8 fusion.18
  (117 shorter events, 3.0 us)
Async XLA Ops:
  7.2 654.0 %copy-start = (f32[13,128,128]{2,1,0:T(8,128)S(1)}, f32[13,128,128]{2,1,0:T(8,128)}, u32[]{:S(2)}) copy-start(f32[13,128,128]{2,1,0:T(8,128)} %param.19) | copy-start | bytes 2555908
  7.2 4.0 copy-start.1
  7.2 4.6 copy-start.18
  7.2 110.1 %all-gather.4.cloned.1.call-start = ((), (), s32[]{:S(2)}) async-start(), calls=%async_computation.6 | async-start | bytes 14057472 | tf_op jit(solution)/shard_map/all_gather | solution.py:649
  9.4 154.6 %all-gather.6.cloned.1.call-start = ((), (), s32[]{:S(2)}) async-start(), calls=%async_computation.9 | async-start | bytes 7864320 | tf_op jit(solution)/shard_map/all_gather | solution.py:653
  11.2 2.5 copy-start.19
  11.2 2.5 copy-start.17
  11.8 2.2 copy-start.23
  11.9 2.1 copy-start.21
  15.3 114.9 %all-to-all-start = ((bf16[4,2,192,512]{3,2,1,0:T(8,128)(2,1)}), bf16[4,2,192,512]{3,2,1,0:T(8,128)(2,1)}, u32[]{:S(2)}, u32[]{:S(2)}) async-start(bf16[4,2,192,512]{3,2,1,0:T(8,128)(2,1)} %concatenate.15), calls=%async_computation | async-start | bytes 3145728 | tf_op jit(solution)/shard_map/all_to_all | solution.py:659
  123.8 3.3 slice-start.4
  198.4 23.6 %all-to-all-start.1 = ((bf16[4,2,192,512]{3,2,1,0:T(8,128)(2,1)}), bf16[4,2,192,512]{3,2,1,0:T(8,128)(2,1)S(1)}, u32[]{:S(2)}, u32[]{:S(2)}) async-start(bf16[4,2,192,512]{3,2,1,0:T(8,128)(2,1)} %get-tuple-element.33.o_ref), calls=%async_computation.1 | async-start | bytes 3145728 | tf_op jit(solution)/shard_map/all_to_all | solution.py:678
  222.0 1.2 copy-start.9
  274.3 3.8 copy-start.11
  274.3 3.8 copy-start.13
  274.3 3.8 copy-start.14
  274.4 23.8 %all-to-all-start.2 = ((bf16[4,2,192,512]{3,2,1,0:T(8,128)(2,1)}), bf16[4,2,192,512]{3,2,1,0:T(8,128)(2,1)S(1)}, u32[]{:S(2)}, u32[]{:S(2)}) async-start(bf16[4,2,192,512]{3,2,1,0:T(8,128)(2,1)} %get-tuple-element.39), calls=%async_computation.2 | async-start | bytes 3145728 | tf_op jit(solution)/shard_map/all_to_all | solution.py:697
  278.1 165.2 %reduce-scatter.3.cloned.1.call-start = ((), (), s32[]{:S(2)}) async-start(), calls=%async_computation.7 | async-start | bytes 7864320 | tf_op jit(solution)/shard_map/reduce_scatter | solution.py:706
  298.1 1.1 copy-start.10
  338.1 274.4 %reduce-scatter.5.cloned.1.call-start = ((), (), s32[]{:S(2)}) async-start(), calls=%async_computation.8 | async-start | bytes 14057472 | tf_op jit(solution)/shard_map/reduce_scatter | solution.py:750
  338.2 20.7 %copy-start.8 = (f32[576,768]{1,0:T(8,128)S(1)}, f32[576,768]{1,0:T(8,128)}, u32[]{:S(2)}) copy-start(f32[576,768]{1,0:T(8,128)} %get-tuple-element.43) | copy-start | bytes 5308420
  359.3 0.8 copy-start.7
  368.7 7.9 %slice-start.2 = ((s8[4718592]{0:T(1024)(128)(4,1)}), s8[524288]{0:T(1024)(128)(4,1)S(1)}, s32[]{:S(2)}) async-start(s8[4718592]{0:T(1024)(128)(4,1)} %bitcast.89), calls=%async_computation.12 | async-start | bytes 1048576
  370.0 2.0 copy-start.4
  371.9 1.5 copy-start.5
  372.0 3.4 copy-start.12
  372.0 4.6 slice-start.3
  376.6 3.2 slice-start
  376.6 3.3 slice-start.1
  384.0 3.8 copy-start.6
  384.0 5.0 copy-start.27
  384.1 5.1 copy-start.28
  384.1 32.7 %all-to-all-start.3 = ((bf16[4,2,192,512]{3,2,1,0:T(8,128)(2,1)}), bf16[4,2,192,512]{3,2,1,0:T(8,128)(2,1)S(1)}, u32[]{:S(2)}, u32[]{:S(2)}) async-start(bf16[4,2,192,512]{3,2,1,0:T(8,128)(2,1)} %get-tuple-element.42), calls=%async_computation.4 | async-start | bytes 3145728 | tf_op jit(solution)/shard_map/all_to_all | solution.py:710
  417.0 26.3 %copy-start.2 = (bf16[2,512,768]{2,1,0:T(8,128)(2,1)S(1)}, bf16[2,512,768]{2,1,0:T(8,128)(2,1)}, u32[]{:S(2)}) copy-start(bf16[2,512,768]{2,1,0:T(8,128)(2,1)} %tok_ref.1) | copy-start | bytes 4718596
  417.0 26.3 %copy-start.20 = (f32[2,512]{1,0:T(2,128)S(1)}, f32[2,512]{1,0:T(2,128)}, u32[]{:S(2)}) copy-start(f32[2,512]{1,0:T(2,128)} %copy-done.19) | copy-start | bytes 12292
  417.0 26.3 %copy-start.22 = (f32[768]{0:T(1024)S(1)}, f32[768]{0:T(1024)}, u32[]{:S(2)}) copy-start(f32[768]{0:T(1024)} %copy-done.21) | copy-start | bytes 9220
  417.0 26.3 %copy-start.24 = (f32[2,512]{1,0:T(2,128)S(1)}, f32[2,512]{1,0:T(2,128)}, u32[]{:S(2)}) copy-start(f32[2,512]{1,0:T(2,128)} %copy-done.23) | copy-start | bytes 12292
  418.3 27.8 %copy-start.26 = (f32[1,3072]{1,0:T(1,128)S(1)}, f32[1,3072]{1,0:T(1,128)}, u32[]{:S(2)}) copy-start(f32[1,3072]{1,0:T(1,128)} %get-tuple-element.54) | copy-start | bytes 36868
  615.7 43.7 %copy-start.25 = (f32[8832]{0:T(1024)S(1)}, f32[8832]{0:T(1024)}, u32[]{:S(2)}) copy-start(f32[8832]{0:T(1024)} %param.21) | copy-start | bytes 105988
  661.2 8.6 %copy-start.3 = (f32[13,128,128]{2,1,0:T(8,128)}, f32[13,128,128]{2,1,0:T(8,128)S(1)}, u32[]{:S(2)}) copy-start(f32[13,128,128]{2,1,0:T(8,128)S(1)} %broadcast_multiply_fusion) | copy-start | bytes 2555908
  662.8 4.6 copy-start.15
  667.3 2.4 copy-start.16
Sparse Core Ops, SparseCore 0:
  11.5 105.7 all-gather.3
  119.4 44.5 all-gather.5
  338.3 104.9 reduce-scatter.2
  445.6 166.9 reduce-scatter.4

commit v2 on v1

--- a/solution.py
+++ b/solution.py
@@ -19,6 +19,9 @@
 KEY_BLOCK = 512
 BACK_QUERY_BLOCK = 512
 BACK_KEY_BLOCK = 512
+HALF_BLOCK = 256
+SUB_ROWS = 256
+SUB_COLS = 256
 N_QKV = 90
 N_OUT = 36
 N_HID = 144
@@ -41,6 +44,7 @@
 NT = (((1,), (1,)), ((), ()))
 TN = (((0,), (0,)), ((), ()))
 VMEM_LIMIT = 60 << 20
+MESH = pl.DeviceIdType.MESH
 
 
 def dot(left_in, right_in, dims=NN):
@@ -82,14 +86,279 @@
     return pltpu.CompilerParams(dimension_semantics=("arbitrary",), vmem_limit_bytes=VMEM_LIMIT)
 
 
+W_SLOTS = 56
+W_SHARE = W_SLOTS // 4
+W_CHUNKS = ((0, 4), (4, 4), (8, 4), (12, 2))
+X_CHUNKS = 4
+
+
+def front_fits(dp, seq, owned):
+    return dp == 8 and seq == 4 and 8 * owned >= N_QKV
+
+
+def front_kernel(
+    tok_ref,
+    rows_ref,
+    master_ref,
+    x_ref,
+    w_ref,
+    normed,
+    staged,
+    slots,
+    x_send,
+    x_recv,
+    own_sem,
+    first_send,
+    first_recv,
+    w_send,
+    w_recv,
+):
+    dp, s = lax.axis_index("dp"), lax.axis_index("seq")
+    depth = lax.axis_size("dp") // 2
+    z, y, x, core = dp // 2, dp % 2, s // 2, s % 2
+    owned = master_ref.shape[0]
+    first = (dp * 4 + s) * owned
+    seqs, span, _ = tok_ref.shape
+    other_y, other_x, sibling = dp + 1 - 2 * y, s + 2 - 4 * x, s + 1 - 2 * core
+
+    barrier = pltpu.get_barrier_semaphore()
+    for dy in range(2):
+        for ds in range(4):
+            if dy or ds:
+                mate = (2 * z + (y + dy) % 2, (s + ds) % 4)
+                pl.semaphore_signal(barrier, inc=1, device_id=mate, device_id_type=MESH)
+
+    @pl.when(z > 0)
+    def _():
+        pl.semaphore_signal(barrier, inc=1, device_id=(dp - 2, s), device_id_type=MESH)
+
+    @pl.when(z < depth - 1)
+    def _():
+        pl.semaphore_signal(barrier, inc=1, device_id=(dp + 2, s), device_id_type=MESH)
+
+    at_end = (z == 0) | (z == depth - 1)
+
+    @pl.when(at_end)
+    def _():
+        pl.semaphore_wait(barrier, 8)
+
+    @pl.when(jnp.logical_not(at_end))
+    def _():
+        pl.semaphore_wait(barrier, 9)
+
+    def tile_sends(t, act):
+        index = first + t
+        is_value = index >= 2 * N_OUT
+        within = index % N_OUT
+        col = within % (D // TILE)
+        slot = jnp.where(
+            is_value,
+            index,
+            (index // N_OUT) * 18 + (within // (D // TILE)) * 3 + col % 3,
+        )
+        slot = jnp.where(is_value, index - N_OUT, slot)
+        share = slot // W_SHARE
+        chunk = (slot % W_SHARE) // 4
+        for copy_index in range(2):
+            to_x = jnp.where(is_value, copy_index, col // 3)
+            target = (share // 2, to_x * 2 + share % 2)
+            needed = (index < N_QKV) & (is_value | (copy_index == 0))
+            here = (target[0] == dp) & (target[1] == s)
+
+            @pl.when(needed & here)
+            def _():
+                if act == "start":
+                    pltpu.make_async_copy(
+                        staged.at[t], slots.at[slot], first_recv.at[chunk]
+                    ).start()
+
+            @pl.when(needed & jnp.logical_not(here))
+            def _():
+                copy = pltpu.make_async_remote_copy(
+                    src_ref=staged.at[t],
+                    dst_ref=slots.at[slot],
+                    send_sem=first_send.at[t, copy_index],
+                    recv_sem=first_recv.at[chunk],
+                    device_id=target,
+                    device_id_type=MESH,
+                )
+                if act == "start":
+                    copy.start()
+                else:
+                    copy.wait_send()
+
+    @pl.when(first < N_QKV)
+    def _():
+        for t in range(owned):
+            staged[t] = master_ref[t].astype(bf16).T
+        for t in range(owned):
+            tile_sends(t, "start")
+
+    rows_each = seqs * span // X_CHUNKS
+    per_seq = span // rows_each
+
+    def x_copy(kind, j):
+        n, part = j // per_seq, j % per_seq
+        at = pl.ds(part * rows_each, rows_each)
+        block = other_x if kind == 2 else s
+        return pltpu.make_async_remote_copy(
+            src_ref=x_ref.at[block, n, at] if kind == 2 else normed.at[n, at],
+            dst_ref=x_ref.at[block, n, at],
+            send_sem=x_send.at[kind, j],
+            recv_sem=x_recv.at[kind, j],
+            device_id=(dp, other_x) if kind == 0 else (dp, sibling),
+            device_id_type=MESH,
+        )
+
+    def own_copy(j):
+        n, part = j // per_seq, j % per_seq
+        at = pl.ds(part * rows_each, rows_each)
+        return pltpu.make_async_copy(normed.at[n, at], x_ref.at[s, n, at], own_sem.at[j])
+
+    for j in range(X_CHUNKS):
+        n, part = j // per_seq, j % per_seq
+        at = pl.ds(part * rows_each, rows_each)
+        value = tok_ref[n, at, :].astype(f32)
+        normed[n, at, :] = norm_forward(value, rows_ref[0:1, :], rows_ref[1:2, :])[0].astype(bf16)
+        x_copy(0, j).start()
+        x_copy(1, j).start()
+        own_copy(j).start()
+
+    share = y * 2 + core
+
+    def w_copy(kind, j):
+        low, size = W_CHUNKS[j]
+        base = ((1 - y) * 2 + core) * W_SHARE if kind == 3 else share * W_SHARE
+        at = pl.ds(base + low, size)
+        device = ((dp + 2, s), (other_y, s), (dp, sibling), (dp, sibling))[kind]
+        return pltpu.make_async_remote_copy(
+            src_ref=slots.at[at],
+            dst_ref=slots.at[at],
+            send_sem=w_send.at[kind, j],
+            recv_sem=w_recv.at[kind, j],
+            device_id=device,
+            device_id_type=MESH,
+        )
+
+    def landed(j, size):
+        low, _ = W_CHUNKS[j]
+        at = pl.ds(share * W_SHARE + low, size)
+        pltpu.make_async_copy(slots.at[at], slots.at[at], first_recv.at[j]).wait()
+
+    used = 3 * 18 - 3 * W_SHARE
+    @pl.when((z == 0) & (share == 3))
+    def _():
+        slots[3 * W_SHARE + used : W_SLOTS] = jnp.zeros(
+            (W_SHARE - used,) + slots.shape[1:], bf16
+        )
+
+    for j in range(max(len(W_CHUNKS), X_CHUNKS)):
+        if j < len(W_CHUNKS):
+            low, size = W_CHUNKS[j]
+            short = min(size, used - low)
+
+            @pl.when((z == 0) & (share < 3))
+            def _():
+                landed(j, size)
+
+            if short > 0:
+
+                @pl.when((z == 0) & (share == 3))
+                def _():
+                    landed(j, short)
+
+            @pl.when(z > 0)
+            def _():
+                w_copy(0, j).wait_recv()
+
+            @pl.when(z < depth - 1)
+            def _():
+                w_copy(0, j).start()
+
+            w_copy(1, j).start()
+            w_copy(2, j).start()
+        if j < X_CHUNKS:
+            x_copy(0, j).wait_recv()
+            x_copy(2, j).start()
+        if j < len(W_CHUNKS):
+            w_copy(1, j).wait_recv()
+            w_copy(3, j).start()
+    for j in range(len(W_CHUNKS)):
+        w_copy(2, j).wait_recv()
+        w_copy(3, j).wait_recv()
+    width = HD * 3
+    for which in range(3):
+        for piece in range(3):
+            unit = core * 3 + piece
+            rows = pl.ds(pl.multiple_of((unit % 2) * HD, HD), HD)
+            at = which * width + piece * HD
+            for r in range(D // TILE):
+                w_ref[at : at + HD, r * TILE : (r + 1) * TILE] = slots[
+                    which * 18 + r * 3 + unit // 2, rows, :
+                ]
+    for j in range(X_CHUNKS):
+        x_copy(1, j).wait_recv()
+        x_copy(2, j).wait_recv()
+        own_copy(j).wait()
+        for kind in range(3):
+            x_copy(kind, j).wait_send()
+    for j in range(len(W_CHUNKS)):
+
+        @pl.when(z < depth - 1)
+        def _():
+            w_copy(0, j).wait_send()
+
+        for kind in range(1, 4):
+            w_copy(kind, j).wait_send()
+
+    @pl.when(first < N_QKV)
+    def _():
+        for t in range(owned):
+            tile_sends(t, "wait")
+
+
+def front(tokens, rows, master):
+    seqs, span, _ = tokens.shape
+    owned = master.shape[0]
+    vm = pl.BlockSpec(memory_space=pltpu.VMEM)
+    dma = pltpu.SemaphoreType.DMA
+    chunks = len(W_CHUNKS)
+    return pl.pallas_call(
+        front_kernel,
+        in_specs=[vm] * 3,
+        out_specs=[pl.BlockSpec(memory_space=pl.ANY), vm],
+        out_shape=[
+            jax.ShapeDtypeStruct((4, seqs, span, D), bf16),
+            jax.ShapeDtypeStruct((9 * HD, D), bf16),
+        ],
+        scratch_shapes=[
+            pltpu.VMEM((seqs, span, D), bf16),
+            pltpu.VMEM((owned, TILE, TILE), bf16),
+            pltpu.VMEM((W_SLOTS, TILE, TILE), bf16),
+            dma((3, X_CHUNKS)),
+            dma((3, X_CHUNKS)),
+            dma((X_CHUNKS,)),
+            dma((owned, 2)),
+            dma((chunks,)),
+            dma((4, chunks)),
+            dma((4, chunks)),
+        ],
+        compiler_params=pltpu.CompilerParams(
+            collective_id=3, has_side_effects=True, vmem_limit_bytes=VMEM_LIMIT
+        ),
+        cost_estimate=pl.CostEstimate(
+            flops=40_000_000_000, bytes_accessed=20_000_000, transcendentals=0
+        ),
+        name="front",
+    )(tokens, rows, master)
+
+
 def attend_forward_kernel(
     heads,
     len_ref,
     fresh_ref,
     x_ref,
-    wq_ref,
-    wk_ref,
-    wv_ref,
+    w_ref,
     qb_ref,
     vb_ref,
     fv_ref,
@@ -99,80 +368,94 @@
     v_ref,
     lse_ref,
     k_heads,
+    q_wide,
     values,
     acc,
     top,
-    total,
 ):
     blocks, _, span, width_in = x_ref.shape
     count = blocks * span
     length = len_ref[pl.program_id(0)]
     x = x_ref[...].reshape(count, width_in)
-    q_ref[0] = (dot(wq_ref[...], x, NT) + qb_ref[...]).astype(bf16)
-    keys = dot(x, wk_ref[...], NT).astype(bf16)
-    k_ref[0] = keys
+    width = heads * HD
+    q_ref[0] = (dot(w_ref[0:width, :], x, NT) + qb_ref[...]).astype(bf16)
+    keys = dot(x, w_ref[width : 2 * width, :], NT).astype(bf16)
+    k_ref[0] = keys.T
+    dead = lax.broadcasted_iota(jnp.int32, (count, 1), 0) >= length
+    bias = jnp.broadcast_to(jnp.where(dead, masked_score, 0.0).astype(bf16), (count, 16))
+    ones = (lax.broadcasted_iota(jnp.int32, (16, count), 0) == 0).astype(f32).astype(bf16)
     for h in range(heads):
-        k_heads[h] = keys[:, h * HD : (h + 1) * HD]
+        k_heads[h, :, 0:HD] = keys[:, h * HD : (h + 1) * HD]
+        k_heads[h, :, HD : HD + 16] = bias
+        q_wide[h, 0:HD] = q_ref[0, h * HD : (h + 1) * HD, :]
+        q_wide[h, HD : HD + 16] = ones
 
     @pl.when(fresh_ref[0] == 1)
     def _():
-        values[...] = (dot(wv_ref[...], x, NT) + vb_ref[...]).astype(bf16)
+        v_ref[0] = (dot(w_ref[2 * width :, :], x, NT) + vb_ref[...]).astype(bf16)
 
     @pl.when(fresh_ref[0] == 0)
     def _():
         for b in range(blocks):
-            values[:, b * span : (b + 1) * span] = fv_ref[b, 0]
-
-    v_ref[0] = values[...].T
+            v_ref[0, :, b * span : (b + 1) * span] = fv_ref[b, 0]
+
+    for h in range(heads):
+        values[h, 0:HD] = v_ref[0, h * HD : (h + 1) * HD, :]
+        values[h, HD : HD + 16] = ones
     bq, bk = QUERY_BLOCK, KEY_BLOCK
 
     def one_query_block(qi, carry):
         q0 = pl.multiple_of(qi * bq, bq)
         top[...] = jnp.full_like(top, masked_score)
-        total[...] = jnp.zeros_like(total)
         acc[...] = jnp.zeros_like(acc)
 
-        def step(ki, masked):
-            k0 = pl.multiple_of(ki * bk, bk)
+        def step(ki, masked, low=0, rows_here=bk):
+            k0 = pl.multiple_of(ki * bk + low, HALF_BLOCK)
+            skip = low if masked else 0
+            cols = slice(skip, bq)
             if masked:
-                key_pos = k0 + lax.broadcasted_iota(jnp.int32, (bk, bq), 0)
-                query_pos = q0 + lax.broadcasted_iota(jnp.int32, (bk, bq), 1)
+                shape = (rows_here, bq - skip)
+                key_pos = k0 + lax.broadcasted_iota(jnp.int32, shape, 0)
+                query_pos = q0 + skip + lax.broadcasted_iota(jnp.int32, shape, 1)
                 allowed = (key_pos <= query_pos) & (key_pos < length)
             for h in range(heads):
                 rows = slice(h * HD, (h + 1) * HD)
-                s = dot(k_heads[h, pl.ds(k0, bk), :], q_ref[0, rows, pl.ds(q0, bq)])
+                at = pl.ds(pl.multiple_of(q0 + skip, HALF_BLOCK), bq - skip)
+                s = dot(k_heads[h, pl.ds(k0, rows_here), :], q_wide[h, :, at])
                 s = s * (SCALE * LOG2E)
                 if masked:
                     s = jnp.where(allowed, s, masked_score)
-                top_old = top[h : h + 1, :]
+                top_old = top[h : h + 1, cols]
                 top_new = jnp.maximum(top_old, jnp.max(s, axis=0, keepdims=True))
                 p = jnp.exp2(s - top_new)
                 fade = jnp.exp2(top_old - top_new)
-                top[h : h + 1, :] = top_new
-                total[h : h + 1, :] = total[h : h + 1, :] * fade + jnp.sum(
-                    p, axis=0, keepdims=True
+                top[h : h + 1, cols] = top_new
+                acc[h, :, cols] = acc[h, :, cols] * fade + dot(
+                    values[h, :, pl.ds(k0, rows_here)], p.astype(bf16)
                 )
-                acc[rows, :] = acc[rows, :] * fade + dot(
-                    values[rows, pl.ds(k0, bk)], p.astype(bf16)
-                )
-
-        plain = jnp.minimum(q0, length) // bk
-        end = (jnp.minimum(q0 + bq, length) + bk - 1) // bk
-        lax.fori_loop(0, plain, lambda i, c: (step(i, False), c)[1], 0)
-        lax.fori_loop(plain, end, lambda i, c: (step(i, True), c)[1], 0)
+
+        lax.fori_loop(
+            0, jnp.minimum(qi, (length + bk - 1) // bk), lambda i, c: (step(i, False), c)[1], 0
+        )
+
+        @pl.when(q0 < length)
+        def _():
+            step(qi, True, 0, HALF_BLOCK)
+            step(qi, True, HALF_BLOCK, HALF_BLOCK)
+
         for h in range(heads):
             rows = slice(h * HD, (h + 1) * HD)
-            sums = total[h : h + 1, :]
-            o_ref[qi, 0, rows, :] = (acc[rows, :] / sums).astype(bf16)
+            sums = acc[h, HD : HD + 1, :]
+            o_ref[qi, 0, rows, :] = (acc[h, 0:HD, :] / sums).astype(bf16)
             lse_ref[0, h : h + 1, pl.ds(q0, bq)] = top[h : h + 1, :] + jnp.log2(sums)
         return carry
 
     lax.fori_loop(0, count // bq, one_query_block, 0)
 
 
-def attend_forward(lengths, fresh, x, wq, wk, wv, qb, vb, fv):
+def attend_forward(lengths, fresh, x, w, qb, vb, fv):
     blocks, seqs, span, _ = x.shape
-    width = wq.shape[0]
+    width = w.shape[0] // 3
     heads = width // HD
     count = blocks * span
     one = lambda shape: pl.BlockSpec((1,) + shape, lambda i, *_: (i,) + (0,) * len(shape))
@@ -183,29 +466,29 @@
             num_scalar_prefetch=2,
             grid=(seqs,),
             in_specs=[mid((span, D))]
-            + [whole((width, D))] * 3
+            + [whole((3 * width, D))]
             + [whole((width, 1))] * 2
             + [mid((width, span))],
             out_specs=[
                 mid((width, span)),
                 one((width, count)),
-                one((count, width)),
-                one((count, width)),
+                one((width, count)),
+                one((width, count)),
                 one((8, count)),
             ],
             scratch_shapes=[
-                pltpu.VMEM((heads, count, HD), bf16),
-                pltpu.VMEM((width, count), bf16),
-                pltpu.VMEM((width, QUERY_BLOCK), f32),
-                pltpu.VMEM((8, QUERY_BLOCK), f32),
+                pltpu.VMEM((heads, count, HD + 16), bf16),
+                pltpu.VMEM((heads, HD + 16, count), bf16),
+                pltpu.VMEM((heads, HD + 16, count), bf16),
+                pltpu.VMEM((heads, HD + 16, QUERY_BLOCK), f32),
                 pltpu.VMEM((8, QUERY_BLOCK), f32),
             ],
         ),
         out_shape=[
             jax.ShapeDtypeStruct((blocks, seqs, width, span), bf16),
             jax.ShapeDtypeStruct((seqs, width, count), bf16),
-            jax.ShapeDtypeStruct((seqs, count, width), bf16),
-            jax.ShapeDtypeStruct((seqs, count, width), bf16),
+            jax.ShapeDtypeStruct((seqs, width, count), bf16),
+            jax.ShapeDtypeStruct((seqs, width, count), bf16),
             jax.ShapeDtypeStruct((seqs, 8, count), f32),
         ],
         compiler_params=params(),
@@ -213,13 +496,14 @@
             flops=40_000_000_000, bytes_accessed=20_000_000, transcendentals=0
         ),
         name="attend_forward",
-    )(lengths, fresh, x, wq, wk, wv, qb, vb, fv)
+    )(lengths, fresh, x, w, qb, vb, fv)
 
 
 def attend_backward_kernel(
     heads,
     len_ref,
     fresh_ref,
+    group_ref,
     q_ref,
     k_ref,
     v_ref,
@@ -228,10 +512,14 @@
     lse_ref,
     x_ref,
     w_ref,
+    all_in_ref,
     dx_ref,
     dv_ref,
+    all_ref,
+    db_ref,
     dw_ref,
-    db_ref,
+    tiles,
+    sem,
     k_heads,
     v_heads,
     q_heads,
@@ -253,8 +541,8 @@
     delta[...] = jnp.zeros_like(delta)
     for h in range(heads):
         rows = slice(h * HD, (h + 1) * HD)
-        k_heads[h] = k_ref[0, :, rows]
-        v_heads[h] = v_ref[0, :, rows]
+        k_heads[h] = k_ref[0, rows, :].T
+        v_heads[h] = v_ref[0, rows, :].T
         q_heads[h] = q_ref[0, rows, :].T
     for b in range(blocks):
         at = slice(b * span, (b + 1) * span)
@@ -265,7 +553,7 @@
             rows = slice(h * HD, (h + 1) * HD)
             g_heads[h, at, :] = g_block[rows, :].T
             delta[h : h + 1, at] = jnp.sum(product[rows, :], axis=0, keepdims=True)
-    k_turned[...] = k_ref[0].T
+    k_turned[...] = k_ref[0]
     dq_acc[...] = jnp.zeros_like(dq_acc)
     grads[...] = jnp.zeros_like(grads)
     key_blocks = (length + bk - 1) // bk
@@ -332,8 +620,33 @@
         dw_ref[...] += dw
         db_ref[...] += db
 
-
-def attend_backward(lengths, fresh, q, k, v, o, g, lse, x, w):
+    @pl.when(n == pl.num_programs(0) - 1)
+    def _():
+        tiles[...] = jnp.zeros_like(tiles)
+        for which, (start, per_row) in enumerate(
+            ((0, D // TILE), (N_OUT, D // TILE), (2 * N_OUT, VW // TILE))
+        ):
+
+            def put(group):
+                for piece in range(heads):
+                    unit = group * heads + piece
+                    rows = pl.ds(pl.multiple_of((unit % 2) * HD, HD), HD)
+                    at = which * width + piece * HD
+                    for r in range(D // TILE):
+                        tiles[start + r * per_row + unit // 2, rows, :] = dw_ref[
+                            at : at + HD, r * TILE : (r + 1) * TILE
+                        ].astype(bf16)
+
+            if which < 2:
+                put(group_ref[0])
+            else:
+                pl.when(fresh_ref[0] == 1)(lambda: put(group_ref[0]))
+        copy = pltpu.make_async_copy(tiles, all_ref.at[pl.ds(0, N_QKV)], sem.at[0])
+        copy.start()
+        copy.wait()
+
+
+def attend_backward(lengths, fresh, group, q, k, v, o, g, lse, x, w, all_tiles):
     blocks, seqs, span, _ = x.shape
     width = q.shape[1]
     heads = width // HD
@@ -343,25 +656,31 @@
     return pl.pallas_call(
         functools.partial(attend_backward_kernel, heads),
         grid_spec=pltpu.PrefetchScalarGridSpec(
-            num_scalar_prefetch=2,
+            num_scalar_prefetch=3,
             grid=(seqs,),
             in_specs=[
                 one((width, count)),
-                one((count, width)),
-                one((count, width)),
+                one((width, count)),
+                one((width, count)),
                 mid((width, span)),
                 mid((width, span)),
                 one((8, count)),
                 mid((span, D)),
                 whole((3 * width, D)),
+                pl.BlockSpec(memory_space=pl.ANY),
             ],
             out_specs=[
                 mid((span, D)),
                 mid((width, span)),
-                whole((3 * width, D)),
+                pl.BlockSpec(memory_space=pl.ANY),
                 whole((1, 3 * width)),
             ],
-            scratch_shapes=[pltpu.VMEM((heads, count, HD), bf16)] * 4
+            scratch_shapes=[
+                pltpu.VMEM((3 * width, D), f32),
+                pltpu.VMEM((N_QKV, TILE, TILE), bf16),
+                pltpu.SemaphoreType.DMA((1,)),
+            ]
+            + [pltpu.VMEM((heads, count, HD), bf16)] * 4
             + [
                 pltpu.VMEM((width, count), bf16),
                 pltpu.VMEM((width, count), bf16),
@@ -375,15 +694,16 @@
         out_shape=[
             jax.ShapeDtypeStruct((blocks, seqs, span, D), bf16),
             jax.ShapeDtypeStruct((blocks, seqs, width, span), bf16),
-            jax.ShapeDtypeStruct((3 * width, D), f32),
+            jax.ShapeDtypeStruct(all_tiles.shape, bf16),
             jax.ShapeDtypeStruct((1, 3 * width), f32),
         ],
+        input_output_aliases={11: 2},
         compiler_params=params(),
         cost_estimate=pl.CostEstimate(
             flops=70_000_000_000, bytes_accessed=25_000_000, transcendentals=0
         ),
         name="attend_backward",
-    )(lengths, fresh, q, k, v, o, g, lse, x, w)
+    )(lengths, fresh, group, q, k, v, o, g, lse, x, w, all_tiles)
 
 
 HIDDEN_CHUNK = 512
@@ -414,6 +734,8 @@
     w_out,
     w_hidden,
     w_proj,
+    output_acc,
+    norm_acc,
     sem,
 ):
     n = pl.program_id(0)
@@ -437,11 +759,14 @@
         ):
             copy.wait()
             row_tiles, col_tiles = matrix.shape[0] // TILE, matrix.shape[1] // TILE
-            for r in range(row_tiles):
+
+            def place(r, carry):
+                at = pl.ds(pl.multiple_of(r * TILE, TILE), TILE)
                 for c in range(col_tiles):
-                    matrix[r * TILE : (r + 1) * TILE, c * TILE : (c + 1) * TILE] = tiles[
-                        start + r * col_tiles + c
-                    ]
+                    matrix[at, c * TILE : (c + 1) * TILE] = tiles[start + r * col_tiles + c]
+                return carry
+
+            lax.fori_loop(0, row_tiles, place, 0)
         sums_ref[...] = jnp.zeros_like(sums_ref)
         hsum_ref[...] = jnp.zeros_like(hsum_ref)
 
@@ -456,11 +781,12 @@
     out_grad = jnp.where(live, cot_ref[0].astype(f32), 0.0)
     out_grad_low = out_grad.astype(bf16)
     og_ref[...] = out_grad_low
-    output = residual + proj_bias
-    norm_in = jnp.zeros((span, D), f32)
-    for c in range(FF // HIDDEN_CHUNK):
-        cols = slice(c * HIDDEN_CHUNK, (c + 1) * HIDDEN_CHUNK)
-        hidden = dot(normed, w_hidden[:, cols]) + hb_ref[:, cols]
+    output_acc[...] = residual + proj_bias
+    norm_acc[...] = jnp.zeros_like(norm_acc)
+
+    def chunk(c, carry):
+        cols = pl.ds(pl.multiple_of(c * HIDDEN_CHUNK, HIDDEN_CHUNK), HIDDEN_CHUNK)
+        hidden = dot(nt_ref[...], w_hidden[:, cols]) + hb_ref[:, cols]
         square = hidden * hidden
         bend = jnp.tanh(GELU_A * (hidden + GELU_B * (hidden * square)))
         active = (0.5 * hidden * (1.0 + bend)).astype(bf16)
@@ -468,12 +794,16 @@
             GELU_A * (1.0 + (3.0 * GELU_B) * square)
         )
         act_ref[:, cols] = active
-        hidden_grad = (dot(out_grad_low, w_proj[cols, :], NT) * slope).astype(bf16)
+        hidden_grad = (dot(og_ref[...], w_proj[cols, :], NT) * slope).astype(bf16)
         hg_ref[:, cols] = hidden_grad
         hsum_ref[:, cols] += jnp.sum(hidden_grad.astype(f32), axis=0, keepdims=True)
-        output = output + dot(active, w_proj[cols, :])
-        norm_in = norm_in + dot(hidden_grad, w_hidden[:, cols], NT)
-    out_ref[0] = output.astype(bf16)
+        output_acc[...] += dot(active, w_proj[cols, :])
+        norm_acc[...] += dot(hidden_grad, w_hidden[:, cols], NT)
+        return carry
+
+    lax.fori_loop(0, FF // HIDDEN_CHUNK, chunk, 0)
+    out_ref[0] = output_acc[...].astype(bf16)
+    norm_in = norm_acc[...]
     residual_grad = out_grad + norm_backward(norm_in, unit, inv, gain_two)
     rg_ref[0] = residual_grad
     branch = residual_grad.astype(bf16)
@@ -521,6 +851,8 @@
                 pltpu.VMEM((D, D), bf16),
                 pltpu.VMEM((D, FF), bf16),
                 pltpu.VMEM((FF, D), bf16),
+                pltpu.VMEM((span, D), f32),
+                pltpu.VMEM((span, D), f32),
                 pltpu.SemaphoreType.DMA((3,)),
             ],
         ),
@@ -548,10 +880,61 @@
 
 
 def weight_grad_kernel(
-    att_ref, bg_ref, og_ref, nt_ref, act_ref, hg_ref, out_ref, hid_ref, proj_ref, og_turned, nt_turned
+    att_ref,
+    bg_ref,
+    og_ref,
+    nt_ref,
+    act_ref,
+    hg_ref,
+    all_ref,
+    out_tiles,
+    hid_tiles,
+    proj_tiles,
+    og_turned,
+    nt_turned,
+    sem,
+    out_sem,
 ):
     i = pl.program_id(0)
+    last = pl.num_programs(0) - 1
     groups, seqs, width, span = att_ref.shape
+    d_tiles, f_tiles, per = D // TILE, FF // TILE, GRAD_CHUNK // TILE
+    spare = all_ref.shape[0] - N_QKV - N_REST
+    slot = lax.rem(i, 2)
+
+    def first_copies():
+        copies = [
+            pltpu.make_async_copy(
+                out_tiles.at[pl.ds(0, N_OUT)], all_ref.at[pl.ds(N_QKV, N_OUT)], out_sem.at[0]
+            )
+        ]
+        if spare:
+            copies.append(
+                pltpu.make_async_copy(
+                    out_tiles.at[pl.ds(N_OUT, spare)],
+                    all_ref.at[pl.ds(N_QKV + N_REST, spare)],
+                    out_sem.at[1],
+                )
+            )
+        return copies
+
+    def copies_of(step, slot):
+        made = [
+            pltpu.make_async_copy(
+                hid_tiles.at[slot, r],
+                all_ref.at[pl.ds(N_QKV + N_OUT + r * f_tiles + step * per, per)],
+                sem.at[slot, r],
+            )
+            for r in range(d_tiles)
+        ]
+        made.append(
+            pltpu.make_async_copy(
+                proj_tiles.at[slot],
+                all_ref.at[pl.ds(FIRST_PROJ + step * per * d_tiles, per * d_tiles)],
+                sem.at[slot, d_tiles],
+            )
+        )
+        return made
 
     @pl.when(i == 0)
     def _():
@@ -563,25 +946,47 @@
                 att_ref[:, s].reshape(groups * width, span), bg_ref[s * span : (s + 1) * span, :]
             )
         total = total.astype(bf16)
-        for r in range(D // TILE):
-            for c in range(D // TILE):
-                out_ref[r * (D // TILE) + c] = total[
+        for r in range(d_tiles):
+            for c in range(d_tiles):
+                out_tiles[r * d_tiles + c] = total[
                     r * TILE : (r + 1) * TILE, c * TILE : (c + 1) * TILE
                 ]
+        if spare:
+            out_tiles[N_OUT : N_OUT + spare] = jnp.zeros((spare, TILE, TILE), bf16)
+        for copy in first_copies():
+            copy.start()
 
     proj = dot(og_turned[...], act_ref[...]).astype(bf16)
     hid = dot(nt_turned[...], hg_ref[...]).astype(bf16)
-    for c in range(GRAD_CHUNK // TILE):
-        for r in range(D // TILE):
+
+    @pl.when(i >= 2)
+    def _():
+        for copy in copies_of(i - 2, slot):
+            copy.wait()
+
+    for c in range(per):
+        for r in range(d_tiles):
             rows, cols = slice(r * TILE, (r + 1) * TILE), slice(c * TILE, (c + 1) * TILE)
-            proj_ref[c * (D // TILE) + r] = proj[rows, cols]
-            hid_ref[r, c] = hid[rows, cols]
-
-
-def weight_grads(att, bg, og, nt, act, hg):
+            proj_tiles[slot, c * d_tiles + r] = proj[rows, cols]
+            hid_tiles[slot, r, c] = hid[rows, cols]
+    for copy in copies_of(i, slot):
+        copy.start()
+
+    @pl.when(i == last)
+    def _():
+        for copy in copies_of(i - 1, 1 - slot):
+            copy.wait()
+        for copy in copies_of(i, slot):
+            copy.wait()
+        for copy in first_copies():
+            copy.wait()
+
+
+def weight_grads(total_tiles, att, bg, og, nt, act, hg):
     total = bg.shape[0]
     chunks = FF // GRAD_CHUNK
     per = GRAD_CHUNK // TILE
+    spare = total_tiles - N_QKV - N_REST
     return pl.pallas_call(
         weight_grad_kernel,
         grid=(chunks,),
@@ -593,23 +998,1095 @@
             pl.BlockSpec((total, GRAD_CHUNK), lambda i: (0, i)),
             pl.BlockSpec((total, GRAD_CHUNK), lambda i: (0, i)),
         ],
-        out_specs=[
-            whole((N_OUT, TILE, TILE)),
-            pl.BlockSpec((D // TILE, per, TILE, TILE), lambda i: (0, i, 0, 0)),
-            pl.BlockSpec((per * (D // TILE), TILE, TILE), lambda i: (i, 0, 0)),
+        out_specs=pl.BlockSpec(memory_space=pl.ANY),
+        out_shape=jax.ShapeDtypeStruct((total_tiles, TILE, TILE), bf16),
+        scratch_shapes=[
+            pltpu.VMEM((N_OUT + spare, TILE, TILE), bf16),
+            pltpu.VMEM((2, D // TILE, per, TILE, TILE), bf16),
+            pltpu.VMEM((2, per * (D // TILE), TILE, TILE), bf16),
+            pltpu.VMEM((D, total), bf16),
+            pltpu.VMEM((D, total), bf16),
+            pltpu.SemaphoreType.DMA((2, D // TILE + 1)),
+            pltpu.SemaphoreType.DMA((2,)),
         ],
-        out_shape=[
-            jax.ShapeDtypeStruct((N_OUT, TILE, TILE), bf16),
-            jax.ShapeDtypeStruct((D // TILE, FF // TILE, TILE, TILE), bf16),
-            jax.ShapeDtypeStruct((N_PROJ, TILE, TILE), bf16),
-        ],
-        scratch_shapes=[pltpu.VMEM((D, total), bf16), pltpu.VMEM((D, total), bf16)],
         compiler_params=params(),
         cost_estimate=pl.CostEstimate(
             flops=12_000_000_000, bytes_accessed=40_000_000, transcendentals=0
         ),
         name="weight_grads",
     )(att, bg, og, nt, act, hg)
+
+
+def bits_of(size):
+    return size.bit_length() - 1
+
+
+def exchange_bits(dp, seq):
+    return (
+        [("seq", 0)]
+        + [("dp", b) for b in range(bits_of(dp))]
+        + [("seq", b) for b in range(1, bits_of(seq))]
+    )
+
+
+def partner_of(axis, bit):
+    here = {"dp": lax.axis_index("dp"), "seq": lax.axis_index("seq")}
+    side = (here[axis] // (1 << bit)) % 2
+    here[axis] = here[axis] + (1 << bit) * (1 - 2 * side)
+    return (here["dp"], here["seq"]), side
+
+
+def greet(partners):
+    barrier = pltpu.get_barrier_semaphore()
+    for device in partners:
+        pl.semaphore_signal(barrier, inc=1, device_id=device, device_id_type=MESH)
+    pl.semaphore_wait(barrier, len(partners))
+
+
+def tile_sum_kernel(stages, chunks, g_ref, out_ref, mine, *rest):
+    count = len(stages)
+    received = rest[:count]
+    send_sem, recv_sem, copy_sem = rest[count:]
+    partners = [partner_of(axis, bit) for axis, bit, _, _ in stages]
+    greet([device for device, _ in partners])
+
+    def view(ref, above, below):
+        return ref.reshape(above, 2, below, *ref.shape[-3:])
+
+    def send(stage, k):
+        _, _, above, below = stages[stage]
+        device, side = partners[stage]
+        source = g_ref if stage == 0 else received[stage - 1]
+        at = pl.ds(*chunks[k])
+        return pltpu.make_async_remote_copy(
+            src_ref=view(source, above, below).at[:, 1 - side, :, at],
+            dst_ref=received[stage].reshape(above, below, *received[stage].shape[-3:]).at[:, :, at],
+            send_sem=send_sem.at[stage, k],
+            recv_sem=recv_sem.at[stage, k],
+            device_id=device,
+            device_id_type=MESH,
+        )
+
+    def own(k):
+        _, _, above, below = stages[0]
+        at = pl.ds(*chunks[k])
+        return pltpu.make_async_copy(
+            view(g_ref, above, below).at[:, partners[0][1], :, at],
+            mine.reshape(above, below, *mine.shape[-3:]).at[:, :, at],
+            copy_sem.at[k],
+        )
+
+    for k in range(len(chunks)):
+        send(0, k).start()
+        own(k).start()
+    for step in range(1, len(chunks) + count):
+        for k in range(len(chunks)):
+            stage = step - k
+            if not 1 <= stage <= count:
+                continue
+            send(stage - 1, k).wait_recv()
+            _, _, above, below = stages[stage - 1]
+            side = partners[stage - 1][1]
+            at = pl.ds(*chunks[k])
+            if stage == 1:
+                own(k).wait()
+
+            def add(i, carry):
+                if stage == 1:
+                    kept = mine[i, at]
+                else:
+                    up, low = i // below, i % below
+                    kept = received[stage - 2][(up * 2 + side) * below + low, at]
+                total = kept.astype(f32) + received[stage - 1][i, at].astype(f32)
+                if stage == count:
+                    out_ref[at] = total
+                else:
+                    received[stage - 1][i, at] = total.astype(bf16)
+                return carry
+
+            lax.fori_loop(0, above * below, add, 0)
+            if stage < count:
+                send(stage, k).start()
+    for stage in range(count):
+        for k in range(len(chunks)):
+            send(stage, k).wait_send()
+
+
+def tile_sum(g, dp, seq):
+    devices = dp * seq
+    owned = g.shape[0] // devices
+    tail = (owned, TILE, TILE)
+    left = [("dp", b) for b in reversed(range(bits_of(dp)))] + [
+        ("seq", b) for b in reversed(range(bits_of(seq)))
+    ]
+    stages = []
+    for axis, bit in exchange_bits(dp, seq):
+        place = left.index((axis, bit))
+        stages.append((axis, bit, 1 << place, 1 << (len(left) - 1 - place)))
+        left.pop(place)
+    pieces = min(4, owned)
+    edges = [owned * p // pieces for p in range(pieces + 1)]
+    chunks = [(low, high - low) for low, high in zip(edges, edges[1:])]
+    buffers = [
+        pltpu.VMEM((devices >> (i + 1),) + tail, bf16) for i in range(len(stages))
+    ]
+    return pl.pallas_call(
+        functools.partial(tile_sum_kernel, stages, chunks),
+        in_specs=[pl.BlockSpec(memory_space=pl.ANY)],
+        out_specs=pl.BlockSpec(memory_space=pltpu.VMEM),
+        out_shape=jax.ShapeDtypeStruct(tail, f32),
+        scratch_shapes=[pltpu.VMEM((devices // 2,) + tail, bf16)]
+        + buffers
+        + [
+            pltpu.SemaphoreType.DMA((len(stages), len(chunks))),
+            pltpu.SemaphoreType.DMA((len(stages), len(chunks))),
+            pltpu.SemaphoreType.DMA((len(chunks),)),
+        ],
+        compiler_params=pltpu.CompilerParams(
+            collective_id=1, has_side_effects=True, vmem_limit_bytes=VMEM_LIMIT
+        ),
+        cost_estimate=pl.CostEstimate(
+            flops=60_000_000_000, bytes_accessed=40_000_000, transcendentals=0
+        ),
+        name="tile_sum",
+    )(g.reshape((devices,) + tail))
+
+
+AXIS_BITS = {
+    "far": ("dp", 2),
+    "near": ("dp", 1),
+    "y": ("dp", 0),
+    "x": ("seq", 1),
+    "core": ("seq", 0),
+}
+ADDRESS = ("far", "near", "y", "x")
+FLOW_ORDERS = (("y", "near", "far", "x"), ("near", "x", "y", "far"), ("x", "y", "near", "far"))
+HALF = TILE // 2
+
+
+def flow_stages(order):
+    left = list(ADDRESS)
+    stages = []
+    for name in order:
+        place = left.index(name)
+        stages.append((name, 1 << place, 1 << (len(left) - 1 - place)))
+        left.pop(place)
+    return stages
+
+
+def paired_grad_kernel(
+    att_ref,
+    bg_ref,
+    og_ref,
+    nt_ref,
+    act_ref,
+    hg_ref,
+    half_ref,
+    made,
+    landed,
+    done,
+    out_made,
+    out_landed,
+    out_done,
+    zeros,
+    og_turned,
+    nt_turned,
+    send_sem,
+    recv_sem,
+    done_sem,
+    out_sem,
+    zero_sem,
+):
+    i = pl.program_id(0)
+    last = pl.num_programs(0) - 1
+    groups, seqs, width, span = att_ref.shape
+    d_tiles, f_tiles, per = D // TILE, FF // TILE, GRAD_CHUNK // TILE
+    count = per * d_tiles
+    spare = half_ref.shape[0] - N_QKV - N_REST
+    sibling, core = partner_of("seq", 0)
+    kept = pl.ds(pl.multiple_of(core * HALF, HALF), HALF)
+    given = pl.ds(pl.multiple_of((1 - core) * HALF, HALF), HALF)
+    slot = lax.rem(i, 2)
+
+    def to_sibling(step, slot):
+        return pltpu.make_async_remote_copy(
+            src_ref=made.at[slot, :, given],
+            dst_ref=landed.at[step],
+            send_sem=send_sem.at[slot],
+            recv_sem=recv_sem.at[step],
+            device_id=sibling,
+            device_id_type=MESH,
+        )
+
+    def out_to_sibling():
+        return pltpu.make_async_remote_copy(
+            src_ref=out_made.at[:, given],
+            dst_ref=out_landed,
+            send_sem=out_sem.at[0],
+            recv_sem=out_sem.at[1],
+            device_id=sibling,
+            device_id_type=MESH,
+        )
+
+    def out_copy():
+        return pltpu.make_async_copy(out_done, half_ref.at[pl.ds(N_QKV, N_OUT)], out_sem.at[2])
+
+    def zero_copies():
+        spots = [(N_QKV // 3 * j, N_QKV // 3) for j in range(3)]
+        if spare:
+            spots.append((N_QKV + N_REST, spare))
+        return [
+            pltpu.make_async_copy(
+                zeros.at[pl.ds(0, size)], half_ref.at[pl.ds(low, size)], zero_sem.at[j]
+            )
+            for j, (low, size) in enumerate(spots)
+        ]
+
+    def done_copies(step, slot):
+        copies = [
+            pltpu.make_async_copy(
+                done.at[slot, pl.ds(r * per, per)],
+                half_ref.at[pl.ds(N_QKV + N_OUT + r * f_tiles + step * per, per)],
+                done_sem.at[slot, r],
+            )
+            for r in range(d_tiles)
+        ]
+        copies.append(
+            pltpu.make_async_copy(
+                done.at[slot, pl.ds(count, count)],
+                half_ref.at[pl.ds(FIRST_PROJ + step * count, count)],
+                done_sem.at[slot, d_tiles],
+            )
+        )
+        return copies
+
+    @pl.when(i == 0)
+    def _():
+        greet([sibling])
+        zeros[...] = jnp.zeros_like(zeros)
+        for copy in zero_copies():
+            copy.start()
+        total = jnp.zeros((D, D), f32)
+        for s in range(seqs):
+            total = total + dot(
+                att_ref[:, s].reshape(groups * width, span), bg_ref[s * span : (s + 1) * span, :]
+            )
+        total = total.astype(bf16)
+        for r in range(d_tiles):
+            for c in range(d_tiles):
+                out_made[r * d_tiles + c] = total[
+                    r * TILE : (r + 1) * TILE, c * TILE : (c + 1) * TILE
+                ]
+        out_to_sibling().start()
+        og_turned[...] = og_ref[...].T
+        nt_turned[...] = nt_ref[...].T
+
+    @pl.when(i < last)
+    def _():
+        @pl.when(i >= 2)
+        def _():
+            to_sibling(i - 2, slot).wait_send()
+
+        proj = dot(og_turned[...], act_ref[...]).astype(bf16)
+        hid = dot(nt_turned[...], hg_ref[...]).astype(bf16)
+        for c in range(per):
+            for r in range(d_tiles):
+                rows, cols = slice(r * TILE, (r + 1) * TILE), slice(c * TILE, (c + 1) * TILE)
+                made[slot, count + c * d_tiles + r] = proj[rows, cols]
+                made[slot, r * per + c] = hid[rows, cols]
+        to_sibling(i, slot).start()
+
+    @pl.when(i >= 1)
+    def _():
+        before = 1 - slot
+
+        @pl.when(i >= 3)
+        def _():
+            for copy in done_copies(i - 3, before):
+                copy.wait()
+
+        to_sibling(i - 1, before).wait_recv()
+        done[before] = (
+            made[before, :, kept].astype(f32) + landed[i - 1].astype(f32)
+        ).astype(bf16)
+        for copy in done_copies(i - 1, before):
+            copy.start()
+
+    @pl.when(i == 1)
+    def _():
+        out_to_sibling().wait_recv()
+        out_done[...] = (out_made[:, kept].astype(f32) + out_landed[...].astype(f32)).astype(bf16)
+        out_copy().start()
+
+    @pl.when(i == last)
+    def _():
+        to_sibling(i - 2, slot).wait_send()
+        to_sibling(i - 1, 1 - slot).wait_send()
+        out_to_sibling().wait_send()
+        out_copy().wait()
+        for copy in zero_copies():
+            copy.wait()
+        for copy in done_copies(i - 2, slot):
+            copy.wait()
+        for copy in done_copies(i - 1, 1 - slot):
+            copy.wait()
+
+
+def paired_grads(total_tiles, att, bg, og, nt, act, hg):
+    total = bg.shape[0]
+    chunks = FF // GRAD_CHUNK
+    per = GRAD_CHUNK // TILE
+    count = per * (D // TILE)
+    dma = pltpu.SemaphoreType.DMA
+    column = pl.BlockSpec((total, GRAD_CHUNK), lambda i: (0, jnp.minimum(i, chunks - 1)))
+    return pl.pallas_call(
+        paired_grad_kernel,
+        grid=(chunks + 1,),
+        in_specs=[whole(a.shape) for a in (att, bg, og, nt)] + [column, column],
+        out_specs=pl.BlockSpec(memory_space=pl.ANY),
+        out_shape=jax.ShapeDtypeStruct((total_tiles, HALF, TILE), bf16),
+        scratch_shapes=[
+            pltpu.VMEM((2, 2 * count, TILE, TILE), bf16),
+            pltpu.VMEM((chunks, 2 * count, HALF, TILE), bf16),
+            pltpu.VMEM((2, 2 * count, HALF, TILE), bf16),
+            pltpu.VMEM((N_OUT, TILE, TILE), bf16),
+            pltpu.VMEM((N_OUT, HALF, TILE), bf16),
+            pltpu.VMEM((N_OUT, HALF, TILE), bf16),
+            pltpu.VMEM((N_QKV // 3, HALF, TILE), bf16),
+            pltpu.VMEM((D, total), bf16),
+            pltpu.VMEM((D, total), bf16),
+            dma((2,)),
+            dma((chunks,)),
+            dma((2, D // TILE + 1)),
+            dma((3,)),
+            dma((4,)),
+        ],
+        compiler_params=pltpu.CompilerParams(
+            dimension_semantics=("arbitrary",),
+            collective_id=4,
+            has_side_effects=True,
+            vmem_limit_bytes=VMEM_LIMIT,
+        ),
+        cost_estimate=pl.CostEstimate(
+            flops=12_000_000_000, bytes_accessed=40_000_000, transcendentals=0
+        ),
+        name="paired_grads",
+    )(att, bg, og, nt, act, hg)
+
+
+Q_UNITS = 27
+
+
+def attend_back_sum_kernel(
+    heads,
+    flows,
+    len_ref,
+    fresh_ref,
+    q_ref,
+    k_ref,
+    v_ref,
+    o_ref,
+    g_ref,
+    lse_ref,
+    x_ref,
+    w_ref,
+    half_ref,
+    in_ref,
+    dv_ref,
+    raw_ref,
+    db_ref,
+    dw,
+    q_wide,
+    k_wide,
+    g_wide,
+    v_wide,
+    g_turned,
+    dq_acc,
+    delta,
+    grads,
+    dk_acc,
+    dv_acc,
+    probs,
+    score_grads,
+    dxs,
+    dx_core,
+    dx_across,
+    in_made,
+    mine,
+    final,
+    final_other,
+    q_parts,
+    q_y,
+    q_near,
+    q_far,
+    q_own,
+    core_sem,
+    across_sem,
+    in_sem,
+    own_sem,
+    flow_send,
+    flow_recv,
+    final_sem,
+    q_send,
+    q_recv,
+    q_out,
+    q_in,
+    *lands,
+):
+    i = pl.program_id(0)
+    blocks, _, span, width_in = x_ref.shape
+    count = blocks * span
+    width = heads * HD
+    bq, bk = BACK_QUERY_BLOCK, BACK_KEY_BLOCK
+    per_seq = count // bk
+    seqs = dxs.shape[0]
+    n, ki = i // per_seq, i % per_seq
+    length = len_ref[n]
+    dp, s = lax.axis_index("dp"), lax.axis_index("seq")
+    y, x, core = dp % 2, s // 2, s % 2
+    near, far = (dp // 2) % 2, dp // 4
+    owned = raw_ref.shape[0]
+    first_tile = (dp * 4 + s) * owned
+    partners = {name: partner_of(axis, bit) for name, (axis, bit) in AXIS_BITS.items()}
+
+    def view(ref, above, below):
+        return ref.reshape(above, 2, below, *ref.shape[-3:])
+
+    def flow_send_copy(f, k):
+        low, size, stages = flows[f]
+        name, above, below = stages[k]
+        device, side = partners[name]
+        land = lands[f * 4 + k]
+        if k == 0:
+            source = view(half_ref, above, below).at[:, 1 - side, :, pl.ds(low, size)]
+        else:
+            source = view(lands[f * 4 + k - 1], above, below).at[:, 1 - side]
+        return pltpu.make_async_remote_copy(
+            src_ref=source,
+            dst_ref=land.reshape(above, below, *land.shape[-3:]),
+            send_sem=flow_send.at[f, k],
+            recv_sem=flow_recv.at[f, k],
+            device_id=device,
+            device_id_type=MESH,
+        )
+
+    def own_copy(f):
+        low, size, stages = flows[f]
+        name, above, below = stages[0]
+        return pltpu.make_async_copy(
+            view(half_ref, above, below).at[:, partners[name][1], :, pl.ds(low, size)],
+            mine.reshape(above, below, *mine.shape[-3:]).at[:, :, pl.ds(0, size)],
+            own_sem.at[f],
+        )
+
+    def flow_add(f, k):
+        low, size, stages = flows[f]
+        name, above, below = stages[k]
+        side = partners[name][1]
+        land = lands[f * 4 + k]
+        flow_send_copy(f, k).wait_recv()
+        if k == 0:
+            own_copy(f).wait()
+
+        def add(e, carry):
+            if k == 0:
+                kept = mine[e, 0:size]
+            else:
+                kept = lands[f * 4 + k - 1][((e // below) * 2 + side) * below + e % below]
+            total = kept.astype(f32) + land[e].astype(f32)
+            if k == 3:
+                final[low : low + size] = total
+            else:
+                land[e] = total.astype(bf16)
+            return carry
+
+        lax.fori_loop(0, above * below, add, 0)
+
+    def dx_core_copy(m, block):
+        return pltpu.make_async_remote_copy(
+            src_ref=dxs.at[m, block],
+            dst_ref=dx_core.at[m, block // 2],
+            send_sem=core_sem.at[m, block // 2, 0],
+            recv_sem=core_sem.at[m, block // 2, 1],
+            device_id=partners["core"][0],
+            device_id_type=MESH,
+        )
+
+    def dx_across_copy(m):
+        return pltpu.make_async_remote_copy(
+            src_ref=dx_core.at[m, 1 - x],
+            dst_ref=dx_across.at[m],
+            send_sem=across_sem.at[m, 0],
+            recv_sem=across_sem.at[m, 1],
+            device_id=partners["x"][0],
+            device_id_type=MESH,
+        )
+
+    def dx_pass(m, block):
+        @pl.when(block % 2 == core)
+        def _():
+            dx_core_copy(m, block).wait_recv()
+
+            @pl.when(block // 2 != x)
+            def _():
+                dx_core[m, 1 - x] = (
+                    dxs[m, block].astype(f32) + dx_core[m, 1 - x].astype(f32)
+                ).astype(bf16)
+                dx_across_copy(m).start()
+
+    def dx_end(m):
+        dx_across_copy(m).wait_recv()
+        if m:
+            in_copy(m - 1).wait()
+        in_made[...] = (
+            dxs[m, s].astype(f32) + dx_core[m, x].astype(f32) + dx_across[m].astype(f32)
+        )
+        in_copy(m).start()
+
+    def in_copy(m):
+        return pltpu.make_async_copy(in_made, in_ref.at[m], in_sem.at[m])
+
+    @pl.when(i == 0)
+    def _():
+        mates = [
+            (dp - y + (y + dy) % 2, (s + ds) % 4) for dy in range(2) for ds in range(4) if dy or ds
+        ]
+        greet(mates + [partners["near"][0], partners["far"][0]])
+        for f in range(3):
+            flow_send_copy(f, 0).start()
+        own_copy(0).start()
+        delta[...] = jnp.zeros_like(delta)
+        dw[...] = jnp.zeros_like(dw)
+        db_ref[...] = jnp.zeros_like(db_ref)
+
+    @pl.when(i == per_seq - 1)
+    def _():
+        for f in range(3):
+            flow_add(f, 0)
+            if f < 2:
+                own_copy(f + 1).start()
+            flow_send_copy(f, 1).start()
+
+    @pl.when(i > 0)
+    def _():
+        dx_pass((i - 1) // per_seq, (i - 1) % per_seq)
+
+    @pl.when(i == per_seq + 1)
+    def _():
+        for f in range(3):
+            flow_add(f, 1)
+            flow_send_copy(f, 2).start()
+
+    @pl.when(i == per_seq + 2)
+    def _():
+        for f in range(1, 3):
+            flow_add(f, 2)
+            flow_send_copy(f, 3).start()
+
+    @pl.when(i == per_seq + 3)
+    def _():
+        flow_add(0, 2)
+        flow_send_copy(0, 3).start()
+
+    @pl.when(ki == 0)
+    def _():
+        row = lax.broadcasted_iota(jnp.int32, (16, count), 0)
+        dead = lax.broadcasted_iota(jnp.int32, (16, count), 1) >= length
+        ones = jnp.where(row < 3, 1.0, 0.0)
+        key_side = jnp.where((row == 3) & dead, masked_score, ones).astype(bf16)
+        ones = ones.astype(bf16)
+
+        def in_parts(line, last):
+            high = line.astype(bf16).astype(f32)
+            rest = line - high
+            middle = rest.astype(bf16).astype(f32)
+            low = rest - middle
+            parts = jnp.where(row == 0, high, jnp.where(row == 1, middle, low))
+            return jnp.where(row < 3, parts, jnp.where(row == 3, last, 0.0)).astype(bf16)
+
+        for b in range(blocks):
+            at = slice(b * span, (b + 1) * span)
+            g_block = g_ref[b, 0]
+            g_turned[:, at] = g_block
+            product = o_ref[b, 0].astype(f32) * g_block.astype(f32)
+            for h in range(heads):
+                rows = slice(h * HD, (h + 1) * HD)
+                delta[h : h + 1, at] = jnp.sum(product[rows, :], axis=0, keepdims=True)
+        for h in range(heads):
+            rows = slice(h * HD, (h + 1) * HD)
+            lse_part = in_parts(lse_ref[0, h : h + 1, :] * (-1.0 / (SCALE * LOG2E)), 1.0)
+            delta_part = in_parts(-delta[h : h + 1, :], 0.0)
+            q_wide[h] = jnp.concatenate([q_ref[0, rows, :], lse_part], axis=0).T
+            g_wide[h] = jnp.concatenate([g_turned[rows, :], delta_part], axis=0).T
+            k_wide[h, 0:HD] = k_ref[0, rows, :]
+            k_wide[h, HD : HD + 16] = key_side
+            v_wide[h, 0:HD] = v_ref[0, rows, :]
+            v_wide[h, HD : HD + 16] = ones
+        dq_acc[...] = jnp.zeros_like(dq_acc)
+
+    k0 = pl.multiple_of(ki * bk, bk)
+    dk_acc[...] = jnp.zeros_like(dk_acc)
+    dv_acc[...] = jnp.zeros_like(dv_acc)
+
+    def step(qi, masked, low=0, cols_here=bk):
+        skip = low if masked else 0
+        here = slice(low, low + cols_here)
+        keys = pl.ds(pl.multiple_of(k0 + low, HALF_BLOCK), cols_here)
+        at = pl.ds(pl.multiple_of(qi * bq + skip, HALF_BLOCK), bq - skip)
+        tall = bq - skip
+        for h in range(heads):
+            rows = slice(h * HD, (h + 1) * HD)
+            for c0 in range(0, cols_here, SUB_COLS):
+                some = pl.ds(pl.multiple_of(k0 + low + c0, TILE), SUB_COLS)
+                cols = slice(c0, c0 + SUB_COLS)
+                for r0 in range(0, tall, SUB_ROWS):
+                    part = pl.ds(pl.multiple_of(qi * bq + skip + r0, TILE), SUB_ROWS)
+                    p = jnp.exp2(dot(q_wide[h, part, :], k_wide[h, :, some]) * (SCALE * LOG2E))
+                    if masked and r0 < c0 + SUB_COLS - 1:
+                        shape = (SUB_ROWS, SUB_COLS)
+                        allowed = c0 + lax.broadcasted_iota(
+                            jnp.int32, shape, 1
+                        ) <= r0 + lax.broadcasted_iota(jnp.int32, shape, 0)
+                        p = jnp.where(allowed, p, 0.0)
+                    probs[h, r0 : r0 + SUB_ROWS, cols] = p.astype(bf16)
+                    score_grads[h, r0 : r0 + SUB_ROWS, cols] = (
+                        p * dot(g_wide[h, part, :], v_wide[h, :, some])
+                    ).astype(bf16)
+        for h in range(heads):
+            rows = slice(h * HD, (h + 1) * HD)
+            p = probs[h, 0:tall, 0:cols_here]
+            ds = score_grads[h, 0:tall, 0:cols_here]
+            dv_acc[rows, here] = dv_acc[rows, here] + dot(g_turned[rows, at], p)
+            dk_acc[rows, here] = dk_acc[rows, here] + dot(q_ref[0, rows, at], ds)
+            dq_acc[rows, at] = dq_acc[rows, at] + dot(k_ref[0, rows, keys], ds, NT)
+
+    step(ki, True, 0, HALF_BLOCK)
+    step(ki, True, HALF_BLOCK, HALF_BLOCK)
+    lax.fori_loop(ki + 1, count // bq, lambda j, c: (step(j, False), c)[1], 0)
+    grads[0:width, :] = (dq_acc[:, pl.ds(k0, bk)] * SCALE).astype(bf16)
+    grads[width : 2 * width, :] = (dk_acc[...] * SCALE).astype(bf16)
+    grads[2 * width :, :] = dv_acc[...].astype(bf16)
+    dv_ref[ki, 0] = grads[2 * width :, :]
+
+    @pl.when(x == 1)
+    def _():
+        grads[2 * width :, :] = jnp.zeros((width, bk), bf16)
+
+    dw[...] += dot(grads[...], x_ref[ki, 0])
+    db_ref[...] += dot(jnp.ones((8, bk), bf16), grads[...], NT)[0:1]
+
+    def q_copy(kind, c):
+        at = pl.ds(c * 9, 9)
+        if kind == 0:
+            source, target, name = q_parts.at[1 - y, at], q_y.at[at], "y"
+        elif kind == 1:
+            source, target, name = q_y.at[at], q_near.at[at], "near"
+        else:
+            source, target, name = q_y.at[at], q_far.at[at], "far"
+        return pltpu.make_async_remote_copy(
+            src_ref=source,
+            dst_ref=target,
+            send_sem=q_send.at[kind, c],
+            recv_sem=q_recv.at[kind, c],
+            device_id=partners[name][0],
+            device_id_type=MESH,
+        )
+
+    def q_deliver(c, act):
+        for e in range(c * 9, c * 9 + 9):
+            r = 3 * y + (e // 3) % 3
+            unit = core * 3 + e % 3
+            if c < 2:
+                index = c * N_OUT + r * (D // TILE) + 3 * x + unit // 2
+            else:
+                index = 2 * N_OUT + r * (VW // TILE) + unit // 2
+            owner = index // owned
+            target = (owner // 4, owner % 4)
+            rows = pl.ds(pl.multiple_of((unit % 2) * HALF, HALF), HALF)
+            here = (target[0] == dp) & (target[1] == s)
+            real = (x == 0) if c == 2 else (x >= 0)
+            spot = q_own.at[index % owned, rows]
+
+            @pl.when(real & here)
+            def _():
+                if act == "start":
+                    pltpu.make_async_copy(q_y.at[e], spot, q_in).start()
+
+            @pl.when(real & jnp.logical_not(here))
+            def _():
+                copy = pltpu.make_async_remote_copy(
+                    src_ref=q_y.at[e],
+                    dst_ref=spot,
+                    send_sem=q_out.at[e],
+                    recv_sem=q_in,
+                    device_id=target,
+                    device_id_type=MESH,
+                )
+                if act == "start":
+                    copy.start()
+                else:
+                    copy.wait_send()
+
+    def q_add(c, extra):
+        at = slice(c * 9, c * 9 + 9)
+        kept = q_parts[y, at] if extra is q_y else q_y[at]
+        q_y[at] = (kept.astype(f32) + extra[at].astype(f32)).astype(bf16)
+
+    @pl.when(i == seqs * per_seq - 1)
+    def _():
+        for e in range(Q_UNITS):
+            which, rr, piece = e // 9, (e // 3) % 3, e % 3
+            at = which * width + piece * HALF
+            for yy in range(2):
+                r = 3 * yy + rr
+                q_parts[yy, e] = dw[at : at + HALF, r * TILE : (r + 1) * TILE].astype(bf16)
+        for c in range(3):
+            q_copy(0, c).start()
+
+    dxs[n, ki] = dot(grads[...], w_ref[...], TN).astype(bf16)
+
+    @pl.when(ki % 2 != core)
+    def _():
+        dx_core_copy(n, ki).start()
+
+    @pl.when(i == seqs * per_seq - 1)
+    def _():
+        to_sibling = pltpu.make_async_remote_copy(
+            src_ref=final.at[pl.ds((1 - core) * owned, owned)],
+            dst_ref=final_other,
+            send_sem=final_sem.at[0],
+            recv_sem=final_sem.at[1],
+            device_id=partners["core"][0],
+            device_id_type=MESH,
+        )
+
+        def q_first(c):
+            q_copy(0, c).wait_recv()
+            q_add(c, q_y)
+
+            @pl.when(near == 1)
+            def _():
+                q_copy(1, c).start()
+
+        def q_second(c):
+            @pl.when(near == 0)
+            def _():
+                q_copy(1, c).wait_recv()
+                q_add(c, q_near)
+
+                @pl.when(far == 1)
+                def _():
+                    q_copy(2, c).start()
+
+        def q_third(c):
+            @pl.when((near == 0) & (far == 0))
+            def _():
+                q_copy(2, c).wait_recv()
+                q_add(c, q_far)
+                q_deliver(c, "start")
+
+        q_first(0)
+        dx_pass(seqs - 1, per_seq - 1)
+        q_first(1)
+        q_second(0)
+        q_first(2)
+        q_second(1)
+        for f in range(3):
+            flow_add(f, 3)
+        to_sibling.start()
+        q_third(0)
+        q_second(2)
+        q_third(1)
+        dx_end(0)
+        q_third(2)
+        to_sibling.wait_recv()
+        kept = pl.ds(pl.multiple_of(core * HALF, HALF), HALF)
+        given = pl.ds(pl.multiple_of((1 - core) * HALF, HALF), HALF)
+        raw_ref[:, kept, :] = final[pl.ds(core * owned, owned)]
+        raw_ref[:, given, :] = final_other[...]
+        for m in range(1, seqs):
+            dx_end(m)
+
+        @pl.when(first_tile + owned <= N_QKV)
+        def _():
+            pltpu.make_async_copy(q_own, q_own, q_in).wait()
+            raw_ref[...] = q_own[...].astype(f32)
+
+        part = N_QKV % owned
+        if part:
+
+            @pl.when((first_tile < N_QKV) & (first_tile + owned > N_QKV))
+            def _():
+                at = pl.ds(0, part)
+                pltpu.make_async_copy(q_own.at[at], q_own.at[at], q_in).wait()
+                raw_ref[0:part] = q_own[0:part].astype(f32)
+
+        in_copy(seqs - 1).wait()
+        to_sibling.wait_send()
+        for m in range(seqs):
+            for pair in range(2):
+                dx_core_copy(m, 2 * pair + 1 - core).wait_send()
+            dx_across_copy(m).wait_send()
+        for f in range(3):
+            for k in range(4):
+                flow_send_copy(f, k).wait_send()
+        for c in range(3):
+            q_copy(0, c).wait_send()
+
+            @pl.when(near == 1)
+            def _():
+                q_copy(1, c).wait_send()
+
+            @pl.when((near == 0) & (far == 1))
+            def _():
+                q_copy(2, c).wait_send()
+
+            @pl.when((near == 0) & (far == 0))
+            def _():
+                q_deliver(c, "wait")
+
+
+def attend_back_sum(lengths, fresh, q, k, v, o, g, lse, x, w, half):
+    blocks, seqs, span, _ = x.shape
+    width = q.shape[1]
+    heads = width // HD
+    count = blocks * span
+    owned = half.shape[0] // 32
+    per_seq = count // BACK_KEY_BLOCK
+    pair = 2 * owned
+    edges = [pair * p // 3 for p in range(4)]
+    flows = [
+        (low, high - low, flow_stages(order))
+        for low, high, order in zip(edges, edges[1:], FLOW_ORDERS)
+    ]
+    one = lambda shape: pl.BlockSpec((1,) + shape, lambda i, *_: (i // per_seq,) + (0,) * len(shape))
+    mid = lambda shape: pl.BlockSpec((blocks, 1) + shape, lambda i, *_: (0, i // per_seq, 0, 0))
+    single = lambda shape: pl.BlockSpec(
+        (1,) + shape, lambda i, *_: (i // per_seq, 0, 0), pipeline_mode=pl.Buffered(1)
+    )
+    dma = pltpu.SemaphoreType.DMA
+    return pl.pallas_call(
+        functools.partial(attend_back_sum_kernel, heads, flows),
+        grid_spec=pltpu.PrefetchScalarGridSpec(
+            num_scalar_prefetch=2,
+            grid=(seqs * per_seq,),
+            in_specs=[
+                one((width, count)),
+                single((width, count)),
+                single((width, count)),
+                pl.BlockSpec(
+                    (blocks, 1, width, span),
+                    lambda i, *_: (0, i // per_seq, 0, 0),
+                    pipeline_mode=pl.Buffered(1),
+                ),
+                mid((width, span)),
+                one((8, count)),
+                pl.BlockSpec(
+                    (blocks, 1, span, D),
+                    lambda i, *_: (0, i // per_seq, 0, 0),
+                    pipeline_mode=pl.Buffered(1),
+                ),
+                pl.BlockSpec(
+                    (3 * width, D), lambda i, *_: (0, 0), pipeline_mode=pl.Buffered(1)
+                ),
+                pl.BlockSpec(memory_space=pl.ANY),
+            ],
+            out_specs=[
+                pl.BlockSpec(memory_space=pl.ANY),
+                mid((width, span)),
+                whole((owned, TILE, TILE)),
+                whole((1, 3 * width)),
+            ],
+            scratch_shapes=[
+                pltpu.VMEM((3 * width, D), f32),
+                pltpu.VMEM((heads, count, HD + 16), bf16),
+                pltpu.VMEM((heads, HD + 16, count), bf16),
+                pltpu.VMEM((heads, count, HD + 16), bf16),
+                pltpu.VMEM((heads, HD + 16, count), bf16),
+                pltpu.VMEM((width, count), bf16),
+                pltpu.VMEM((width, count), f32),
+                pltpu.VMEM((8, count), f32),
+                pltpu.VMEM((3 * width, BACK_KEY_BLOCK), bf16),
+                pltpu.VMEM((width, BACK_KEY_BLOCK), f32),
+                pltpu.VMEM((width, BACK_KEY_BLOCK), f32),
+                pltpu.VMEM((heads, BACK_QUERY_BLOCK, BACK_KEY_BLOCK), bf16),
+                pltpu.VMEM((heads, BACK_QUERY_BLOCK, BACK_KEY_BLOCK), bf16),
+                pltpu.VMEM((seqs, blocks, span, D), bf16),
+                pltpu.VMEM((seqs, 2, span, D), bf16),
+                pltpu.VMEM((seqs, span, D), bf16),
+                pltpu.VMEM((span, D), f32),
+                pltpu.VMEM((8, -(-pair // 3), HALF, TILE), bf16),
+                pltpu.VMEM((pair, HALF, TILE), f32),
+                pltpu.VMEM((owned, HALF, TILE), f32),
+                pltpu.VMEM((2, Q_UNITS, HALF, TILE), bf16),
+                pltpu.VMEM((Q_UNITS, HALF, TILE), bf16),
+                pltpu.VMEM((Q_UNITS, HALF, TILE), bf16),
+                pltpu.VMEM((Q_UNITS, HALF, TILE), bf16),
+                pltpu.VMEM((owned, TILE, TILE), bf16),
+                dma((seqs, 2, 2)),
+                dma((seqs, 2)),
+                dma((seqs,)),
+                dma((3,)),
+                dma((3, 4)),
+                dma((3, 4)),
+                dma((2,)),
+                dma((3, 3)),
+                dma((3, 3)),
+                dma((Q_UNITS,)),
+                dma(()),
+            ]
+            + [
+                pltpu.VMEM((8 >> k, size, HALF, TILE), bf16)
+                for _, size, _ in flows
+                for k in range(4)
+            ],
+        ),
+        out_shape=[
+            jax.ShapeDtypeStruct((seqs, span, D), f32),
+            jax.ShapeDtypeStruct((blocks, seqs, width, span), bf16),
+            jax.ShapeDtypeStruct((owned, TILE, TILE), f32),
+            jax.ShapeDtypeStruct((1, 3 * width), f32),
+        ],
+        compiler_params=pltpu.CompilerParams(
+            dimension_semantics=("arbitrary",),
+            collective_id=5,
+            has_side_effects=True,
+            vmem_limit_bytes=VMEM_LIMIT,
+        ),
+        cost_estimate=pl.CostEstimate(
+            flops=70_000_000_000, bytes_accessed=25_000_000, transcendentals=0
+        ),
+        name="attend_back_sum",
+    )(lengths, fresh, q, k, v, o, g, lse, x, w, half.reshape(16, pair, HALF, TILE))
+
+
+VEC_ROWS = 72
+
+
+def finish_kernel(
+    stages,
+    raw_ref,
+    gain_ref,
+    rows_ref,
+    hsum_ref,
+    db_ref,
+    master_ref,
+    left_ref,
+    right_ref,
+    left_root_ref,
+    right_root_ref,
+    par_ref,
+    stat_ref,
+    clip_out,
+    left_out,
+    right_out,
+    tiles_out,
+    vec_out,
+    stat_out,
+    par_out,
+    norm_out,
+    total,
+    landing,
+    send_sem,
+    recv_sem,
+):
+    owned = raw_ref.shape[0]
+    used = par_ref.shape[0]
+    partners = [partner_of(axis, bit)[0] for axis, bit in stages]
+    greet(partners)
+    squares = jnp.zeros((TILE, TILE), f32)
+    for t in range(owned):
+        squares = squares + raw_ref[t] * raw_ref[t]
+    per = D // TILE
+    width = db_ref.shape[1] // 3
+    group = lax.axis_index("seq")
+    total[...] = jnp.zeros_like(total)
+    for piece, (ref, row) in enumerate(
+        ((gain_ref, 0), (gain_ref, 1), (rows_ref, 0), (rows_ref, 1), (None, 0), (rows_ref, 2), (rows_ref, 3))
+    ):
+        if ref is not None:
+            for c in range(per):
+                total[piece * per + c : piece * per + c + 1, :] = ref[
+                    row : row + 1, c * TILE : (c + 1) * TILE
+                ]
+    for part, start in ((0, 4 * per), (2, 7 * per)):
+        for unit in range(width // HALF):
+            value = db_ref[:, part * width + unit * HALF : part * width + (unit + 1) * HALF]
+            both = jnp.concatenate([value, value], axis=1)
+            lane = lax.broadcasted_iota(jnp.int32, (1, TILE), 1) // HALF
+            place = group * (width // HALF) + unit
+            room = (D if part == 0 else VW) // HALF
+            row = start + jnp.minimum(place, room - 1) // 2
+            keep = (lane == place % 2) & (place < room)
+            total[pl.ds(row, 1), :] = total[pl.ds(row, 1), :] + jnp.where(keep, both, 0.0)
+    for c in range(FF // TILE):
+        at = 7 * per + VW // TILE + c
+        total[at : at + 1, :] = hsum_ref[:, c * TILE : (c + 1) * TILE]
+    total[used : used + 1, :] = jnp.sum(squares, axis=0, keepdims=True)
+    for i, device in enumerate(partners):
+        landing[i, 0] = total[...]
+        copy = pltpu.make_async_remote_copy(
+            src_ref=landing.at[i, 0],
+            dst_ref=landing.at[i, 1],
+            send_sem=send_sem.at[i],
+            recv_sem=recv_sem.at[i],
+            device_id=device,
+            device_id_type=MESH,
+        )
+        copy.start()
+        copy.wait()
+        total[...] = total[...] + landing[i, 1]
+    vector = total[0:used, :]
+    square_sum = jnp.sum(total[used : used + 1, :], axis=1, keepdims=True) + jnp.sum(
+        jnp.sum(vector * vector, axis=0, keepdims=True), axis=1, keepdims=True
+    )
+    grad_norm = jnp.sqrt(square_sum)
+    factor = jnp.minimum(1.0, CLIP / (grad_norm + clip_eps))
+    norm_out[...] = jnp.broadcast_to(grad_norm, norm_out.shape)
+    grads = vector * factor
+    vec_out[...] = grads
+    stat = decay_rate * stat_ref[...] + (1.0 - decay_rate) * grads * grads
+    stat_out[...] = stat
+    par_out[...] = par_ref[...] - vector_rate * grads / (jnp.sqrt(stat) + moment_eps)
+    first = (lax.axis_index("dp") * lax.axis_size("seq") + lax.axis_index("seq")) * owned
+
+    def exact(a, b, dims):
+        return lax.dot_general(a, b, dims, precision=highest, preferred_element_type=f32)
+
+    for t in range(owned):
+        index = first + t
+        turned = (index < N_QKV) | (index >= FIRST_PROJ)
+        raw = raw_ref[t]
+        tile = jnp.where(turned, raw.T, raw) * factor
+        clip_out[t] = tile
+        left_out[t] = decay_rate * left_ref[t] + (1.0 - decay_rate) * exact(tile, tile, NT)
+        flipped = tile.T
+        right_out[t] = decay_rate * right_ref[t] + (1.0 - decay_rate) * exact(flipped, flipped, NT)
+        inner = exact(tile, right_root_ref[t], NN)
+        tiles_out[t] = master_ref[t] - matrix_rate * exact(left_root_ref[t], inner, NN)
+
+
+def finish(raw, vectors, master, left, right, left_root, right_root, par, stat, dp, seq):
+    stages = exchange_bits(dp, seq)
+    tiles = jax.ShapeDtypeStruct(raw.shape, f32)
+    vector = jax.ShapeDtypeStruct(par.shape, f32)
+    vm = pl.BlockSpec(memory_space=pltpu.VMEM)
+    return pl.pallas_call(
+        functools.partial(finish_kernel, stages),
+        in_specs=[vm] * 12,
+        out_specs=[vm] * 8,
+        out_shape=[tiles] * 4 + [vector] * 3 + [jax.ShapeDtypeStruct((8, TILE), f32)],
+        scratch_shapes=[
+            pltpu.VMEM((VEC_ROWS, TILE), f32),
+            pltpu.VMEM((len(stages), 2, VEC_ROWS, TILE), f32),
+            pltpu.SemaphoreType.DMA((len(stages),)),
+            pltpu.SemaphoreType.DMA((len(stages),)),
+        ],
+        compiler_params=pltpu.CompilerParams(
+            collective_id=2, has_side_effects=True, vmem_limit_bytes=VMEM_LIMIT
+        ),
+        name="finish",
+    )(raw, *vectors, master, left, right, left_root, right_root, par, stat)
 
 
 def per_device(
@@ -629,7 +2106,6 @@
     owned_count = master_tiles.shape[0]
     groups = lax.axis_size("seq")
     me_seq = lax.axis_index("seq")
-    me = lax.axis_index("dp") * groups + me_seq
     width = D // groups
     fresh_groups = VW // width
     total_tiles = owned_count * groups * lax.axis_size("dp")
@@ -647,10 +2123,17 @@
     ) = split_vector(vector_params)
 
     gathered = lax.all_gather(master_tiles.astype(bf16), ("dp", "seq"), axis=0, tiled=True)
+    fits = front_fits(lax.axis_size("dp"), groups, owned_count)
     flat_tokens = tokens.reshape(-1, D).astype(f32)
     normed_one, unit_one, inv_one = norm_forward(flat_tokens, gain_one, shift_one)
-    normed_one = normed_one.astype(bf16).reshape(seqs, span, D)
-    x_all = lax.all_gather(normed_one, "seq", axis=0, tiled=False)
+    if fits:
+        norm_rows = jnp.concatenate(
+            [jnp.stack([gain_one, shift_one]), jnp.zeros((6, D), f32)]
+        )
+        x_all, w_mine = front(tokens, norm_rows, master_tiles)
+    else:
+        normed_one = normed_one.astype(bf16).reshape(seqs, span, D)
+        x_all = lax.all_gather(normed_one, "seq", axis=0, tiled=False)
     first_turned = first_values.transpose(2, 0, 1).reshape(groups - fresh_groups, width, seqs, span)
     first_turned = first_turned.transpose(0, 2, 1, 3)
     first_send = jnp.concatenate(
@@ -666,14 +2149,16 @@
         tiles = gathered[start : start + amount].reshape(D // TILE, cols // TILE, TILE, TILE)
         return tiles.transpose(1, 3, 0, 2).reshape(cols, D)
 
-    wq = lax.dynamic_slice_in_dim(turned(0, D), me_seq * width, width, 0)
-    wk = lax.dynamic_slice_in_dim(turned(N_OUT, D), me_seq * width, width, 0)
-    wv = lax.dynamic_slice_in_dim(turned(2 * N_OUT, VW), fresh_seq * width, width, 0)
+    if not fits:
+        wq = lax.dynamic_slice_in_dim(turned(0, D), me_seq * width, width, 0)
+        wk = lax.dynamic_slice_in_dim(turned(N_OUT, D), me_seq * width, width, 0)
+        wv = lax.dynamic_slice_in_dim(turned(2 * N_OUT, VW), fresh_seq * width, width, 0)
+        w_mine = jnp.concatenate([wq, wk, wv], axis=0)
     qb = lax.dynamic_slice_in_dim(query_bias, me_seq * width, width, 0).reshape(width, 1)
     vb = lax.dynamic_slice_in_dim(value_bias, fresh_seq * width, width, 0).reshape(width, 1)
 
     o_heads, q, k, v, lse = attend_forward(
-        lengths, is_fresh, x_all, wq, wk, wv, qb, vb, first_mine
+        lengths, is_fresh, x_all, w_mine, qb, vb, first_mine
     )
     att = lax.all_to_all(o_heads, "seq", 0, 0, tiled=True)
     rows = jnp.concatenate(
@@ -695,18 +2180,22 @@
         lengths, position, att, tokens, cotangent, gathered, rows, hidden_bias.reshape(1, FF)
     )
     g_heads = lax.all_to_all(att_grad, "seq", 0, 0, tiled=True)
-    grad_out, grad_hidden, grad_proj = weight_grads(
-        att, branch_grad, out_grad, normed_two, act, hidden_grad
-    )
-    w_mine = jnp.concatenate([wq, wk, wv], axis=0)
-    dx, dv, dw, db = attend_backward(
-        lengths, is_fresh, q, k, v, o_heads, g_heads, lse, x_all, w_mine
-    )
-    norm_one_in = (
-        lax.psum_scatter(dx, "seq", scatter_dimension=0, tiled=True)
-        .reshape(-1, D)
-        .astype(f32)
-    )
+    grad_args = (att, branch_grad, out_grad, normed_two, act, hidden_grad)
+    back_args = (q, k, v, o_heads, g_heads, lse, x_all, w_mine)
+    if fits:
+        half_tiles = paired_grads(total_tiles, *grad_args)
+        norm_one_in, dv, owned, db = attend_back_sum(lengths, is_fresh, *back_args, half_tiles)
+        norm_one_in = norm_one_in.reshape(-1, D)
+    else:
+        all_tiles = weight_grads(total_tiles, *grad_args)
+        group = me_seq.astype(jnp.int32).reshape(1)
+        dx, dv, all_tiles, db = attend_backward(lengths, is_fresh, group, *back_args, all_tiles)
+        norm_one_in = (
+            lax.psum_scatter(dx, "seq", scatter_dimension=0, tiled=True)
+            .reshape(-1, D)
+            .astype(f32)
+        )
+        owned = tile_sum(all_tiles, lax.axis_size("dp"), groups)
     dv_back = lax.all_to_all(dv, "seq", 0, 0, tiled=True)
     first_grad = (
         dv_back[fresh_groups:]
@@ -719,74 +2208,22 @@
     gain_one_grad = jnp.sum(norm_one_in * unit_one, axis=0)
     shift_one_grad = jnp.sum(norm_one_in, axis=0)
 
-    dw = dw.astype(bf16)
-    big = jnp.zeros((2 * D, D), bf16)
-    big = lax.dynamic_update_slice(big, dw[0:width], (me_seq * width, 0))
-    big = lax.dynamic_update_slice(big, dw[width : 2 * width], (D + me_seq * width, 0))
-    small = lax.dynamic_update_slice(
-        jnp.zeros((VW, D), bf16), dw[2 * width :], (fresh_seq * width, 0)
-    )
-
-    def turned_tiles(matrix):
-        cols = matrix.shape[0]
-        return (
-            matrix.reshape(cols // TILE, TILE, D // TILE, TILE)
-            .transpose(2, 0, 1, 3)
-            .reshape(-1, TILE, TILE)
+    used = vector_params.shape[0] // TILE
+    gain_sums = jnp.stack([gain_one_grad, shift_one_grad])
+    clipped, left_new, right_new, tiles_new, vector_grads, vector_stat_new, vector_new, norm = (
+        finish(
+            owned,
+            (gain_sums, row_sums, hidden_bias_grad, db),
+            master_tiles,
+            left_stat,
+            right_stat,
+            left_root,
+            right_root,
+            vector_params.reshape(used, TILE),
+            vector_stat.reshape(used, TILE),
+            lax.axis_size("dp"),
+            groups,
         )
-
-    grad_stack = jnp.concatenate(
-        [
-            turned_tiles(big[:D]),
-            turned_tiles(big[D:]),
-            turned_tiles(small),
-            grad_out,
-            grad_hidden.reshape(N_HID, TILE, TILE),
-            grad_proj,
-            jnp.zeros((total_tiles - N_QKV - N_REST, TILE, TILE), bf16),
-        ],
-        axis=0,
-    )
-    owned = lax.psum_scatter(grad_stack, ("dp", "seq"), scatter_dimension=0, tiled=True)
-    index = me * owned_count + jnp.arange(owned_count)
-    flipped = (index < N_QKV) | (index >= FIRST_PROJ)
-    owned = owned.astype(f32)
-    owned = jnp.where(flipped[:, None, None], owned.swapaxes(1, 2), owned)
-
-    query_bias_grad = lax.dynamic_update_slice(
-        jnp.zeros((D,), f32), db[0, 0:width], (me_seq * width,)
-    )
-    value_bias_grad = lax.dynamic_update_slice(
-        jnp.zeros((VW,), f32), db[0, 2 * width :], (fresh_seq * width,)
-    )
-    vector_local = jnp.concatenate(
-        [
-            gain_one_grad,
-            shift_one_grad,
-            row_sums[0],
-            row_sums[1],
-            query_bias_grad,
-            row_sums[2],
-            row_sums[3],
-            value_bias_grad,
-            hidden_bias_grad[0],
-        ]
-    )
-    summed_vector, owned_square = lax.psum((vector_local, jnp.sum(owned * owned)), ("dp", "seq"))
-    grad_norm = jnp.sqrt(owned_square + jnp.sum(summed_vector * summed_vector))
-    factor = jnp.minimum(1.0, CLIP / (grad_norm + clip_eps))
-    clipped = owned * factor
-    left_gram = jnp.einsum("tij,tkj->tik", clipped, clipped, precision=highest)
-    right_gram = jnp.einsum("tji,tjk->tik", clipped, clipped, precision=highest)
-    inner = jnp.einsum("tij,tjk->tik", clipped, right_root, precision=highest)
-    step = jnp.einsum("tij,tjk->tik", left_root, inner, precision=highest)
-    left_new = decay_rate * left_stat + (1.0 - decay_rate) * left_gram
-    right_new = decay_rate * right_stat + (1.0 - decay_rate) * right_gram
-    tiles_new = master_tiles - matrix_rate * step
-    vector_grads = summed_vector * factor
-    vector_stat_new = decay_rate * vector_stat + (1.0 - decay_rate) * vector_grads * vector_grads
-    vector_new = vector_params - vector_rate * vector_grads / (
-        jnp.sqrt(vector_stat_new) + moment_eps
     )
     return (
         block_output,
@@ -796,10 +2233,10 @@
         left_new,
         right_new,
         tiles_new,
-        vector_grads,
-        vector_stat_new,
-        vector_new,
-        grad_norm,
+        vector_grads.reshape(-1),
+        vector_stat_new.reshape(-1),
+        vector_new.reshape(-1),
+        norm[0, 0],
     )
 
 

time: 685 us -> 422 us (0.62)
  waiting for transfers between devices: 383 us -> 17.7 us
  Pallas kernels: 145 us -> 341 us
  blocking collectives: 37.7 us -> 0 us
  local copies, waits for them, and re-layouts: 53.3 us -> 18.9 us
  matrix products: 10.1 us -> 0 us
    pallas_call x2 -> x4, Pallas kernels: 59.6 us -> 266 us  [the longest x1 139 us: attend_back_sum(): pl.pallas_call(functools.partial(attend_back_sum_kernel, heads, flows), g...]
    reduce_scatter x2 -> x0, waiting for transfers between devices: 188 us -> none  [the longest x1 166 us: per_device(): lax.psum_scatter(grad_stack, ('dp', 'seq'), scatter_dimension=0, tiled=True)]
    all_gather x1, waiting for transfers between devices: 95.9 us -> 0.01 us  [per_device(): lax.all_gather(master_tiles.astype(bf16), ('dp', 'seq'), axis=0, tiled=True)]
    psum x1 -> x0, blocking collectives: 37.7 us -> none  [per_device(): lax.psum((vector_local, jnp.sum(owned * owned)), ('dp', 'seq'))]
    all_gather x1 -> x0, waiting for transfers between devices: 33.7 us -> none  [per_device(): x_all = lax.all_gather(normed_one, 'seq', axis=0, tiled=False)]
    all_to_all x1, waiting for transfers between devices: 27.2 us -> 0.01 us  [per_device(): dv_back = lax.all_to_all(dv, 'seq', 0, 0, tiled=True)]
    all_to_all x1, waiting for transfers between devices: 19 us -> 0.01 us  [per_device(): g_heads = lax.all_to_all(att_grad, 'seq', 0, 0, tiled=True)]
    reshape x6 -> x0, local copies, waits for them, and re-layouts: 11.9 us -> none  [the longest x3 7.53 us: turned_tiles(): matrix.reshape(cols // TILE, TILE, D // TILE, TILE).transpose(2, 0, 1, 3)]
  transfers between devices with their start and end apart: 8 -> 5, of which waited for: 7 -> 1; matrix products, arithmetic and copies ran while one was open for 8% -> 4% of each run, Pallas kernels for 3% -> 38%
where the time goes in v2:
time: 422 us; the launch traced here: 420 us
  Pallas kernels  341 us (81%)
  local copies, waits for them, and re-layouts  18.9 us (4%)
  waiting for transfers between devices  17.7 us (4%)
  starting transfers between devices  15.9 us (4%)
  between operations  14.3 us (3%)
  other arithmetic  11.9 us (3%)
    pallas_call x1, Pallas kernels, attend_back_sum(): pl.pallas_call(functools.partial(attend_back_sum_kernel, heads, flows), g...  139 us
    pallas_call x1, Pallas kernels, front(): pl.pallas_call(front_kernel, in_specs=[vm] * 3, out_specs=[pl.BlockSpec(m...  79.1 us
    pallas_call x1, Pallas kernels, feed_forward(): pl.pallas_call(feed_forward_kernel, grid_spec=pltpu.PrefetchScalarGridSpe...  43.9 us
    pallas_call x1, Pallas kernels, attend_forward(): pl.pallas_call(functools.partial(attend_forward_kernel, heads), grid_spec...  30.6 us
    pallas_call x1, Pallas kernels, finish(): pl.pallas_call(functools.partial(finish_kernel, stages), in_specs=[vm] *...  24.2 us
    pallas_call x1, Pallas kernels, paired_grads(): pl.pallas_call(paired_grad_kernel, grid=(chunks + 1,), in_specs=[whole(a....  24 us
    all_to_all x1, waiting for transfers between devices, per_device(): att = lax.all_to_all(o_heads, 'seq', 0, 0, tiled=True)  17.7 us
    unnamed x37, local copies, waits for them, and re-layouts  13.2 us
  transfers between devices with their start and end apart: 5, of which 1 were waited for; matrix products, arithmetic and copies ran while one was open for 4% of the time, Pallas kernels for 38%

profile of v2, /device:TPU:0, one launch (start us, length us, event | category | flops | bytes accessed | tf_op | source)
XLA Modules:
  0.0 419.6 jit_solution(13463192647196982835)
XLA Ops:
  7.2 0.0 all-gather.2.cloned.1.call-start
  7.2 2.0 convert_element_type.21
  9.2 0.0 all-gather.2.cloned.1.call-update
  9.2 1.4 copy.28
  10.7 0.1 copy.35
  10.7 0.0 copy-start.8
  10.7 1.3 concatenate.10
  12.0 4.2 %all-to-all-start = ((bf16[4,2,192,512]{3,2,1,0:T(8,128)(2,1)}), bf16[4,2,192,512]{3,2,1,0:T(8,128)(2,1)S(1)}, u32[]{:S(2)}, u32[]{:S(2)}) async-start(bf16[4,2,192,512]{3,2,1,0:T(8,128)(2,1)} %concatenate.10), calls=%async_computation | async-start | bytes 3145728 | tf_op jit(solution)/shard_map/all_to_all | solution.py:2142
  16.2 0.0 copy-done.8
  16.2 0.0 copy-start.9
  16.3 0.1 pad.5.clone
  16.3 0.7 maximum_maximum_fusion.rows_ref
  17.0 79.1 %front.1 = (bf16[4,2,512,768]{3,2,1,0:T(8,128)(2,1)}, bf16[576,768]{1,0:T(8,128)(2,1)}) custom-call(bf16[2,512,768]{2,1,0:T(8,128)(2,1)} %tok_ref.3, f32[8,768]{1,0:T(8,128)} %maximum_maximum_fusion.rows_ref, f32[13,128,128]{2,1,0:T(8,128)} %master_ref.3), custom_call_target="tpu_custom_call" | custom-call | flops 40000000000 | bytes 20000000 | tf_op jit(solution)/shard_map/front/pallas_call | solution.py:326
  96.1 0.0 copy-done.9
  96.2 0.1 dynamic_slice.6
  96.2 0.8 copy.30.qb_ref
  97.0 0.1 dynamic_slice.7
  97.1 0.8 copy.31.vb_ref
  97.9 0.0 all-to-all-done.fv_ref
  97.9 1.1 copy-done.2
  99.0 30.6 %attend_forward.1 = (bf16[4,2,192,512]{3,2,1,0:T(8,128)(2,1)}, bf16[2,192,2048]{2,1,0:T(8,128)(2,1)}, bf16[2,192,2048]{2,1,0:T(8,128)(2,1)}, bf16[2,192,2048]{2,1,0:T(8,128)(2,1)}, f32[2,8,2048]{2,1,0:T(8,128)}) custom-call(s32[2]{0:T(128)} %len_ref.5, s32[1]{0:T(128)} %bitcast.1.fresh_ref, bf16[4,2,512,768]{3,2,1,0:T(8,128)(2,1)} %get-tuple-element.40.x_ref, ...), custom_call_target="tpu_custom_call" | custom-call | flops 40000000000 | bytes 20000000 | tf_op jit(solution)/shard_map/attend_forward/pallas_call | solution.py:463
  129.6 3.9 all-to-all-start.1
  133.5 0.6 slice.41
  134.1 0.6 concatenate.11.rows_ref
  134.8 0.0 copy-done
  134.8 0.3 convert_reduce_fusion
  135.1 0.6 fusion.10
  135.7 17.7 %all-to-all-done.1.att_ref = bf16[4,2,192,512]{3,2,1,0:T(8,128)(2,1)S(1)} async-done(((bf16[4,2,192,512]{3,2,1,0:T(8,128)(2,1)}), bf16[4,2,192,512]{3,2,1,0:T(8,128)(2,1)S(1)}, u32[]{:S(2)}, u32[]{:S(2)}) %all-to-all-start.1) | async-done | bytes 1572896 | tf_op jit(solution)/shard_map/all_to_all | solution.py:2163
  153.4 1.1 copy-done.3
  154.5 43.9 %feed_forward.1 = (bf16[2,512,768]{2,1,0:T(8,128)(2,1)}, f32[2,512,768]{2,1,0:T(8,128)}, bf16[4,2,192,512]{3,2,1,0:T(8,128)(2,1)}, bf16[1024,3072]{1,0:T(8,128)(...) custom-call(s32[2]{0:T(128)} %len_ref.5, ...), custom_call_target="tpu_custom_call" | custom-call | flops 24000000000 | bytes 40000000 | tf_op jit(solution)/shard_map/feed_forward/pallas_call | solution.py:824
  198.4 3.8 all-to-all-start.2
  202.2 24.0 %paired_grads.1 = bf16[416,64,128]{2,1,0:T(8,128)(2,1)} custom-call(bf16[4,2,192,512]{3,2,1,0:T(8,128)(2,1)} %copy-done.3, bf16[1024,768]{1,0:T(8,128)(2,1)} %get-tuple-element.50.bg_ref, bf16[1024,768]{1,0:T(8,128)(2,1)} %get-tuple-element.51.og_ref, bf16[1024,768]{1,0:T(8,128)(2,1)} %get-tuple-element.52.nt_ref, ...), custom_call_target="tpu_custom_call" | custom-call | flops 12000000000 | bytes 40000000 | tf_op jit(solution)/shard_map/paired_grads/pallas_call | solution.py:1342
  226.2 0.0 all-to-all-done.2.g_ref
  226.2 0.0 copy-start.4
  226.2 1.1 copy-done.4
  227.4 139.0 %attend_back_sum.1 = (f32[2,512,768]{2,1,0:T(8,128)}, bf16[4,2,192,512]{3,2,1,0:T(8,128)(2,1)}, f32[13,128,128]{2,1,0:T(8,128)}, f32[1,576]{1,0:T(1,128)}) custom-call(s32[2]{0:T(128)} %len_ref.5, s32[1]{0:T(128)} %bitcast.1.fresh_ref, bf16[2,192,2048]{2,1,0:T(8,128)(2,1)} %get-tuple-element.45.q_ref, bf16[2,192,2048]{2,1,0:T(8,128)(2,1)} %get-tuple-element.46.k_ref, ...), custom_call_target="tpu_custom_call" | custom-call | flops 70000001024 | bytes 25000000 | tf_op jit(solution)/shard_map/attend_back_sum/pallas_call | solution.py:1868
  366.3 0.0 copy-start.1
  366.4 0.0 copy-start.10
  366.4 4.0 all-to-all-start.3
  370.3 0.0 copy-done.1
  370.3 0.0 copy-done.10
  370.4 3.0 fusion.9
  373.3 0.6 pad_maximum_fusion.gain_ref
  373.9 24.2 %finish.1 = (f32[13,128,128]{2,1,0:T(8,128)}, f32[13,128,128]{2,1,0:T(8,128)}, f32[13,128,128]{2,1,0:T(8,128)}, f32[13,128,128]{2,1,0:T(8,128)}, f32[69,128]{1,0...) custom-call(f32[13,128,128]{2,1,0:T(8,128)} %get-tuple-element.57.raw_ref, ...), custom_call_target="tpu_custom_call" | custom-call | tf_op jit(solution)/shard_map/finish/pallas_call | solution.py:2074
  398.2 1.2 slice.43
  399.4 4.5 %fusion.8 = f32[2,512,768]{2,1,0:T(8,128)} fusion(f32[2,512,768]{2,1,0:T(8,128)} %get-tuple-element.44, bf16[2,512,768]{2,1,0:T(8,128)(2,1)S(1)} %copy-done.1, f32[2,512,768]{2,1,0:T(8,128)} %get-tuple-element.55, f32[2,512]{1,0:T(2,128)S(1)} %get-tuple-element.102, f32[2,512]{1,0:T(2,128)S(1)} %add_rsqrt_fusion, f32[2,512]{1,0:T(2,128)S(1)} %broadcast_multiply_fusion.1, ...), kind=kLoop, calls=%fused_computation.10 | loop fusion | flops 7077888 | bytes 11029504 | tf_op jit(solution)/shard_map/add | solution.py:2207
  403.9 0.0 all-to-all-done.3
  403.9 0.2 convert_bitcast_fusion
  404.2 0.1 copy.32
  404.3 0.0 copy-start.7
  404.3 0.0 copy-start.6
  404.3 1.6 copy.33
  405.9 2.2 copy.43
  408.1 0.0 copy-done.7
  408.1 0.9 copy.44
  409.0 0.0 copy-done.6
  409.0 0.9 copy.45
  409.9 0.0 copy-done.5
  409.9 0.9 copy.46
  410.8 0.0 copy-done.13
  410.8 0.6 copy.47
  411.5 0.0 copy-done.12
  411.5 0.6 copy.48
  412.1 0.6 copy.49
  (24 shorter events, 0.1 us)
Async XLA Ops:
  7.2 146.2 %all-gather.2.cloned.1.call-start = ((), (), s32[]{:S(2)}) async-start(), calls=%async_computation.4 | async-start | bytes 14057472 | tf_op jit(solution)/shard_map/all_gather | solution.py:2125
  10.7 5.5 %copy-start.8 = (f32[8832]{0:T(1024)S(1)}, f32[8832]{0:T(1024)}, u32[]{:S(2)}) copy-start(f32[8832]{0:T(1024)} %param.20) | copy-start | bytes 105988
  12.0 85.9 %all-to-all-start = ((bf16[4,2,192,512]{3,2,1,0:T(8,128)(2,1)}), bf16[4,2,192,512]{3,2,1,0:T(8,128)(2,1)S(1)}, u32[]{:S(2)}, u32[]{:S(2)}) async-start(bf16[4,2,192,512]{3,2,1,0:T(8,128)(2,1)} %concatenate.10), calls=%async_computation | async-start | bytes 3145728 | tf_op jit(solution)/shard_map/all_to_all | solution.py:2142
  16.2 79.9 %copy-start.9 = (f32[768]{0:T(1024)}, f32[768]{0:T(1024)S(1)}, u32[]{:S(2)}) copy-start(f32[768]{0:T(1024)S(1)} %get-tuple-element.101) | copy-start | bytes 9220
  97.9 1.1 copy-start.2
  129.6 5.2 %copy-start = (bf16[2,512,768]{2,1,0:T(8,128)(2,1)S(1)}, bf16[2,512,768]{2,1,0:T(8,128)(2,1)}, u32[]{:S(2)}) copy-start(bf16[2,512,768]{2,1,0:T(8,128)(2,1)} %tok_ref.3) | copy-start | bytes 4718596
  129.6 23.8 %all-to-all-start.1 = ((bf16[4,2,192,512]{3,2,1,0:T(8,128)(2,1)}), bf16[4,2,192,512]{3,2,1,0:T(8,128)(2,1)S(1)}, u32[]{:S(2)}, u32[]{:S(2)}) async-start(bf16[4,2,192,512]{3,2,1,0:T(8,128)(2,1)} %get-tuple-element.42.o_ref), calls=%async_computation.1 | async-start | bytes 3145728 | tf_op jit(solution)/shard_map/all_to_all | solution.py:2163
  153.4 1.1 copy-start.3
  198.4 27.8 %all-to-all-start.2 = ((bf16[4,2,192,512]{3,2,1,0:T(8,128)(2,1)}), bf16[4,2,192,512]{3,2,1,0:T(8,128)(2,1)S(1)}, u32[]{:S(2)}, u32[]{:S(2)}) async-start(bf16[4,2,192,512]{3,2,1,0:T(8,128)(2,1)} %get-tuple-element.48), calls=%async_computation.2 | async-start | bytes 3145728 | tf_op jit(solution)/shard_map/all_to_all | solution.py:2182
  226.2 1.1 copy-start.4
  366.3 4.0 copy-start.1
  366.4 4.0 copy-start.10
  366.4 37.6 %all-to-all-start.3 = ((bf16[4,2,192,512]{3,2,1,0:T(8,128)(2,1)}), bf16[4,2,192,512]{3,2,1,0:T(8,128)(2,1)S(1)}, u32[]{:S(2)}, u32[]{:S(2)}) async-start(bf16[4,2,192,512]{3,2,1,0:T(8,128)(2,1)} %get-tuple-element.56), calls=%async_computation.3 | async-start | bytes 3145728 | tf_op jit(solution)/shard_map/all_to_all | solution.py:2199
  404.3 3.8 copy-start.7
  404.3 4.7 %copy-start.6 = (f32[13,128,128]{2,1,0:T(8,128)S(1)}, f32[13,128,128]{2,1,0:T(8,128)}, u32[]{:S(2)}) copy-start(f32[13,128,128]{2,1,0:T(8,128)} %get-tuple-element.120) | copy-start | bytes 2555908
  405.9 4.0 copy-start.5
  405.9 4.9 %copy-start.13 = (f32[69,128]{1,0:T(8,128)S(1)}, f32[69,128]{1,0:T(8,128)}, u32[]{:S(2)}) copy-start(f32[69,128]{1,0:T(8,128)} %get-tuple-element.65) | copy-start | bytes 105988
  405.9 5.5 %copy-start.12 = (f32[69,128]{1,0:T(8,128)S(1)}, f32[69,128]{1,0:T(8,128)}, u32[]{:S(2)}) copy-start(f32[69,128]{1,0:T(8,128)} %get-tuple-element.66) | copy-start | bytes 105988
  405.9 6.2 %copy-start.11 = (f32[69,128]{1,0:T(8,128)S(1)}, f32[69,128]{1,0:T(8,128)}, u32[]{:S(2)}) copy-start(f32[69,128]{1,0:T(8,128)} %get-tuple-element.67) | copy-start | bytes 105988
Sparse Core Ops, SparseCore 0:
  11.4 120.2 all-gather.1

commit v3 on v2

--- a/solution.py
+++ b/solution.py
@@ -20,6 +20,7 @@
 BACK_QUERY_BLOCK = 512
 BACK_KEY_BLOCK = 512
 HALF_BLOCK = 256
+STRIPE = 256
 SUB_ROWS = 256
 SUB_COLS = 256
 N_QKV = 90
@@ -100,9 +101,14 @@
     tok_ref,
     rows_ref,
     master_ref,
+    fv_ref,
     x_ref,
     w_ref,
+    fv_all,
+    g_one,
+    g_two,
     normed,
+    plain,
     staged,
     slots,
     x_send,
@@ -112,6 +118,13 @@
     first_recv,
     w_send,
     w_recv,
+    g_own,
+    g_send,
+    g_recv,
+    z_send,
+    z_recv,
+    fv_send,
+    fv_recv,
 ):
     dp, s = lax.axis_index("dp"), lax.axis_index("seq")
     depth = lax.axis_size("dp") // 2
@@ -187,10 +200,72 @@
                 else:
                     copy.wait_send()
 
+    one = g_one.shape[2]
+    parts = (
+        (plain.at[pl.ds(0, one)], g_one.at[z, x], (dp, other_x)),
+        (plain.at[pl.ds(one, owned - one)], g_two.at[dp], (other_y, s)),
+    )
+
+    def g_local(f):
+        source, target, _ = parts[f]
+        return pltpu.make_async_copy(source, target, g_own.at[f])
+
+    def g_first(f):
+        source, target, device = parts[f]
+        return pltpu.make_async_remote_copy(
+            src_ref=source,
+            dst_ref=target,
+            send_sem=g_send.at[f],
+            recv_sem=g_recv.at[f],
+            device_id=device,
+            device_id_type=MESH,
+        )
+
+    def z_copy(up, h, f):
+        plane = z - h if up else z + h
+        block = g_one.at[plane] if f == 0 else g_two.at[pl.ds(2 * plane, 2)]
+        return pltpu.make_async_remote_copy(
+            src_ref=block,
+            dst_ref=block,
+            send_sem=z_send.at[up, h, f],
+            recv_sem=z_recv.at[up, h, f],
+            device_id=(dp + 2, s) if up else (dp - 2, s),
+            device_id_type=MESH,
+        )
+
+    def z_landed(up, h, f):
+        plane = z - 1 - h if up else z + 1 + h
+        block = g_one.at[plane] if f == 0 else g_two.at[pl.ds(2 * plane, 2)]
+        return pltpu.make_async_copy(block, block, z_recv.at[up, h, f])
+
+    def z_hop(h):
+        for up in (1, 0):
+            if h:
+                came = (z - h >= 0) if up else (z + h <= depth - 1)
+
+                @pl.when(came)
+                def _():
+                    for f in range(2):
+                        z_landed(up, h - 1, f).wait()
+
+            if h < z_send.shape[1]:
+                goes = ((z < depth - 1) & (z - h >= 0)) if up else ((z > 0) & (z + h <= depth - 1))
+
+                @pl.when(goes)
+                def _():
+                    for f in range(2):
+                        z_copy(up, h, f).start()
+
+    for t in range(owned):
+        plain[t] = master_ref[t].astype(bf16)
+    for f in range(2):
+        g_first(f).start()
+        g_local(f).start()
+
     @pl.when(first < N_QKV)
     def _():
         for t in range(owned):
-            staged[t] = master_ref[t].astype(bf16).T
+            staged[t] = plain[t].T
         for t in range(owned):
             tile_sends(t, "start")
 
@@ -223,6 +298,30 @@
         x_copy(0, j).start()
         x_copy(1, j).start()
         own_copy(j).start()
+
+    def fv_copies(act):
+        for c in range(2):
+            to = 2 + c
+
+            @pl.when(s == to)
+            def _():
+                copy = pltpu.make_async_copy(fv_ref.at[c], fv_all.at[s], fv_recv.at[to])
+                if act == "start":
+                    copy.start()
+
+            @pl.when(s != to)
+            def _():
+                copy = pltpu.make_async_remote_copy(
+                    src_ref=fv_ref.at[c],
+                    dst_ref=fv_all.at[s],
+                    send_sem=fv_send.at[c],
+                    recv_sem=fv_recv.at[s],
+                    device_id=(dp, to),
+                    device_id_type=MESH,
+                )
+                copy.start() if act == "start" else copy.wait_send()
+
+    fv_copies("start")
 
     share = y * 2 + core
 
@@ -252,7 +351,11 @@
             (W_SHARE - used,) + slots.shape[1:], bf16
         )
 
-    for j in range(max(len(W_CHUNKS), X_CHUNKS)):
+    for f in range(2):
+        g_first(f).wait_recv()
+        g_local(f).wait()
+    z_hop(0)
+    for j in range(len(W_CHUNKS)):
         if j < len(W_CHUNKS):
             low, size = W_CHUNKS[j]
             short = min(size, used - low)
@@ -277,12 +380,15 @@
 
             w_copy(1, j).start()
             w_copy(2, j).start()
-        if j < X_CHUNKS:
-            x_copy(0, j).wait_recv()
-            x_copy(2, j).start()
         if j < len(W_CHUNKS):
             w_copy(1, j).wait_recv()
             w_copy(3, j).start()
+    z_hop(1)
+    for j in range(X_CHUNKS):
+        if j == X_CHUNKS - 1:
+            z_hop(2)
+        x_copy(0, j).wait_recv()
+        x_copy(2, j).start()
     for j in range(len(W_CHUNKS)):
         w_copy(2, j).wait_recv()
         w_copy(3, j).wait_recv()
@@ -302,6 +408,25 @@
         own_copy(j).wait()
         for kind in range(3):
             x_copy(kind, j).wait_send()
+    @pl.when(x == 1)
+    def _():
+        for block in range(4):
+            pltpu.make_async_copy(fv_all.at[block], fv_all.at[block], fv_recv.at[block]).wait()
+
+    fv_copies("wait")
+    z_hop(3)
+    for f in range(2):
+        g_first(f).wait_send()
+        for h in range(z_send.shape[1]):
+
+            @pl.when((z < depth - 1) & (z - h >= 0))
+            def _():
+                z_copy(1, h, f).wait_send()
+
+            @pl.when((z > 0) & (z + h <= depth - 1))
+            def _():
+                z_copy(0, h, f).wait_send()
+
     for j in range(len(W_CHUNKS)):
 
         @pl.when(z < depth - 1)
@@ -317,22 +442,27 @@
             tile_sends(t, "wait")
 
 
-def front(tokens, rows, master):
+def front(tokens, rows, master, first_turned):
     seqs, span, _ = tokens.shape
     owned = master.shape[0]
-    vm = pl.BlockSpec(memory_space=pltpu.VMEM)
+    one = (owned + 1) // 2
+    vm, hbm = pl.BlockSpec(memory_space=pltpu.VMEM), pl.BlockSpec(memory_space=pl.ANY)
     dma = pltpu.SemaphoreType.DMA
     chunks = len(W_CHUNKS)
     return pl.pallas_call(
         front_kernel,
-        in_specs=[vm] * 3,
-        out_specs=[pl.BlockSpec(memory_space=pl.ANY), vm],
+        in_specs=[vm] * 3 + [hbm],
+        out_specs=[hbm, vm, hbm, hbm, hbm],
         out_shape=[
             jax.ShapeDtypeStruct((4, seqs, span, D), bf16),
             jax.ShapeDtypeStruct((9 * HD, D), bf16),
+            jax.ShapeDtypeStruct((4,) + first_turned.shape[1:], bf16),
+            jax.ShapeDtypeStruct((4, 2, one, TILE, TILE), bf16),
+            jax.ShapeDtypeStruct((8, owned - one, TILE, TILE), bf16),
         ],
         scratch_shapes=[
             pltpu.VMEM((seqs, span, D), bf16),
+            pltpu.VMEM((owned, TILE, TILE), bf16),
             pltpu.VMEM((owned, TILE, TILE), bf16),
             pltpu.VMEM((W_SLOTS, TILE, TILE), bf16),
             dma((3, X_CHUNKS)),
@@ -342,6 +472,13 @@
             dma((chunks,)),
             dma((4, chunks)),
             dma((4, chunks)),
+            dma((2,)),
+            dma((2,)),
+            dma((2,)),
+            dma((2, 3, 2)),
+            dma((2, 3, 2)),
+            dma((2,)),
+            dma((4,)),
         ],
         compiler_params=pltpu.CompilerParams(
             collective_id=3, has_side_effects=True, vmem_limit_bytes=VMEM_LIMIT
@@ -350,7 +487,7 @@
             flops=40_000_000_000, bytes_accessed=20_000_000, transcendentals=0
         ),
         name="front",
-    )(tokens, rows, master)
+    )(tokens, rows, master, first_turned)
 
 
 def attend_forward_kernel(
@@ -372,6 +509,8 @@
     values,
     acc,
     top,
+    fades,
+    probs,
 ):
     blocks, _, span, width_in = x_ref.shape
     count = blocks * span
@@ -412,26 +551,35 @@
         def step(ki, masked, low=0, rows_here=bk):
             k0 = pl.multiple_of(ki * bk + low, HALF_BLOCK)
             skip = low if masked else 0
-            cols = slice(skip, bq)
-            if masked:
-                shape = (rows_here, bq - skip)
-                key_pos = k0 + lax.broadcasted_iota(jnp.int32, shape, 0)
-                query_pos = q0 + skip + lax.broadcasted_iota(jnp.int32, shape, 1)
-                allowed = (key_pos <= query_pos) & (key_pos < length)
             for h in range(heads):
-                rows = slice(h * HD, (h + 1) * HD)
-                at = pl.ds(pl.multiple_of(q0 + skip, HALF_BLOCK), bq - skip)
-                s = dot(k_heads[h, pl.ds(k0, rows_here), :], q_wide[h, :, at])
-                s = s * (SCALE * LOG2E)
-                if masked:
-                    s = jnp.where(allowed, s, masked_score)
-                top_old = top[h : h + 1, cols]
-                top_new = jnp.maximum(top_old, jnp.max(s, axis=0, keepdims=True))
-                p = jnp.exp2(s - top_new)
-                fade = jnp.exp2(top_old - top_new)
-                top[h : h + 1, cols] = top_new
-                acc[h, :, cols] = acc[h, :, cols] * fade + dot(
-                    values[h, :, pl.ds(k0, rows_here)], p.astype(bf16)
+                for c0 in range(skip, bq, STRIPE):
+                    cols = slice(c0, c0 + STRIPE)
+                    at = pl.ds(pl.multiple_of(q0 + c0, TILE), STRIPE)
+                    parts = []
+                    for r0 in range(0, rows_here, HALF_BLOCK):
+                        keys = pl.ds(pl.multiple_of(k0 + r0, HALF_BLOCK), HALF_BLOCK)
+                        s = dot(k_heads[h, keys, :], q_wide[h, :, at])
+                        if masked and c0 - low - r0 < HALF_BLOCK:
+                            shape = (HALF_BLOCK, STRIPE)
+                            allowed = low + r0 + lax.broadcasted_iota(
+                                jnp.int32, shape, 0
+                            ) <= c0 + lax.broadcasted_iota(jnp.int32, shape, 1)
+                            s = jnp.where(allowed, s, masked_score)
+                        parts.append(s)
+                    top_old = top[h : h + 1, cols]
+                    top_new = top_old
+                    for s in parts:
+                        top_new = jnp.maximum(top_new, jnp.max(s, axis=0, keepdims=True))
+                    top[h : h + 1, cols] = top_new
+                    fades[h : h + 1, cols] = jnp.exp2((top_old - top_new) * (SCALE * LOG2E))
+                    for part, s in enumerate(parts):
+                        probs[h, part * HALF_BLOCK : (part + 1) * HALF_BLOCK, cols] = jnp.exp2(
+                            (s - top_new) * (SCALE * LOG2E)
+                        ).astype(bf16)
+            wide = slice(skip, bq)
+            for h in range(heads):
+                acc[h, :, wide] = acc[h, :, wide] * fades[h : h + 1, wide] + dot(
+                    values[h, :, pl.ds(k0, rows_here)], probs[h, 0:rows_here, wide]
                 )
 
         lax.fori_loop(
@@ -447,7 +595,9 @@
             rows = slice(h * HD, (h + 1) * HD)
             sums = acc[h, HD : HD + 1, :]
             o_ref[qi, 0, rows, :] = (acc[h, 0:HD, :] / sums).astype(bf16)
-            lse_ref[0, h : h + 1, pl.ds(q0, bq)] = top[h : h + 1, :] + jnp.log2(sums)
+            lse_ref[0, h : h + 1, pl.ds(q0, bq)] = (
+                top[h : h + 1, :] * (SCALE * LOG2E) + jnp.log2(sums)
+            )
         return carry
 
     lax.fori_loop(0, count // bq, one_query_block, 0)
@@ -482,6 +632,8 @@
                 pltpu.VMEM((heads, HD + 16, count), bf16),
                 pltpu.VMEM((heads, HD + 16, QUERY_BLOCK), f32),
                 pltpu.VMEM((8, QUERY_BLOCK), f32),
+                pltpu.VMEM((8, QUERY_BLOCK), f32),
+                pltpu.VMEM((heads, KEY_BLOCK, QUERY_BLOCK), bf16),
             ],
         ),
         out_shape=[
@@ -712,14 +864,31 @@
 
 
 def feed_forward_kernel(
+    part_count,
     len_ref,
     pos_ref,
     att_ref,
     tok_ref,
     cot_ref,
-    tiles_ref,
     rows_ref,
     hb_ref,
+    *rest,
+):
+    sources, rest = rest[:part_count], rest[part_count:]
+    feed_forward_body(
+        len_ref, pos_ref, att_ref, tok_ref, cot_ref, rows_ref, hb_ref, sources, *rest
+    )
+
+
+def feed_forward_body(
+    len_ref,
+    pos_ref,
+    att_ref,
+    tok_ref,
+    cot_ref,
+    rows_ref,
+    hb_ref,
+    sources,
     out_ref,
     rg_ref,
     ag_ref,
@@ -735,7 +904,6 @@
     w_hidden,
     w_proj,
     output_acc,
-    norm_acc,
     sem,
 ):
     n = pl.program_id(0)
@@ -743,21 +911,47 @@
 
     @pl.when(n == 0)
     def _():
-        copies = []
-        for i, (start, amount) in enumerate(
-            ((0, N_OUT), (N_OUT, N_HID), (N_OUT + N_HID, N_PROJ))
-        ):
-            copy = pltpu.make_async_copy(
-                tiles_ref.at[pl.ds(N_QKV + start, amount)],
-                tiles.at[pl.ds(start, amount)],
-                sem.at[i],
-            )
+        if len(sources) == 1:
+            skipped = N_QKV
+            copies = [
+                pltpu.make_async_copy(
+                    sources[0].at[pl.ds(N_QKV, N_REST)], tiles, sem.at[0]
+                )
+            ]
+        else:
+            skipped = 0
+            dp, s = lax.axis_index("dp"), lax.axis_index("seq")
+            y, x, core = dp % 2, s // 2, s % 2
+            one = sources[0].shape[2]
+            owned = tiles.shape[0] // 32
+            spread = tiles.reshape(4, 2, 2, 2, owned, TILE, TILE)
+            copies = []
+            for c in range(2):
+                at_core = core if c == 0 else 1 - core
+                for other in range(2):
+                    at_y = y if other == 0 else 1 - y
+                    at_x = x if other == 0 else 1 - x
+                    copies.append(
+                        pltpu.make_async_copy(
+                            sources[c * 4 + other],
+                            spread.at[:, at_y, :, at_core, pl.ds(0, one)],
+                            sem.at[c * 4 + other],
+                        )
+                    )
+                    source = sources[c * 4 + 2 + other]
+                    copies.append(
+                        pltpu.make_async_copy(
+                            source.reshape(4, 2, owned - one, TILE, TILE),
+                            spread.at[:, :, at_x, at_core, pl.ds(one, owned - one)],
+                            sem.at[c * 4 + 2 + other],
+                        )
+                    )
+        for copy in copies:
             copy.start()
-            copies.append(copy)
-        for copy, start, matrix in zip(
-            copies, (0, N_OUT, N_OUT + N_HID), (w_out, w_hidden, w_proj)
-        ):
+        for copy in copies:
             copy.wait()
+        for start, matrix in zip((0, N_OUT, N_OUT + N_HID), (w_out, w_hidden, w_proj)):
+            start = start + N_QKV - skipped
             row_tiles, col_tiles = matrix.shape[0] // TILE, matrix.shape[1] // TILE
 
             def place(r, carry):
@@ -782,7 +976,7 @@
     out_grad_low = out_grad.astype(bf16)
     og_ref[...] = out_grad_low
     output_acc[...] = residual + proj_bias
-    norm_acc[...] = jnp.zeros_like(norm_acc)
+    rg_ref[0] = jnp.zeros((span, D), f32)
 
     def chunk(c, carry):
         cols = pl.ds(pl.multiple_of(c * HIDDEN_CHUNK, HIDDEN_CHUNK), HIDDEN_CHUNK)
@@ -798,12 +992,12 @@
         hg_ref[:, cols] = hidden_grad
         hsum_ref[:, cols] += jnp.sum(hidden_grad.astype(f32), axis=0, keepdims=True)
         output_acc[...] += dot(active, w_proj[cols, :])
-        norm_acc[...] += dot(hidden_grad, w_hidden[:, cols], NT)
+        rg_ref[0] += dot(hidden_grad, w_hidden[:, cols], NT)
         return carry
 
     lax.fori_loop(0, FF // HIDDEN_CHUNK, chunk, 0)
     out_ref[0] = output_acc[...].astype(bf16)
-    norm_in = norm_acc[...]
+    norm_in = rg_ref[0]
     residual_grad = out_grad + norm_backward(norm_in, unit, inv, gain_two)
     rg_ref[0] = residual_grad
     branch = residual_grad.astype(bf16)
@@ -815,25 +1009,32 @@
     sums_ref[3:4, :] += jnp.sum(out_grad, axis=0, keepdims=True)
 
 
-def feed_forward(lengths, position, att, tokens, cotangent, tiles, rows, hidden_bias):
+def feed_forward(lengths, position, att, tokens, cotangent, sources, total_tiles, rows, hidden_bias):
     groups, seqs, width, span = att.shape
     one = lambda shape: pl.BlockSpec((1,) + shape, lambda i, *_: (i,) + (0,) * len(shape))
     mid = lambda shape: pl.BlockSpec((groups, 1) + shape, lambda i, *_: (0, i, 0, 0))
     row = lambda cols: pl.BlockSpec((span, cols), lambda i, *_: (i, 0))
+    single = pl.BlockSpec(
+        (1, span, D), lambda i, *_: (i, 0, 0), pipeline_mode=pl.Buffered(1)
+    )
     total = seqs * span
     return pl.pallas_call(
-        feed_forward_kernel,
+        functools.partial(feed_forward_kernel, len(sources)),
         grid_spec=pltpu.PrefetchScalarGridSpec(
             num_scalar_prefetch=2,
             grid=(seqs,),
             in_specs=[
-                mid((width, span)),
-                one((span, D)),
-                one((span, D)),
-                pl.BlockSpec(memory_space=pl.ANY),
+                pl.BlockSpec(
+                    (groups, 1, width, span),
+                    lambda i, *_: (0, i, 0, 0),
+                    pipeline_mode=pl.Buffered(1),
+                ),
+                single,
+                single,
                 whole((8, D)),
                 whole((1, FF)),
-            ],
+            ]
+            + [pl.BlockSpec(memory_space=pl.ANY)] * len(sources),
             out_specs=[
                 one((span, D)),
                 one((span, D)),
@@ -847,13 +1048,12 @@
                 whole((1, FF)),
             ],
             scratch_shapes=[
-                pltpu.VMEM((N_REST, TILE, TILE), bf16),
+                pltpu.VMEM((N_REST if len(sources) == 1 else total_tiles, TILE, TILE), bf16),
                 pltpu.VMEM((D, D), bf16),
                 pltpu.VMEM((D, FF), bf16),
                 pltpu.VMEM((FF, D), bf16),
                 pltpu.VMEM((span, D), f32),
-                pltpu.VMEM((span, D), f32),
-                pltpu.SemaphoreType.DMA((3,)),
+                pltpu.SemaphoreType.DMA((8,)),
             ],
         ),
         out_shape=[
@@ -873,7 +1073,7 @@
             flops=24_000_000_000, bytes_accessed=40_000_000, transcendentals=0
         ),
         name="feed_forward",
-    )(lengths, position, att, tokens, cotangent, tiles, rows, hidden_bias)
+    )(lengths, position, att, tokens, cotangent, rows, hidden_bias, *sources)
 
 
 GRAD_CHUNK = 256
@@ -2122,25 +2322,36 @@
         hidden_bias,
     ) = split_vector(vector_params)
 
-    gathered = lax.all_gather(master_tiles.astype(bf16), ("dp", "seq"), axis=0, tiled=True)
     fits = front_fits(lax.axis_size("dp"), groups, owned_count)
     flat_tokens = tokens.reshape(-1, D).astype(f32)
     normed_one, unit_one, inv_one = norm_forward(flat_tokens, gain_one, shift_one)
+    first_turned = first_values.transpose(2, 0, 1).reshape(groups - fresh_groups, width, seqs, span)
+    first_turned = first_turned.transpose(0, 2, 1, 3)
     if fits:
         norm_rows = jnp.concatenate(
             [jnp.stack([gain_one, shift_one]), jnp.zeros((6, D), f32)]
         )
-        x_all, w_mine = front(tokens, norm_rows, master_tiles)
+        x_all, w_mine, first_mine, g_one, g_two = front(
+            tokens, norm_rows, master_tiles, first_turned
+        )
+
+        def swap(value, bit):
+            pairs = [(d, d ^ bit) for d in range(32)]
+            return lax.ppermute(value, ("dp", "seq"), pairs)
+
+        g_one_y, g_two_x = swap(g_one, 4), swap(g_two, 2)
+        g_one_core, g_two_core = swap(g_one, 1), swap(g_two, 1)
     else:
         normed_one = normed_one.astype(bf16).reshape(seqs, span, D)
         x_all = lax.all_gather(normed_one, "seq", axis=0, tiled=False)
-    first_turned = first_values.transpose(2, 0, 1).reshape(groups - fresh_groups, width, seqs, span)
-    first_turned = first_turned.transpose(0, 2, 1, 3)
-    first_send = jnp.concatenate(
-        [jnp.zeros((fresh_groups,) + first_turned.shape[1:], bf16), first_turned], axis=0
-    )
-    first_mine = lax.all_to_all(first_send, "seq", 0, 0, tiled=True)
-
+        gathered = lax.all_gather(
+            master_tiles.astype(bf16), ("dp", "seq"), axis=0, tiled=True
+        )
+        sources = (gathered,)
+        first_send = jnp.concatenate(
+            [jnp.zeros((fresh_groups,) + first_turned.shape[1:], bf16), first_turned], axis=0
+        )
+        first_mine = lax.all_to_all(first_send, "seq", 0, 0, tiled=True)
     is_fresh = (me_seq < fresh_groups).astype(jnp.int32).reshape(1)
     fresh_seq = jnp.minimum(me_seq, fresh_groups - 1)
 
@@ -2160,6 +2371,10 @@
     o_heads, q, k, v, lse = attend_forward(
         lengths, is_fresh, x_all, w_mine, qb, vb, first_mine
     )
+    if fits:
+        g_one_y, g_two_x, o_heads = lax.optimization_barrier((g_one_y, g_two_x, o_heads))
+        sources = (g_one, g_one_y, g_two, g_two_x)
+        sources += (g_one_core, swap(g_one_y, 1), g_two_core, swap(g_two_x, 1))
     att = lax.all_to_all(o_heads, "seq", 0, 0, tiled=True)
     rows = jnp.concatenate(
         [jnp.stack([gain_two, shift_two, out_bias, proj_bias]), jnp.zeros((4, D), f32)]
@@ -2177,7 +2392,15 @@
         row_sums,
         hidden_bias_grad,
     ) = feed_forward(
-        lengths, position, att, tokens, cotangent, gathered, rows, hidden_bias.reshape(1, FF)
+        lengths,
+        position,
+        att,
+        tokens,
+        cotangent,
+        sources,
+        total_tiles,
+        rows,
+        hidden_bias.reshape(1, FF),
     )
     g_heads = lax.all_to_all(att_grad, "seq", 0, 0, tiled=True)
     grad_args = (att, branch_grad, out_grad, normed_two, act, hidden_grad)

time: 422 us -> 404 us (0.957)
  between operations: 14.3 us -> 0.92 us
  Pallas kernels: 341 us -> 336 us
    pallas_call x1, Pallas kernels: 139 us -> 115 us  [attend_back_sum(): pl.pallas_call(functools.partial(attend_back_sum_kernel, heads, flows), g...]
    pallas_call x2, Pallas kernels: 123 us -> 138 us  [the longest x1 88.1 us: front(): pl.pallas_call(front_kernel, in_specs=[vm] * 3 + [hbm], out_specs=[hbm, v...]
    ppermute x0 -> x6, starting transfers between devices: none -> 6.87 us  [swap(): return lax.ppermute(value, ('dp', 'seq'), pairs)]
    unnamed x37 -> x33, local copies, waits for them, and re-layouts: 13.2 us -> 12.8 us
  transfers between devices with their start and end apart: 5 -> 9, of which waited for: 1 -> 1; matrix products, arithmetic and copies ran while one was open for 4% -> 4% of each run, Pallas kernels for 38% -> 21%
where the time goes in v3:
time: 404 us; the launch traced here: 403 us
  Pallas kernels  336 us (83%)
  local copies, waits for them, and re-layouts  20.3 us (5%)
  starting transfers between devices  18.4 us (5%)
  waiting for transfers between devices  17 us (4%)
  other arithmetic  9.89 us (2%)
    pallas_call x1, Pallas kernels, attend_back_sum(): pl.pallas_call(functools.partial(attend_back_sum_kernel, heads, flows), g...  115 us
    pallas_call x1, Pallas kernels, front(): pl.pallas_call(front_kernel, in_specs=[vm] * 3 + [hbm], out_specs=[hbm, v...  88.1 us
    pallas_call x1, Pallas kernels, feed_forward(): pl.pallas_call(functools.partial(feed_forward_kernel, len(sources)), grid...  50.1 us
    pallas_call x1, Pallas kernels, attend_forward(): pl.pallas_call(functools.partial(attend_forward_kernel, heads), grid_spec...  34.5 us
    pallas_call x1, Pallas kernels, finish(): pl.pallas_call(functools.partial(finish_kernel, stages), in_specs=[vm] *...  24.3 us
    pallas_call x1, Pallas kernels, paired_grads(): pl.pallas_call(paired_grad_kernel, grid=(chunks + 1,), in_specs=[whole(a....  24 us
    all_to_all x1, waiting for transfers between devices, per_device(): att = lax.all_to_all(o_heads, 'seq', 0, 0, tiled=True)  17 us
    unnamed x33, local copies, waits for them, and re-layouts  12.8 us
  transfers between devices with their start and end apart: 9, of which 1 were waited for; matrix products, arithmetic and copies ran while one was open for 4% of the time, Pallas kernels for 21%

profile of v3, /device:TPU:0, one launch (start us, length us, event | category | flops | bytes accessed | tf_op | source)
XLA Modules:
  0.0 402.7 jit_solution(9421045480727290111)
XLA Ops:
  0.6 0.8 fusion.11
  1.5 0.6 copy-done.7
  2.0 1.4 copy.22
  3.4 0.9 copy.29
  4.4 0.1 pad.4.clone
  4.5 0.7 maximum_maximum_fusion.rows_ref
  5.1 88.1 %front.1 = (bf16[4,2,512,768]{3,2,1,0:T(8,128)(2,1)}, bf16[576,768]{1,0:T(8,128)(2,1)}, bf16[4,2,192,512]{3,2,1,0:T(8,128)(2,1)}, bf16[4,2,7,128,128]{4,3,2,1,0:T(8,128)(2,1)}, bf16[8,6,128,128]{3,2,1,0:T(8,128)(2,1)}) custom-call(bf16[2,512,768]{2,1,0:T(8,128)(2,1)} %tok_ref.3, f32[8,768]{1,0:T(8,128)} %maximum_maximum_fusion.rows_ref, ...), custom_call_target="tpu_custom_call" | custom-call | flops 40000000000 | bytes 20000000 | tf_op jit(solution)/shard_map/front/pallas_call | solution.py:452
  93.2 0.9 collective-permute-start
  94.1 0.0 collective-permute-start.2
  94.1 5.3 %collective-permute-start.1 = (bf16[8,6,128,128]{3,2,1,0:T(8,128)(2,1)}, bf16[8,6,128,128]{3,2,1,0:T(8,128)(2,1)}, u32[]{:S(2)}, u32[]{:S(2)}) collective-permute-start(bf16[8,6,128,128]{3,2,1,0:T(8,128)(2,1)} %get-tuple-element.47.rest_2_), channel_id=1, source_target_pairs={{0,2},{1,3},{2,0},{3,1},{4,6},{5,7},{6,4},{7,5},{8,10},{9,11},{10,... | collective-permute-start | bytes 4718600 | tf_op jit(solution)/shard_map/ppermute | solution.py:2340
  99.4 0.7 slice.36
  100.0 0.1 dynamic_slice.6
  100.1 0.8 copy.24.qb_ref
  100.9 0.1 dynamic_slice.7
  101.0 0.8 copy.25.vb_ref
  101.7 34.5 %attend_forward.1 = (bf16[4,2,192,512]{3,2,1,0:T(8,128)(2,1)}, bf16[2,192,2048]{2,1,0:T(8,128)(2,1)}, bf16[2,192,2048]{2,1,0:T(8,128)(2,1)}, bf16[2,192,2048]{2,1,0:T(8,128)(2,1)}, f32[2,8,2048]{2,1,0:T(8,128)}) custom-call(s32[2]{0:T(128)} %len_ref.5, s32[1]{0:T(128)} %bitcast.4.fresh_ref, bf16[4,2,512,768]{3,2,1,0:T(8,128)(2,1)} %get-tuple-element.48.x_ref, ...), custom_call_target="tpu_custom_call" | custom-call | flops 40000000000 | bytes 20000000 | tf_op jit(solution)/shard_map/attend_forward/pallas_call | solution.py:613
  136.3 0.0 collective-permute-done.1.rest_3_
  136.3 0.0 collective-permute-done.rest_1_
  136.3 0.2 collective-permute-start.3
  136.5 0.3 collective-permute-start.4
  136.9 0.2 collective-permute-start.5
  137.0 3.7 all-to-all-start
  140.8 1.3 slice.41
  142.1 0.6 concatenate.7.rows_ref
  142.8 0.0 copy-done
  142.8 0.3 convert_reduce_fusion
  143.1 0.6 fusion.10
  143.7 0.0 collective-permute-done.4.rest_6_
  143.7 0.0 collective-permute-done.2.rest_4_
  143.7 17.0 %all-to-all-done.att_ref = bf16[4,2,192,512]{3,2,1,0:T(8,128)(2,1)S(1)} async-done(((bf16[4,2,192,512]{3,2,1,0:T(8,128)(2,1)}), bf16[4,2,192,512]{3,2,1,0:T(8,128)(2,1)S(1)}, u32[]{:S(2)}, u32[]{:S(2)}) %all-to-all-start) | async-done | bytes 1572896 | tf_op jit(solution)/shard_map/all_to_all | solution.py:2378
  160.7 0.0 collective-permute-done.5.rest_7_
  160.7 0.0 collective-permute-done.3.rest_5_
  160.7 1.2 copy-done.2
  161.8 50.1 %feed_forward.1 = (bf16[2,512,768]{2,1,0:T(8,128)(2,1)}, f32[2,512,768]{2,1,0:T(8,128)}, bf16[4,2,192,512]{3,2,1,0:T(8,128)(2,1)}, bf16[1024,3072]{1,0:T(8,128)(...) custom-call(s32[2]{0:T(128)} %len_ref.5, ...), custom_call_target="tpu_custom_call" | custom-call | flops 24000000000 | bytes 40000000 | tf_op jit(solution)/shard_map/feed_forward/pallas_call | solution.py:1021
  211.9 3.8 all-to-all-start.1
  215.8 24.0 %paired_grads.1 = bf16[416,64,128]{2,1,0:T(8,128)(2,1)} custom-call(bf16[4,2,192,512]{3,2,1,0:T(8,128)(2,1)} %copy-done.2, bf16[1024,768]{1,0:T(8,128)(2,1)} %get-tuple-element.62.bg_ref, bf16[1024,768]{1,0:T(8,128)(2,1)} %get-tuple-element.63.og_ref, bf16[1024,768]{1,0:T(8,128)(2,1)} %get-tuple-element.64.nt_ref, ...), custom_call_target="tpu_custom_call" | custom-call | flops 12000000000 | bytes 40000000 | tf_op jit(solution)/shard_map/paired_grads/pallas_call | solution.py:1542
  239.7 0.0 all-to-all-done.1.g_ref
  239.8 0.0 copy-start.3
  239.8 1.2 copy-done.3
  241.0 115.4 %attend_back_sum.1 = (f32[2,512,768]{2,1,0:T(8,128)}, bf16[4,2,192,512]{3,2,1,0:T(8,128)(2,1)}, f32[13,128,128]{2,1,0:T(8,128)}, f32[1,576]{1,0:T(1,128)}) custom-call(s32[2]{0:T(128)} %len_ref.5, s32[1]{0:T(128)} %bitcast.4.fresh_ref, bf16[2,192,2048]{2,1,0:T(8,128)(2,1)} %get-tuple-element.57.q_ref, bf16[2,192,2048]{2,1,0:T(8,128)(2,1)} %get-tuple-element.58.k_ref, ...), custom_call_target="tpu_custom_call" | custom-call | flops 70000001024 | bytes 25000000 | tf_op jit(solution)/shard_map/attend_back_sum/pallas_call | solution.py:2068
  356.3 0.0 copy-start.1
  356.4 0.0 copy-start.8
  356.4 4.0 all-to-all-start.2
  360.3 0.0 copy-done.1
  360.4 3.0 fusion.9
  363.3 0.6 pad_maximum_fusion.gain_ref
  363.9 24.3 %finish.1 = (f32[13,128,128]{2,1,0:T(8,128)}, f32[13,128,128]{2,1,0:T(8,128)}, f32[13,128,128]{2,1,0:T(8,128)}, f32[13,128,128]{2,1,0:T(8,128)}, f32[69,128]{1,0...) custom-call(f32[13,128,128]{2,1,0:T(8,128)} %get-tuple-element.69.raw_ref, ...), custom_call_target="tpu_custom_call" | custom-call | tf_op jit(solution)/shard_map/finish/pallas_call | solution.py:2274
  388.2 1.2 slice.43
  389.4 4.5 %fusion.8 = f32[2,512,768]{2,1,0:T(8,128)} fusion(f32[2,512,768]{2,1,0:T(8,128)} %get-tuple-element.56, bf16[2,512,768]{2,1,0:T(8,128)(2,1)S(1)} %copy-done.1, f32[2,512,768]{2,1,0:T(8,128)} %get-tuple-element.67, f32[2,512]{1,0:T(2,128)S(1)} %get-tuple-element.103, f32[2,512]{1,0:T(2,128)S(1)} %add_rsqrt_fusion, f32[2,512]{1,0:T(2,128)S(1)} %broadcast_multiply_fusion.1, ...), kind=kLoop, calls=%fused_computation.10 | loop fusion | flops 7077888 | bytes 11029504 | tf_op jit(solution)/shard_map/add | solution.py:2430
  394.0 0.0 all-to-all-done.2
  394.0 0.2 convert_bitcast_fusion
  394.2 0.1 copy.26
  394.3 0.0 copy-start.6
  394.3 0.0 copy-start.5
  394.3 1.6 copy.27
  396.0 2.2 copy.37
  398.2 0.9 copy.38
  399.1 0.9 copy.39
  400.0 0.9 copy.40
  400.9 0.0 copy-done.11
  400.9 0.6 copy.41
  401.5 0.6 copy.42
  402.1 0.0 copy-done.9
  402.1 0.6 copy.43
  (25 shorter events, 0.1 us)
Async XLA Ops:
  1.4 0.6 copy-start.7
  93.2 43.1 %collective-permute-start = (bf16[4,2,7,128,128]{4,3,2,1,0:T(8,128)(2,1)}, bf16[4,2,7,128,128]{4,3,2,1,0:T(8,128)(2,1)}, u32[]{:S(2)}, u32[]{:S(2)}) collective-permute-start(bf16[4,2,7,128,128]{4,3,2,1,0:T(8,128)(2,1)} %get-tuple-element.46.rest_0_), channel_id=1, source_target_pairs={{0,4},{1,5},{2,6},{3,7},{4,0},{5,1},{6,2},{7,3},{8,12},{9,13},{10,... | collective-permute-start | bytes 5505032 | tf_op jit(solution)/shard_map/ppermute | solution.py:2340
  94.1 49.6 %collective-permute-start.2 = (bf16[4,2,7,128,128]{4,3,2,1,0:T(8,128)(2,1)}, bf16[4,2,7,128,128]{4,3,2,1,0:T(8,128)(2,1)}, u32[]{:S(2)}, u32[]{:S(2)}) collective-permute-start(bf16[4,2,7,128,128]{4,3,2,1,0:T(8,128)(2,1)} %get-tuple-element.46.rest_0_), channel_id=1, source_target_pairs={{0,1},{1,0},{2,3},{3,2},{4,5},{5,4},{6,7},{7,6},{8,9},{9,8},{10,11... | collective-permute-start | bytes 5505032 | tf_op jit(solution)/shard_map/ppermute | solution.py:2340
  94.1 42.2 %collective-permute-start.1 = (bf16[8,6,128,128]{3,2,1,0:T(8,128)(2,1)}, bf16[8,6,128,128]{3,2,1,0:T(8,128)(2,1)}, u32[]{:S(2)}, u32[]{:S(2)}) collective-permute-start(bf16[8,6,128,128]{3,2,1,0:T(8,128)(2,1)} %get-tuple-element.47.rest_2_), channel_id=1, source_target_pairs={{0,2},{1,3},{2,0},{3,1},{4,6},{5,7},{6,4},{7,5},{8,10},{9,11},{10,... | collective-permute-start | bytes 4718600 | tf_op jit(solution)/shard_map/ppermute | solution.py:2340
  136.3 6.5 %copy-start = (bf16[2,512,768]{2,1,0:T(8,128)(2,1)S(1)}, bf16[2,512,768]{2,1,0:T(8,128)(2,1)}, u32[]{:S(2)}) copy-start(bf16[2,512,768]{2,1,0:T(8,128)(2,1)} %tok_ref.3) | copy-start | bytes 4718596
  136.3 24.4 %collective-permute-start.3 = (bf16[4,2,7,128,128]{4,3,2,1,0:T(8,128)(2,1)}, bf16[4,2,7,128,128]{4,3,2,1,0:T(8,128)(2,1)}, u32[]{:S(2)}, u32[]{:S(2)}) collective-permute-start(bf16[4,2,7,128,128]{4,3,2,1,0:T(8,128)(2,1)} %collective-permute-done.rest_1_), channel_id=1, source_target_pairs={{0,1},{1,0},{2,3},{3,2},{4,5},{5,4},{6,7},{7,6},{8,9},{9,8},{10,11... | collective-permute-start | bytes 5505032 | tf_op jit(solution)/shard_map/ppermute | solution.py:2340
  136.5 7.2 %collective-permute-start.4 = (bf16[8,6,128,128]{3,2,1,0:T(8,128)(2,1)}, bf16[8,6,128,128]{3,2,1,0:T(8,128)(2,1)}, u32[]{:S(2)}, u32[]{:S(2)}) collective-permute-start(bf16[8,6,128,128]{3,2,1,0:T(8,128)(2,1)} %get-tuple-element.47.rest_2_), channel_id=1, source_target_pairs={{0,1},{1,0},{2,3},{3,2},{4,5},{5,4},{6,7},{7,6},{8,9},{9,8},{10,11... | collective-permute-start | bytes 4718600 | tf_op jit(solution)/shard_map/ppermute | solution.py:2340
  136.9 23.8 %collective-permute-start.5 = (bf16[8,6,128,128]{3,2,1,0:T(8,128)(2,1)}, bf16[8,6,128,128]{3,2,1,0:T(8,128)(2,1)}, u32[]{:S(2)}, u32[]{:S(2)}) collective-permute-start(bf16[8,6,128,128]{3,2,1,0:T(8,128)(2,1)} %collective-permute-done.1.rest_3_), channel_id=1, source_target_pairs={{0,1},{1,0},{2,3},{3,2},{4,5},{5,4},{6,7},{7,6},{8,9},{9,8},{10,11... | collective-permute-start | bytes 4718600 | tf_op jit(solution)/shard_map/ppermute | solution.py:2340
  137.0 23.6 %all-to-all-start = ((bf16[4,2,192,512]{3,2,1,0:T(8,128)(2,1)}), bf16[4,2,192,512]{3,2,1,0:T(8,128)(2,1)S(1)}, u32[]{:S(2)}, u32[]{:S(2)}) async-start(bf16[4,2,192,512]{3,2,1,0:T(8,128)(2,1)} %get-tuple-element.52.o_ref), calls=%async_computation | async-start | bytes 3145728 | tf_op jit(solution)/shard_map/all_to_all | solution.py:2378
  160.7 1.2 copy-start.2
  211.9 27.8 %all-to-all-start.1 = ((bf16[4,2,192,512]{3,2,1,0:T(8,128)(2,1)}), bf16[4,2,192,512]{3,2,1,0:T(8,128)(2,1)S(1)}, u32[]{:S(2)}, u32[]{:S(2)}) async-start(bf16[4,2,192,512]{3,2,1,0:T(8,128)(2,1)} %get-tuple-element.60), calls=%async_computation.1 | async-start | bytes 3145728 | tf_op jit(solution)/shard_map/all_to_all | solution.py:2405
  239.8 1.2 copy-start.3
  356.3 4.0 copy-start.1
  356.4 4.0 copy-start.8
  356.4 37.6 %all-to-all-start.2 = ((bf16[4,2,192,512]{3,2,1,0:T(8,128)(2,1)}), bf16[4,2,192,512]{3,2,1,0:T(8,128)(2,1)S(1)}, u32[]{:S(2)}, u32[]{:S(2)}) async-start(bf16[4,2,192,512]{3,2,1,0:T(8,128)(2,1)} %get-tuple-element.68), calls=%async_computation.2 | async-start | bytes 3145728 | tf_op jit(solution)/shard_map/all_to_all | solution.py:2422
  394.3 3.8 copy-start.6
  394.3 4.7 %copy-start.5 = (f32[13,128,128]{2,1,0:T(8,128)S(1)}, f32[13,128,128]{2,1,0:T(8,128)}, u32[]{:S(2)}) copy-start(f32[13,128,128]{2,1,0:T(8,128)} %get-tuple-element.121) | copy-start | bytes 2555908
  395.9 4.0 copy-start.4
  396.0 4.9 %copy-start.11 = (f32[69,128]{1,0:T(8,128)S(1)}, f32[69,128]{1,0:T(8,128)}, u32[]{:S(2)}) copy-start(f32[69,128]{1,0:T(8,128)} %get-tuple-element.77) | copy-start | bytes 105988
  396.0 5.5 %copy-start.10 = (f32[69,128]{1,0:T(8,128)S(1)}, f32[69,128]{1,0:T(8,128)}, u32[]{:S(2)}) copy-start(f32[69,128]{1,0:T(8,128)} %get-tuple-element.78) | copy-start | bytes 105988
  396.0 6.2 %copy-start.9 = (f32[69,128]{1,0:T(8,128)S(1)}, f32[69,128]{1,0:T(8,128)}, u32[]{:S(2)}) copy-start(f32[69,128]{1,0:T(8,128)} %get-tuple-element.79) | copy-start | bytes 105988

commit v4 on v3

--- a/solution.py
+++ b/solution.py
@@ -858,7 +858,7 @@
     )(lengths, fresh, group, q, k, v, o, g, lse, x, w, all_tiles)
 
 
-HIDDEN_CHUNK = 512
+HIDDEN_CHUNK = 1024
 GELU_A = 0.7978845608028654
 GELU_B = 0.044715
 

time: 404 us -> 408 us (level); the launches traced: 403 us -> 401 us
  transfers between devices with their start and end apart: 9 -> 9, of which waited for: 1 -> 2; matrix products, arithmetic and copies ran while one was open for 4% -> 4% of each run, Pallas kernels for 21% -> 20%
where the time goes in v4:
time: 408 us; the launch traced here: 401 us
  Pallas kernels  333 us (82%)
  local copies, waits for them, and re-layouts  20.3 us (5%)
  starting transfers between devices  18.1 us (4%)
  waiting for transfers between devices  18.1 us (4%)
  other arithmetic  9.89 us (2%)
    pallas_call x1, Pallas kernels, attend_back_sum(): pl.pallas_call(functools.partial(attend_back_sum_kernel, heads, flows), g...  117 us
    pallas_call x1, Pallas kernels, front(): pl.pallas_call(front_kernel, in_specs=[vm] * 3 + [hbm], out_specs=[hbm, v...  88.1 us
    pallas_call x1, Pallas kernels, feed_forward(): pl.pallas_call(functools.partial(feed_forward_kernel, len(sources)), grid...  47.3 us
    pallas_call x1, Pallas kernels, attend_forward(): pl.pallas_call(functools.partial(attend_forward_kernel, heads), grid_spec...  32.3 us
    pallas_call x1, Pallas kernels, finish(): pl.pallas_call(functools.partial(finish_kernel, stages), in_specs=[vm] *...  24.3 us
    pallas_call x1, Pallas kernels, paired_grads(): pl.pallas_call(paired_grad_kernel, grid=(chunks + 1,), in_specs=[whole(a....  24.2 us
    all_to_all x1, waiting for transfers between devices, per_device(): att = lax.all_to_all(o_heads, 'seq', 0, 0, tiled=True)  17.5 us
    unnamed x33, local copies, waits for them, and re-layouts  12.8 us
  transfers between devices with their start and end apart: 9, of which 2 were waited for; matrix products, arithmetic and copies ran while one was open for 4% of the time, Pallas kernels for 20%

profile of v4, /device:TPU:0, one launch (start us, length us, event | category | flops | bytes accessed | tf_op | source)
XLA Modules:
  0.0 400.9 jit_solution(4829931484055696871)
XLA Ops:
  0.6 0.8 fusion.11
  1.5 0.6 copy-done.7
  2.0 1.4 copy.22
  3.4 0.9 copy.29
  4.4 0.1 pad.4.clone
  4.5 0.7 maximum_maximum_fusion.rows_ref
  5.1 88.1 %front.1 = (bf16[4,2,512,768]{3,2,1,0:T(8,128)(2,1)}, bf16[576,768]{1,0:T(8,128)(2,1)}, bf16[4,2,192,512]{3,2,1,0:T(8,128)(2,1)}, bf16[4,2,7,128,128]{4,3,2,1,0:T(8,128)(2,1)}, bf16[8,6,128,128]{3,2,1,0:T(8,128)(2,1)}) custom-call(bf16[2,512,768]{2,1,0:T(8,128)(2,1)} %tok_ref.3, f32[8,768]{1,0:T(8,128)} %maximum_maximum_fusion.rows_ref, ...), custom_call_target="tpu_custom_call" | custom-call | flops 40000000000 | bytes 20000000 | tf_op jit(solution)/shard_map/front/pallas_call | solution.py:452
  93.2 0.9 collective-permute-start
  94.1 0.0 collective-permute-start.2
  94.1 5.3 %collective-permute-start.1 = (bf16[8,6,128,128]{3,2,1,0:T(8,128)(2,1)}, bf16[8,6,128,128]{3,2,1,0:T(8,128)(2,1)}, u32[]{:S(2)}, u32[]{:S(2)}) collective-permute-start(bf16[8,6,128,128]{3,2,1,0:T(8,128)(2,1)} %get-tuple-element.47.rest_2_), channel_id=1, source_target_pairs={{0,2},{1,3},{2,0},{3,1},{4,6},{5,7},{6,4},{7,5},{8,10},{9,11},{10,... | collective-permute-start | bytes 4718600 | tf_op jit(solution)/shard_map/ppermute | solution.py:2340
  99.4 0.7 slice.36
  100.0 0.1 dynamic_slice.6
  100.1 0.8 copy.24.qb_ref
  100.9 0.1 dynamic_slice.7
  101.0 0.8 copy.25.vb_ref
  101.7 32.3 %attend_forward.1 = (bf16[4,2,192,512]{3,2,1,0:T(8,128)(2,1)}, bf16[2,192,2048]{2,1,0:T(8,128)(2,1)}, bf16[2,192,2048]{2,1,0:T(8,128)(2,1)}, bf16[2,192,2048]{2,1,0:T(8,128)(2,1)}, f32[2,8,2048]{2,1,0:T(8,128)}) custom-call(s32[2]{0:T(128)} %len_ref.5, s32[1]{0:T(128)} %bitcast.4.fresh_ref, bf16[4,2,512,768]{3,2,1,0:T(8,128)(2,1)} %get-tuple-element.48.x_ref, ...), custom_call_target="tpu_custom_call" | custom-call | flops 40000000000 | bytes 20000000 | tf_op jit(solution)/shard_map/attend_forward/pallas_call | solution.py:613
  134.0 0.7 collective-permute-done.1.rest_3_
  134.7 0.0 collective-permute-done.rest_1_
  134.7 0.0 collective-permute-start.3
  134.7 0.5 collective-permute-start.4
  135.2 0.0 collective-permute-start.5
  135.2 3.7 all-to-all-start
  138.9 1.3 slice.41
  140.3 0.6 concatenate.7.rows_ref
  140.9 0.0 copy-done
  140.9 0.3 convert_reduce_fusion
  141.2 0.6 fusion.10
  141.8 0.0 collective-permute-done.4.rest_6_
  141.8 0.0 collective-permute-done.2.rest_4_
  141.8 17.5 %all-to-all-done.att_ref = bf16[4,2,192,512]{3,2,1,0:T(8,128)(2,1)S(1)} async-done(((bf16[4,2,192,512]{3,2,1,0:T(8,128)(2,1)}), bf16[4,2,192,512]{3,2,1,0:T(8,128)(2,1)S(1)}, u32[]{:S(2)}, u32[]{:S(2)}) %all-to-all-start) | async-done | bytes 1572896 | tf_op jit(solution)/shard_map/all_to_all | solution.py:2378
  159.3 0.0 collective-permute-done.5.rest_7_
  159.3 0.0 collective-permute-done.3.rest_5_
  159.3 1.2 copy-done.2
  160.5 47.3 %feed_forward.1 = (bf16[2,512,768]{2,1,0:T(8,128)(2,1)}, f32[2,512,768]{2,1,0:T(8,128)}, bf16[4,2,192,512]{3,2,1,0:T(8,128)(2,1)}, bf16[1024,3072]{1,0:T(8,128)(...) custom-call(s32[2]{0:T(128)} %len_ref.5, ...), custom_call_target="tpu_custom_call" | custom-call | flops 24000000000 | bytes 40000000 | tf_op jit(solution)/shard_map/feed_forward/pallas_call | solution.py:1021
  207.8 3.8 all-to-all-start.1
  211.6 24.2 %paired_grads.1 = bf16[416,64,128]{2,1,0:T(8,128)(2,1)} custom-call(bf16[4,2,192,512]{3,2,1,0:T(8,128)(2,1)} %copy-done.2, bf16[1024,768]{1,0:T(8,128)(2,1)} %get-tuple-element.62.bg_ref, bf16[1024,768]{1,0:T(8,128)(2,1)} %get-tuple-element.63.og_ref, bf16[1024,768]{1,0:T(8,128)(2,1)} %get-tuple-element.64.nt_ref, ...), custom_call_target="tpu_custom_call" | custom-call | flops 12000000000 | bytes 40000000 | tf_op jit(solution)/shard_map/paired_grads/pallas_call | solution.py:1542
  235.8 0.0 all-to-all-done.1.g_ref
  235.8 0.0 copy-start.3
  235.8 1.2 copy-done.3
  237.0 117.0 %attend_back_sum.1 = (f32[2,512,768]{2,1,0:T(8,128)}, bf16[4,2,192,512]{3,2,1,0:T(8,128)(2,1)}, f32[13,128,128]{2,1,0:T(8,128)}, f32[1,576]{1,0:T(1,128)}) custom-call(s32[2]{0:T(128)} %len_ref.5, s32[1]{0:T(128)} %bitcast.4.fresh_ref, bf16[2,192,2048]{2,1,0:T(8,128)(2,1)} %get-tuple-element.57.q_ref, bf16[2,192,2048]{2,1,0:T(8,128)(2,1)} %get-tuple-element.58.k_ref, ...), custom_call_target="tpu_custom_call" | custom-call | flops 70000001024 | bytes 25000000 | tf_op jit(solution)/shard_map/attend_back_sum/pallas_call | solution.py:2068
  354.0 0.0 copy-start.1
  354.0 0.0 copy-start.8
  354.0 4.0 all-to-all-start.2
  358.0 0.0 copy-done.1
  358.0 0.0 copy-done.8
  358.0 3.0 fusion.9
  361.0 0.6 pad_maximum_fusion.gain_ref
  361.6 24.3 %finish.1 = (f32[13,128,128]{2,1,0:T(8,128)}, f32[13,128,128]{2,1,0:T(8,128)}, f32[13,128,128]{2,1,0:T(8,128)}, f32[13,128,128]{2,1,0:T(8,128)}, f32[69,128]{1,0...) custom-call(f32[13,128,128]{2,1,0:T(8,128)} %get-tuple-element.69.raw_ref, ...), custom_call_target="tpu_custom_call" | custom-call | tf_op jit(solution)/shard_map/finish/pallas_call | solution.py:2274
  385.9 1.2 slice.43
  387.1 4.5 %fusion.8 = f32[2,512,768]{2,1,0:T(8,128)} fusion(f32[2,512,768]{2,1,0:T(8,128)} %get-tuple-element.56, bf16[2,512,768]{2,1,0:T(8,128)(2,1)S(1)} %copy-done.1, f32[2,512,768]{2,1,0:T(8,128)} %get-tuple-element.67, f32[2,512]{1,0:T(2,128)S(1)} %get-tuple-element.103, f32[2,512]{1,0:T(2,128)S(1)} %add_rsqrt_fusion, f32[2,512]{1,0:T(2,128)S(1)} %broadcast_multiply_fusion.1, ...), kind=kLoop, calls=%fused_computation.10 | loop fusion | flops 7077888 | bytes 11029504 | tf_op jit(solution)/shard_map/add | solution.py:2430
  391.7 0.0 all-to-all-done.2
  391.7 0.2 convert_bitcast_fusion
  391.9 0.1 copy.26
  392.0 0.0 copy-start.6
  392.0 0.0 copy-start.5
  392.0 1.6 copy.27
  393.7 2.2 copy.37
  395.9 0.0 copy-done.6
  395.9 0.9 copy.38
  396.8 0.9 copy.39
  397.7 0.9 copy.40
  398.6 0.6 copy.41
  399.2 0.6 copy.42
  399.8 0.6 copy.43
  (25 shorter events, 0.1 us)
Async XLA Ops:
  1.4 0.6 copy-start.7
  93.2 41.4 %collective-permute-start = (bf16[4,2,7,128,128]{4,3,2,1,0:T(8,128)(2,1)}, bf16[4,2,7,128,128]{4,3,2,1,0:T(8,128)(2,1)}, u32[]{:S(2)}, u32[]{:S(2)}) collective-permute-start(bf16[4,2,7,128,128]{4,3,2,1,0:T(8,128)(2,1)} %get-tuple-element.46.rest_0_), channel_id=1, source_target_pairs={{0,4},{1,5},{2,6},{3,7},{4,0},{5,1},{6,2},{7,3},{8,12},{9,13},{10,... | collective-permute-start | bytes 5505032 | tf_op jit(solution)/shard_map/ppermute | solution.py:2340
  94.1 47.7 %collective-permute-start.2 = (bf16[4,2,7,128,128]{4,3,2,1,0:T(8,128)(2,1)}, bf16[4,2,7,128,128]{4,3,2,1,0:T(8,128)(2,1)}, u32[]{:S(2)}, u32[]{:S(2)}) collective-permute-start(bf16[4,2,7,128,128]{4,3,2,1,0:T(8,128)(2,1)} %get-tuple-element.46.rest_0_), channel_id=1, source_target_pairs={{0,1},{1,0},{2,3},{3,2},{4,5},{5,4},{6,7},{7,6},{8,9},{9,8},{10,11... | collective-permute-start | bytes 5505032 | tf_op jit(solution)/shard_map/ppermute | solution.py:2340
  94.1 40.6 %collective-permute-start.1 = (bf16[8,6,128,128]{3,2,1,0:T(8,128)(2,1)}, bf16[8,6,128,128]{3,2,1,0:T(8,128)(2,1)}, u32[]{:S(2)}, u32[]{:S(2)}) collective-permute-start(bf16[8,6,128,128]{3,2,1,0:T(8,128)(2,1)} %get-tuple-element.47.rest_2_), channel_id=1, source_target_pairs={{0,2},{1,3},{2,0},{3,1},{4,6},{5,7},{6,4},{7,5},{8,10},{9,11},{10,... | collective-permute-start | bytes 4718600 | tf_op jit(solution)/shard_map/ppermute | solution.py:2340
  134.0 6.9 %copy-start = (bf16[2,512,768]{2,1,0:T(8,128)(2,1)S(1)}, bf16[2,512,768]{2,1,0:T(8,128)(2,1)}, u32[]{:S(2)}) copy-start(bf16[2,512,768]{2,1,0:T(8,128)(2,1)} %tok_ref.3) | copy-start | bytes 4718596
  134.7 24.6 %collective-permute-start.3 = (bf16[4,2,7,128,128]{4,3,2,1,0:T(8,128)(2,1)}, bf16[4,2,7,128,128]{4,3,2,1,0:T(8,128)(2,1)}, u32[]{:S(2)}, u32[]{:S(2)}) collective-permute-start(bf16[4,2,7,128,128]{4,3,2,1,0:T(8,128)(2,1)} %collective-permute-done.rest_1_), channel_id=1, source_target_pairs={{0,1},{1,0},{2,3},{3,2},{4,5},{5,4},{6,7},{7,6},{8,9},{9,8},{10,11... | collective-permute-start | bytes 5505032 | tf_op jit(solution)/shard_map/ppermute | solution.py:2340
  134.7 7.2 %collective-permute-start.4 = (bf16[8,6,128,128]{3,2,1,0:T(8,128)(2,1)}, bf16[8,6,128,128]{3,2,1,0:T(8,128)(2,1)}, u32[]{:S(2)}, u32[]{:S(2)}) collective-permute-start(bf16[8,6,128,128]{3,2,1,0:T(8,128)(2,1)} %get-tuple-element.47.rest_2_), channel_id=1, source_target_pairs={{0,1},{1,0},{2,3},{3,2},{4,5},{5,4},{6,7},{7,6},{8,9},{9,8},{10,11... | collective-permute-start | bytes 4718600 | tf_op jit(solution)/shard_map/ppermute | solution.py:2340
  135.2 24.1 %collective-permute-start.5 = (bf16[8,6,128,128]{3,2,1,0:T(8,128)(2,1)}, bf16[8,6,128,128]{3,2,1,0:T(8,128)(2,1)}, u32[]{:S(2)}, u32[]{:S(2)}) collective-permute-start(bf16[8,6,128,128]{3,2,1,0:T(8,128)(2,1)} %collective-permute-done.1.rest_3_), channel_id=1, source_target_pairs={{0,1},{1,0},{2,3},{3,2},{4,5},{5,4},{6,7},{7,6},{8,9},{9,8},{10,11... | collective-permute-start | bytes 4718600 | tf_op jit(solution)/shard_map/ppermute | solution.py:2340
  135.2 24.1 %all-to-all-start = ((bf16[4,2,192,512]{3,2,1,0:T(8,128)(2,1)}), bf16[4,2,192,512]{3,2,1,0:T(8,128)(2,1)S(1)}, u32[]{:S(2)}, u32[]{:S(2)}) async-start(bf16[4,2,192,512]{3,2,1,0:T(8,128)(2,1)} %get-tuple-element.52.o_ref), calls=%async_computation | async-start | bytes 3145728 | tf_op jit(solution)/shard_map/all_to_all | solution.py:2378
  159.3 1.2 copy-start.2
  207.8 28.0 %all-to-all-start.1 = ((bf16[4,2,192,512]{3,2,1,0:T(8,128)(2,1)}), bf16[4,2,192,512]{3,2,1,0:T(8,128)(2,1)S(1)}, u32[]{:S(2)}, u32[]{:S(2)}) async-start(bf16[4,2,192,512]{3,2,1,0:T(8,128)(2,1)} %get-tuple-element.60), calls=%async_computation.1 | async-start | bytes 3145728 | tf_op jit(solution)/shard_map/all_to_all | solution.py:2405
  235.8 1.2 copy-start.3
  354.0 4.0 copy-start.1
  354.0 4.0 copy-start.8
  354.0 37.7 %all-to-all-start.2 = ((bf16[4,2,192,512]{3,2,1,0:T(8,128)(2,1)}), bf16[4,2,192,512]{3,2,1,0:T(8,128)(2,1)S(1)}, u32[]{:S(2)}, u32[]{:S(2)}) async-start(bf16[4,2,192,512]{3,2,1,0:T(8,128)(2,1)} %get-tuple-element.68), calls=%async_computation.2 | async-start | bytes 3145728 | tf_op jit(solution)/shard_map/all_to_all | solution.py:2422
  392.0 3.8 copy-start.6
  392.0 4.7 %copy-start.5 = (f32[13,128,128]{2,1,0:T(8,128)S(1)}, f32[13,128,128]{2,1,0:T(8,128)}, u32[]{:S(2)}) copy-start(f32[13,128,128]{2,1,0:T(8,128)} %get-tuple-element.121) | copy-start | bytes 2555908
  393.6 4.0 %copy-start.4 = (f32[13,128,128]{2,1,0:T(8,128)S(1)}, f32[13,128,128]{2,1,0:T(8,128)}, u32[]{:S(2)}) copy-start(f32[13,128,128]{2,1,0:T(8,128)} %get-tuple-element.122) | copy-start | bytes 2555908
  393.7 4.9 %copy-start.11 = (f32[69,128]{1,0:T(8,128)S(1)}, f32[69,128]{1,0:T(8,128)}, u32[]{:S(2)}) copy-start(f32[69,128]{1,0:T(8,128)} %get-tuple-element.77) | copy-start | bytes 105988
  393.7 5.5 %copy-start.10 = (f32[69,128]{1,0:T(8,128)S(1)}, f32[69,128]{1,0:T(8,128)}, u32[]{:S(2)}) copy-start(f32[69,128]{1,0:T(8,128)} %get-tuple-element.78) | copy-start | bytes 105988
  393.7 6.2 %copy-start.9 = (f32[69,128]{1,0:T(8,128)S(1)}, f32[69,128]{1,0:T(8,128)}, u32[]{:S(2)}) copy-start(f32[69,128]{1,0:T(8,128)} %get-tuple-element.79) | copy-start | bytes 105988
